TPU v7x, 128 devices: a whole 4x4x4 slice. The times are simulated.
128 devices in a mesh: tok: 64 (over x, y, z), head: 2 (over core).
Axes of the slice: x: 4, y: 4, z: 4, core: 2. Of those that a mesh axis runs over, the one named last changes fastest.
Arguments:
- queries: bfloat16 [2, 49152, 1536], P(None, 'tok', 'head'), may hold values from -16 to 16
- key_rows: bfloat16 [2, 49152, 1536], P(None, 'tok', 'head'), may hold values from -8 to 8
- value_rows: bfloat16 [2, 49152, 1536], P(None, 'tok', 'head'), may hold values from -6 to 6
- step_rates: float32 [4, 2, 49152], P('head', None, 'tok'), may hold values from 0.01 to 1
- gate_init: float32 [4, 384, 384], P('head'), may hold values from -0.3125 to 0.3125
- up_init: float32 [4, 384, 384], P('head'), may hold values from -0.3125 to 0.3125
- down_init: float32 [4, 384, 384], P('head'), may hold values from -0.3125 to 0.3125
- out_weight: bfloat16 [1536, 1536], P('head'), may hold values from -0.15625 to 0.15625
Outputs:
- mixed_out: bfloat16 [2, 49152, 1536], P(None, 'tok', 'head')
All inputs are finite; a program needn't handle non-finite values.
Results may differ from a plain program's by a relative error of at most 0.009.
Values may be sent and summed in bfloat16 or wider, within the bound.
No kernel may reach another device: no remote copies, remote signals or barrier semaphores. Data moves between devices by JAX's collectives and lax.ppermute only.
A program may use at most 128 MiB of HBM per device.

v0:
```python
import math

import jax
import jax.numpy as jnp
from jax import lax
from jax.sharding import PartitionSpec as P

DH = 384
WINDOW = 384


EPSILON = 1e-06


def shifted(x, axis, by):
    count = lax.axis_size(axis)
    return lax.ppermute(x, axis, [(i, (i + by) % count) for i in range(count)])


def silu_slope(values_in):
    sigmoid_at = jax.nn.sigmoid(values_in)
    return sigmoid_at * (1.0 + values_in * (1.0 - sigmoid_at))


def row_scale(matrix):
    return jnp.sqrt(jnp.mean(matrix * matrix, axis=-1, keepdims=True) + EPSILON)


def renormed(old_weight, gradient, rate_sum):
    updated = old_weight - gradient / rate_sum
    return updated * (row_scale(old_weight) / row_scale(updated))


def shards(queries, key_rows, value_rows, step_rates, gate_init, up_init, down_init, out_weight):
    blocks, local_rows, local_width = queries.shape
    heads_here = local_width // DH
    device_count = lax.axis_size("tok")
    device_at = lax.axis_index("tok")
    score_scale = 1.0 / math.sqrt(DH)
    tail_keys = key_rows[:, local_rows - WINDOW :, :]
    tail_values = value_rows[:, local_rows - WINDOW :, :]
    near_keys, near_values = shifted((tail_keys, tail_values), "tok", 1)
    is_first = device_at == 0
    near_keys = jnp.where(is_first, jnp.roll(near_keys, 1, axis=0), near_keys)
    near_values = jnp.where(is_first, jnp.roll(near_values, 1, axis=0), near_values)
    query_heads = queries.reshape(blocks, local_rows, heads_here, DH)
    key_heads = jnp.concatenate([near_keys, key_rows], axis=1).reshape(
        blocks, WINDOW + local_rows, heads_here, DH
    )
    value_heads = jnp.concatenate([near_values, value_rows], axis=1).reshape(
        blocks, WINDOW + local_rows, heads_here, DH
    )
    scores = (
        jnp.einsum("cqhd,ckhd->chqk", query_heads, key_heads, preferred_element_type=jnp.float32)
        * score_scale
    )
    offset = jnp.arange(WINDOW + local_rows)[None, :] - WINDOW - jnp.arange(local_rows)[:, None]
    block_first = jnp.arange(blocks) * (local_rows * device_count) + device_at * local_rows
    global_key = block_first[:, None] + jnp.arange(WINDOW + local_rows)[None, :] - WINDOW
    allowed = (offset <= 0) & (offset > -WINDOW)
    allowed = allowed[None, None] & (global_key >= 0)[:, None, None, :]
    scores = jnp.where(allowed, scores, -jnp.inf)
    row_max = jnp.max(scores, axis=-1, keepdims=True)
    expos = jnp.exp(scores - row_max)
    weights_bf = (expos / jnp.sum(expos, axis=-1, keepdims=True)).astype(jnp.bfloat16)
    attention = jnp.einsum(
        "chqk,ckhd->cqhd", weights_bf, value_heads, preferred_element_type=jnp.float32
    )
    cast_gate = gate_init.astype(jnp.bfloat16)
    cast_up = up_init.astype(jnp.bfloat16)
    cast_down = down_init.astype(jnp.bfloat16)
    gate_full, up_full, down_full = (gate_init, up_init, down_init)
    head_blocks = []
    for block_at in range(blocks):
        rate_total = lax.psum(jnp.sum(step_rates[:, block_at, :], axis=1), "tok")
        key_now = key_rows[block_at].reshape(local_rows, heads_here, DH)
        value_now = value_rows[block_at].reshape(local_rows, heads_here, DH)
        query_now = query_heads[block_at]
        errors = (
            jnp.transpose(step_rates[:, block_at, :])[:, :, None] * value_now.astype(jnp.float32)
        ).astype(jnp.bfloat16)
        pre_gate = jnp.einsum(
            "nhd,hfd->nhf", key_now, cast_gate, preferred_element_type=jnp.float32
        )
        pre_up = jnp.einsum("nhd,hfd->nhf", key_now, cast_up, preferred_element_type=jnp.float32)
        active = jax.nn.silu(pre_gate)
        hidden = (active * pre_up).astype(jnp.bfloat16)
        backed = jnp.einsum("nhd,hdf->nhf", errors, cast_down, preferred_element_type=jnp.float32)
        back_up = (-backed * active).astype(jnp.bfloat16)
        back_gate = (-backed * pre_up * silu_slope(pre_gate)).astype(jnp.bfloat16)
        grad_gate = jnp.einsum(
            "nhf,nhd->hfd", back_gate, key_now, preferred_element_type=jnp.float32
        )
        grad_up = jnp.einsum("nhf,nhd->hfd", back_up, key_now, preferred_element_type=jnp.float32)
        grad_down = -jnp.einsum("nhd,nhf->hdf", errors, hidden, preferred_element_type=jnp.float32)
        rate_shaped = rate_total[:, None, None]
        sum_gate, sum_up, sum_down = lax.psum((grad_gate, grad_up, grad_down), "tok")
        gate_full = renormed(gate_full, sum_gate, rate_shaped)
        up_full = renormed(up_full, sum_up, rate_shaped)
        down_full = renormed(down_full, sum_down, rate_shaped)
        cast_gate = gate_full.astype(jnp.bfloat16)
        cast_up = up_full.astype(jnp.bfloat16)
        cast_down = down_full.astype(jnp.bfloat16)
        query_gate = jnp.einsum(
            "nhd,hfd->nhf", query_now, cast_gate, preferred_element_type=jnp.float32
        )
        query_up = jnp.einsum(
            "nhd,hfd->nhf", query_now, cast_up, preferred_element_type=jnp.float32
        )
        query_hidden = (jax.nn.silu(query_gate) * query_up).astype(jnp.bfloat16)
        fast_out = jnp.einsum(
            "nhf,hdf->nhd", query_hidden, cast_down, preferred_element_type=jnp.float32
        )
        fast_out = fast_out / row_scale(fast_out)
        head_blocks.append(
            (fast_out + attention[block_at]).astype(jnp.bfloat16).reshape(local_rows, local_width)
        )
    joined = jnp.stack(head_blocks)
    partial_value = jnp.einsum(
        "cnw,wm->cnm", joined, out_weight, preferred_element_type=jnp.float32
    )
    mixed_out = lax.psum_scatter(partial_value, "head", scatter_dimension=2, tiled=True)
    return mixed_out.astype(jnp.bfloat16)


def solution(mesh):
    in_specs = (
        P(None, "tok", "head"),
        P(None, "tok", "head"),
        P(None, "tok", "head"),
        P("head", None, "tok"),
        P("head", None, None),
        P("head", None, None),
        P("head", None, None),
        P("head", None),
    )
    out_specs = P(None, "tok", "head")
    return jax.shard_map(shards, mesh=mesh, in_specs=in_specs, out_specs=out_specs, check_vma=False)
```

profile of v0, /device:TPU:1, one launch (start us, length us, event | category | flops | bytes accessed | tf_op | source)
XLA Modules:
  0.0 470.7 jit_solution(11788628695997670842)
XLA Ops:
  9.9 2.5 collective-permute-start
  12.4 4.3 copy.25
  16.6 2.6 slice.73
  22.9 2.5 slice_convert_fusion
  25.4 2.2 fusion.73
  27.6 2.2 fusion.75
  29.8 3.9 reshape.208
  35.1 3.1 fusion.71
  42.2 2.6 convolution_negate_fusion.1
  46.8 169.9 %all-reduce = (f32[2]{0:T(128)}, f32[2]{0:T(128)}) all-reduce(f32[2]{0:T(128)S(1)} %copy-done.20, f32[2]{0:T(128)S(1)} %copy-done.19), channel_id=1, replica_groups=mesh['tok'=64,'head'=2] {'tok'}, use_global_device_ids=true, to_apply=%region_2.3 | all-reduce | flops 4 | bytes 32 | tf_op jit(solution)/shard_map/psum | solution.py:75
  216.7 2.8 fusion.102
  219.5 2.4 copy.80
  223.3 4.0 reshape.209
  236.7 4.0 multiply_reduce_fusion.8
  246.9 2.1 fusion.64
  249.0 2.5 convolution_negate_fusion
  251.8 13.0 %fusion.106 = (f32[2,2,768]{2,1,0:T(2,128)}, f32[2,2,768,1152]{2,3,1,0:T(8,128)}) fusion(pred[2,768,1152]{1,2,0:T(8,128)(4,1)} %broadcast_and_fusion, bf16[2,1152,2,384]{1,3,2,0:T(8,128)(2,1)} %bitcast.234, bf16[2,96,2,8,384]{4,3,2,1,0:T(8,128)(2,1)} %bitcast.236), kind=kOutput, calls=%fused_computation.167 | convolution fusion | flops 2732065792 | bytes 21835776 | tf_op jit(solution)/shard_map/sub | solution.py:64
  264.8 2.4 copy.37
  267.2 3.9 pad_maximum_fusion
  271.1 5.8 %copy.38 = bf16[2,1152,768]{1,2,0:T(8,128)(2,1)} copy(bf16[2,1152,768]{2,1,0:T(8,128)(2,1)} %pad_maximum_fusion) | data formatting | bytes 7077888 | tf_op jit(solution)/shard_map/concatenate | solution.py:50
  276.9 12.0 %fusion.51 = f32[2,768,2,384]{1,3,2,0:T(8,128)} fusion(bf16[2,1152,2,384]{1,3,2,0:T(8,128)(2,1)} %bitcast.235, f32[2,2,768,1152]{2,3,1,0:T(8,128)} %get-tuple-element.55, f32[2,2,768]{2,1,0:T(2,128)} %get-tuple-element.54), kind=kOutput, calls=%fused_computation.84 | convolution fusion | flops 2724986880 | bytes 22425600 | tf_op jit(solution)/shard_map/chqk,ckhd->cqhd/dot_general | solution.py:66
  288.9 2.2 fusion.87
  291.1 6.5 %fusion.35 = (f32[768,2]{0,1:T(2,128)}, f32[2,384,768]{2,1,0:T(8,128)}) fusion(f32[2,384,768]{2,1,0:T(8,128)} %fusion.87, bf16[768,2,384]{0,2,1:T(8,128)(2,1)} %bitcast.232, f32[2,384,384]{2,1,0:T(8,128)} %copy-done.5, f32[2,384]{1,0:T(2,128)S(1)} %get-tuple-element.62, f32[2,384,384]{2,1,0:T(8,128)} %copy-done.4, f32[2,384]{1,0:T(2,128)S(1)} %rsqrt_multiply_fusion.5), kind=kOutput, calls=%fused_computation.57 | convolution fusion | flops 911866368 | bytes 8269824 | tf_op jit(solution)/shard_map/nhf,hdf->nhd/dot_general | solution.py:111
  298.9 111.4 %all-reduce.6.cloned.1.call-done = (f32[2,384,384]{2,1,0:T(8,128)}, f32[2,384,384]{2,1,0:T(8,128)}, f32[2,384,384]{2,1,0:T(8,128)}) async-done(((f32[2,384,384]{2,1,0:T(8,128)}, f32[2,384,384]{2,1,0:T(8,128)}, f32[2,384,384]{2,1,0:T(8,128)}), (f32[2,384,384]{2,1,0:T(8,128)}, f32[2,384,384]{2,1,0:T(8,128)}, f32[2,384,384]{2,1,0:T(8,128)})) %all-reduce.6.cloned.1.call-update) | async-done | bytes 3538960 | tf_op jit(solution)/shard_map/psum | solution.py:97
  410.3 3.8 multiply_reduce_fusion.5
  414.1 2.3 fusion.66
  416.5 6.6 %fusion.21 = (f32[768,2]{0,1:T(2,128)S(1)}, f32[2,384,768]{2,1,0:T(8,128)}) fusion(f32[2,384,768]{2,1,0:T(8,128)} %fusion.66, bf16[768,2,384]{0,2,1:T(8,128)(2,1)} %bitcast.237, f32[2,384]{1,0:T(2,128)S(1)} %rsqrt_multiply_fusion, f32[2,384,384]{2,1,0:T(8,128)} %get-tuple-element.16, f32[2,384,384]{2,1,0:T(8,128)} %copy-done.5, f32[2]{0:T(128)S(1)} %copy-done.21, ...), kind=kOutput, calls=%fused_computation.32 | convolution fusion | flops 913635840 | bytes 10635272 | tf_op jit(solution)/shard_map/nhf,hdf->nhd/dot_general | solution.py:111
  423.1 5.5 %fusion.15 = (bf16[768,2,384]{0,2,1:T(8,128)(2,1)S(1)}, bf16[768,2,384]{0,2,1:T(8,128)(2,1)}) fusion(f32[2,768,2,384]{1,3,2,0:T(8,128)} %fusion.51, f32[2,384,768]{2,1,0:T(8,128)} %get-tuple-element.57, f32[768,2]{0,1:T(2,128)} %add_sqrt_fusion.1, f32[768,2]{0,1:T(2,128)S(1)} %add_sqrt_fusion, f32[2,384,768]{2,1,0:T(8,128)} %get-tuple-element.59), kind=kLoop, calls=%fused_computation.24 | loop fusion | flops 3538944 | bytes 11808768 | tf_op jit(solution)/shard_map/convert_element_type | solution.py:116
  428.6 2.4 copy.57
  432.4 8.0 %fusion.16 = f32[2,768,1536]{2,1,0:T(8,128)} fusion(bf16[1,768,768]{2,1,0:T(8,128)(2,1)} %copy.57, bf16[1,768,768]{2,1,0:T(8,128)(2,1)} %copy.56, bf16[768,1536]{1,0:T(8,128)(2,1)S(1)} %copy-done), kind=kOutput, calls=%fused_computation.25 | convolution fusion | flops 3625058304 | bytes 14155776 | tf_op jit(solution)/shard_map/cnw,wm->cnm/dot_general | solution.py:119
  440.4 19.7 %reduce-scatter.2.cloned.1.call-done = f32[2,768,768]{2,1,0:T(8,128)} async-done(((f32[2,768,1536]{2,1,0:T(8,128)}), f32[2,768,768]{2,1,0:T(8,128)}) %reduce-scatter.2.cloned.1.call-update) | async-done | bytes 4718608 | tf_op jit(solution)/shard_map/reduce_scatter | solution.py:122
  460.2 4.0 convert_element_type.107
  (85 shorter events, 34.4 us)
Async XLA Ops:
  6.5 425.9 %copy-start = (bf16[768,1536]{1,0:T(8,128)(2,1)S(1)}, bf16[768,1536]{1,0:T(8,128)(2,1)}, u32[]{:S(2)}) copy-start(bf16[768,1536]{1,0:T(8,128)(2,1)} %param.15) | copy-start | bytes 7077892
  6.5 2.0 slice-start
  6.5 230.2 %all-reduce.8.cloned.1.call-start = ((), (), s32[]{:S(2)}) async-start(), calls=%async_computation.3 | async-start | bytes 7077888 | tf_op jit(solution)/shard_map/psum | solution.py:97
  9.9 219.9 %collective-permute-start = (bf16[2,384,768]{1,2,0:T(8,128)(2,1)}, bf16[2,384,768]{1,2,0:T(8,128)(2,1)}, u32[]{:S(2)}, u32[]{:S(2)}) collective-permute-start(bf16[2,384,768]{1,2,0:T(8,128)(2,1)} %copy.81), channel_id=1, source_target_pairs={{0,2},{2,4},{4,6},{6,8},{8,10},{10,12},{12,14},{14,16},{16,18},{18... | collective-permute-start | bytes 3538952 | tf_op jit(solution)/shard_map/ppermute | solution.py:17
  16.6 4.2 copy-start.1
  19.2 212.0 %collective-permute-start.1 = (bf16[2,384,768]{1,2,0:T(8,128)(2,1)}, bf16[2,384,768]{1,2,0:T(8,128)(2,1)}, u32[]{:S(2)}, u32[]{:S(2)}) collective-permute-start(bf16[2,384,768]{1,2,0:T(8,128)(2,1)} %slice.73), channel_id=1, source_target_pairs={{0,2},{2,4},{4,6},{6,8},{8,10},{10,12},{12,14},{14,16},{16,18},{18... | collective-permute-start | bytes 3538952 | tf_op jit(solution)/shard_map/ppermute | solution.py:17
  20.8 2.1 copy-start.3
  22.9 2.5 copy-start.9
  25.4 2.2 copy-start.10
  35.1 3.1 copy-start.14
  38.2 1.8 copy-start.13
  40.1 2.1 copy-start.7
  44.7 2.0 copy-start.19
  44.8 2.0 copy-start.20
  44.8 365.5 %all-reduce.6.cloned.1.call-start = ((), (), s32[]{:S(2)}) async-start(), calls=%async_computation.2 | async-start | bytes 7077888 | tf_op jit(solution)/shard_map/psum | solution.py:97
  223.3 4.6 copy-start.12
  232.6 2.1 copy-start.2
  234.7 2.1 copy-start.18
  236.7 4.1 copy-start.6
  240.8 1.1 copy-start.5
  240.8 1.9 copy-start.4
  241.9 1.7 copy-start.8
  241.9 1.7 copy-start.17
  251.6 208.6 %reduce-scatter.2.cloned.1.call-start = ((), (), s32[]{:S(2)}) async-start(), calls=%async_computation.1 | async-start | bytes 14155776 | tf_op jit(solution)/shard_map/reduce_scatter | solution.py:122
  276.9 12.0 %copy-start.11 = (bf16[1,768,768]{1,2,0:T(8,128)(2,1)S(1)}, bf16[1,768,768]{1,2,0:T(8,128)(2,1)}, u32[]{:S(2)}) copy-start(bf16[1,768,768]{1,2,0:T(8,128)(2,1)} %copy.80) | copy-start | bytes 3538948
  291.1 119.2 %copy-start.21 = (f32[2]{0:T(128)S(1)}, f32[2]{0:T(128)}, u32[]{:S(2)}) copy-start(f32[2]{0:T(128)} %get-tuple-element.14) | copy-start | bytes 28
  410.3 3.8 copy-start.15
  410.3 3.8 copy-start.16
Sparse Core Ops, SparseCore 0:
  44.9 143.3 all-reduce.7
  251.7 158.5 all-reduce.5
  440.5 19.5 reduce-scatter.1
where the time goes:
time: 472 us; the launch traced here: 471 us
  blocking collectives  170 us (36%)
  waiting for transfers between devices  131 us (28%)
  matrix products  74.2 us (16%)
  local copies, waits for them, and re-layouts  43.8 us (9%)
  other arithmetic  33.8 us (7%)
  between operations  13.3 us (3%)
    psum x1, blocking collectives, shards(): rate_total = lax.psum(jnp.sum(step_rates[:, block_at, :], axis=1), 'tok')  170 us
    psum x2, waiting for transfers between devices, shards(): lax.psum((grad_gate, grad_up, grad_down), 'tok')  111 us
    reduce_scatter x1, waiting for transfers between devices, shards(): lax.psum_scatter(partial_value, 'head', scatter_dimension=2, tiled=True)  19.7 us
    dot_general x2, matrix products, shards(): jnp.einsum('nhf,hdf->nhd', query_hidden, cast_down, preferred_element_typ...  13.1 us
    sub x1, matrix products, shards(): expos = jnp.exp(scores - row_max)  13 us
    unnamed x50, local copies, waits for them, and re-layouts  12.7 us
    dot_general x1, matrix products, shards(): jnp.einsum('chqk,ckhd->cqhd', weights_bf, value_heads, preferred_element_...  12 us
  transfers between devices with their start and end apart: 5, of which 2 were waited for; matrix products, arithmetic and copies ran while one was open for 21% of the time, Pallas kernels for 0%

commit v1 on v0

v1 whole, which is shorter than its diff:
```python
import functools
import math

import jax
import jax.numpy as jnp
from jax import lax
from jax.experimental import pallas as pl
from jax.experimental.pallas import tpu as pltpu
from jax.sharding import PartitionSpec as P

DH = 384
WINDOW = 384
EPSILON = 1e-06
BF16 = jnp.bfloat16
F32 = jnp.float32
TOKENS_AT_ONCE = 256
QUERY_TILE = 128

NT = (((1,), (1,)), ((), ()))
NN = (((1,), (0,)), ((), ()))


def dot(a, b, dims):
    return lax.dot_general(a, b, dims, preferred_element_type=F32)


def cost(flops, bytes_accessed, transcendentals=0):
    return pl.CostEstimate(
        flops=int(flops), bytes_accessed=int(bytes_accessed), transcendentals=int(transcendentals)
    )


def load_packed(packed_ref, flat, rows):
    for at in range(packed_ref.shape[0]):
        flat[at * rows : (at + 1) * rows, :] = packed_ref[at, :rows, :].astype(F32)


def gradient_kernel(first, block_at, rows, *refs):
    if first:
        key_ref, value_ref, rate_ref, gate_ref, up_ref, down_ref, out_ref, flat, sums = refs
        gate, up = gate_ref[...].astype(BF16), up_ref[...].astype(BF16)
        down_t = jnp.transpose(down_ref[...]).astype(BF16)
    else:
        key_ref, value_ref, rate_ref, packed_ref, out_ref, flat, sums = refs
        load_packed(packed_ref, flat, rows)
        gate, up = flat[:DH, :].astype(BF16), flat[DH : 2 * DH, :].astype(BF16)
        down_t = jnp.transpose(flat[2 * DH :, :]).astype(BF16)
    tokens = key_ref.shape[0]
    rates = rate_ref[block_at : block_at + 1, :]
    for at in range(tokens // TOKENS_AT_ONCE):
        piece = slice(at * TOKENS_AT_ONCE, (at + 1) * TOKENS_AT_ONCE)
        key, value = key_ref[piece, :], value_ref[piece, :]
        rate = rates[:, piece]
        pre_gate = dot(gate, key, NT)
        pre_up = dot(up, key, NT)
        backed = dot(down_t, value, NT) * rate
        sigmoid = jax.nn.sigmoid(pre_gate)
        active = pre_gate * sigmoid
        hidden = (active * pre_up * rate).astype(BF16)
        to_up = (backed * active).astype(BF16)
        slope = sigmoid * (1.0 + pre_gate * (1.0 - sigmoid))
        to_gate = (backed * pre_up * slope).astype(BF16)
        for which, (left, right) in enumerate(((to_gate, key), (to_up, key), (hidden, value))):
            term = dot(left, right, NN)
            if at == 0:
                sums[which] = term
            else:
                sums[which] += term
    flat[:DH, :] = sums[0]
    flat[DH : 2 * DH, :] = sums[1]
    flat[2 * DH :, :] = jnp.transpose(sums[2])
    total = jnp.sum(rates, axis=1, keepdims=True)
    high = total.astype(BF16)
    low = (total - high.astype(F32)).astype(BF16)
    extra = out_ref.shape[1] - rows
    place = lax.broadcasted_iota(jnp.int32, (extra, DH), 0)
    tail = jnp.where(place == 0, high.astype(F32), jnp.where(place == 1, low.astype(F32), 0.0))
    for at in range(out_ref.shape[0]):
        piece = jnp.concatenate([flat[at * rows : (at + 1) * rows, :], tail], axis=0)
        out_ref[at] = piece.astype(BF16)


def gradients(block_at, key_rows, value_rows, step_rates, weights, shards, rows, padded):
    _, tokens, width = key_rows.shape
    heads = width // DH
    first = len(weights) == 3
    matrix = pl.BlockSpec((None, DH, DH), lambda h: (h, 0, 0))
    per_head = shards // heads
    packed = pl.BlockSpec((per_head, padded, DH), lambda h: (h, 0, 0))
    rowed = pl.BlockSpec((None, tokens, DH), lambda h: (block_at, 0, h))
    return pl.pallas_call(
        functools.partial(gradient_kernel, first, block_at, rows),
        grid=(heads,),
        in_specs=[rowed, rowed, pl.BlockSpec((None, step_rates.shape[1], tokens), lambda h: (h, 0, 0))]
        + ([matrix] * 3 if first else [packed]),
        out_specs=packed,
        out_shape=jax.ShapeDtypeStruct((shards, padded, DH), BF16),
        scratch_shapes=[pltpu.VMEM((3 * DH, DH), F32), pltpu.VMEM((3, DH, DH), F32)],
        cost_estimate=cost(heads * 12 * tokens * DH * DH, 8e6, heads * tokens * DH * 2),
        name="gradients",
    )(key_rows, value_rows, step_rates, *weights)


def row_scale(matrix):
    return jnp.sqrt(jnp.mean(matrix * matrix, axis=-1, keepdims=True) + EPSILON)


def update_kernel(rows, parts_ref, old_ref, new_ref, copies_ref):
    total = parts_ref[0].astype(F32)
    for at in range(1, parts_ref.shape[0]):
        total += parts_ref[at].astype(F32)
    rate = total[rows : rows + 1, :] + total[rows + 1 : rows + 2, :]
    old = old_ref[...]
    updated = old + total / rate
    new = updated * (row_scale(old) / row_scale(updated))
    new_ref[...] = new
    rounded = new.astype(BF16)
    for at in range(copies_ref.shape[0]):
        copies_ref[at] = rounded


def update(parts, old, rows):
    shards, padded, _ = parts.shape
    return pl.pallas_call(
        functools.partial(update_kernel, rows),
        out_shape=(
            jax.ShapeDtypeStruct((padded, DH), F32),
            jax.ShapeDtypeStruct((shards, padded, DH), BF16),
        ),
        in_specs=[pl.BlockSpec(memory_space=pltpu.VMEM)] * 2,
        out_specs=(pl.BlockSpec(memory_space=pltpu.VMEM),) * 2,
        cost_estimate=cost(2 * shards * padded * DH, 4e6),
        name="update",
    )(parts, old)


def attend(query_ref, keys, values, out_ref, barred):
    scale = 1.0 / math.sqrt(DH)
    span = WINDOW + QUERY_TILE
    row = lax.broadcasted_iota(jnp.int32, (QUERY_TILE, span), 0)
    column = lax.broadcasted_iota(jnp.int32, (QUERY_TILE, span), 1)
    window = (column > row) & (column <= row + WINDOW)
    for at in range(query_ref.shape[0] // QUERY_TILE):
        low = at * QUERY_TILE
        scores = dot(query_ref[low : low + QUERY_TILE, :], keys[low : low + span, :], NT) * scale
        allowed = window if barred is None else window & (column + low >= barred)
        scores = jnp.where(allowed, scores, -jnp.inf)
        expos = jnp.exp(scores - jnp.max(scores, axis=1, keepdims=True))
        weights = (expos * (1.0 / jnp.sum(expos, axis=1, keepdims=True))).astype(BF16)
        out_ref[low : low + QUERY_TILE, :] = dot(weights, values[low : low + span, :], NN)


def local_kernel(query_ref, key_ref, value_ref, out_ref):
    attend(query_ref, key_ref, value_ref, out_ref, None)


def attention_cost(blocks, heads):
    pairs = blocks * heads * WINDOW * (WINDOW + QUERY_TILE)
    return cost(4 * pairs * DH, 10e6, pairs)


def local_attention(queries, key_rows, value_rows):
    blocks, tokens, width = queries.shape
    heads = width // DH
    last = tokens // WINDOW - 1
    return pl.pallas_call(
        local_kernel,
        grid=(blocks, heads),
        in_specs=[
            pl.BlockSpec((None, WINDOW, DH), lambda b, h: (b, last, h)),
            pl.BlockSpec((None, tokens, DH), lambda b, h: (b, 0, h)),
            pl.BlockSpec((None, tokens, DH), lambda b, h: (b, 0, h)),
        ],
        out_specs=pl.BlockSpec((None, WINDOW, DH), lambda b, h: (b, 0, h)),
        out_shape=jax.ShapeDtypeStruct((blocks, WINDOW, width), F32),
        cost_estimate=attention_cost(blocks, heads),
        name="local_attention",
    )(queries, key_rows, value_rows)


def near_kernel(place_ref, query_ref, near_key, near_value, key_ref, value_ref, out_ref, keys, values):
    keys[:WINDOW, :] = near_key[...]
    keys[WINDOW:, :] = key_ref[...]
    values[:WINDOW, :] = near_value[...]
    values[WINDOW:, :] = value_ref[...]
    absent = (place_ref[0] == 0) & (pl.program_id(0) == 0)
    attend(query_ref, keys, values, out_ref, jnp.where(absent, WINDOW, 0))


def near_attention(place, queries, near_keys, near_values, key_rows, value_rows):
    blocks, _, width = queries.shape
    heads = width // DH
    own = pl.BlockSpec((None, WINDOW, DH), lambda b, h, place: (b, 0, h))
    near = pl.BlockSpec(
        (None, WINDOW, DH),
        lambda b, h, place: (jnp.where(place[0] == 0, jnp.maximum(b - 1, 0), b), 0, h),
    )
    return pl.pallas_call(
        near_kernel,
        grid_spec=pltpu.PrefetchScalarGridSpec(
            num_scalar_prefetch=1,
            grid=(blocks, heads),
            in_specs=[own, near, near, own, own],
            out_specs=own,
            scratch_shapes=[pltpu.VMEM((2 * WINDOW, DH), BF16)] * 2,
        ),
        out_shape=jax.ShapeDtypeStruct((blocks, WINDOW, width), F32),
        cost_estimate=attention_cost(blocks, heads),
        name="near_attention",
    )(place, queries, near_keys, near_values, key_rows, value_rows)


def query_kernel(rows, query_ref, packed_ref, near_ref, local_ref, out_ref, flat):
    load_packed(packed_ref, flat, rows)
    gate, up = flat[:DH, :].astype(BF16), flat[DH : 2 * DH, :].astype(BF16)
    down = flat[2 * DH :, :].astype(BF16)
    for at in range(query_ref.shape[0] // WINDOW):
        piece = slice(at * WINDOW, (at + 1) * WINDOW)
        query = query_ref[piece, :]
        pre_gate = dot(query, gate, NT)
        hidden = (pre_gate * jax.nn.sigmoid(pre_gate) * dot(query, up, NT)).astype(BF16)
        fast = dot(hidden, down, NT)
        fast = fast / row_scale(fast)
        out_ref[piece, :] = (fast + (near_ref if at == 0 else local_ref)[...]).astype(BF16)


def query_heads(block_at, queries, packed, near, local, rows):
    _, tokens, width = queries.shape
    heads = width // DH
    shards, padded, _ = packed.shape
    piece = pl.BlockSpec((None, WINDOW, DH), lambda h: (block_at, 0, h))
    return pl.pallas_call(
        functools.partial(query_kernel, rows),
        grid=(heads,),
        in_specs=[
            pl.BlockSpec((None, tokens, DH), lambda h: (block_at, 0, h)),
            pl.BlockSpec((shards // heads, padded, DH), lambda h: (h, 0, 0)),
            piece,
            piece,
        ],
        out_specs=pl.BlockSpec((tokens, DH), lambda h: (0, h)),
        out_shape=jax.ShapeDtypeStruct((tokens, width), BF16),
        scratch_shapes=[pltpu.VMEM((3 * DH, DH), F32)],
        cost_estimate=cost(heads * 6 * tokens * DH * DH, 7e6, heads * tokens * DH),
        name="query_heads",
    )(queries, packed, near, local)


def output_kernel(side_ref, own_ref, other_ref, own_weight, other_weight, *refs):
    out_ref = refs[-1]
    total = dot(own_ref[...], own_weight[...], NN) + dot(other_ref[...], other_weight[...], NN)
    out_ref[...] = total.astype(BF16)


def output(block_at, blocks, side, own, other, weight, other_weight, into):
    tokens, width = own.shape
    tile = 256
    heads = pl.BlockSpec((tile, width), lambda t, side: (t, 0))
    operands = [side, own, other, weight, other_weight] + ([] if into is None else [into])
    return pl.pallas_call(
        output_kernel,
        grid_spec=pltpu.PrefetchScalarGridSpec(
            num_scalar_prefetch=1,
            grid=(tokens // tile,),
            in_specs=[
                heads,
                heads,
                pl.BlockSpec((width, width), lambda t, side: (0, side[0])),
                pl.BlockSpec((width, width), lambda t, side: (0, 0)),
            ]
            + ([] if into is None else [pl.BlockSpec(memory_space=pl.ANY)]),
            out_specs=pl.BlockSpec((None, tile, width), lambda t, side: (block_at, t, 0)),
        ),
        out_shape=jax.ShapeDtypeStruct((blocks, tokens, width), BF16),
        input_output_aliases={} if into is None else {5: 0},
        cost_estimate=cost(4 * tokens * width * width, 6e6),
        name="output",
    )(*operands)


def shards(queries, key_rows, value_rows, step_rates, gate_init, up_init, down_init, out_weight):
    blocks, tokens, width = queries.shape
    heads = width // DH
    count = lax.axis_size("tok")
    place = lax.axis_index("tok")
    side = lax.axis_index("head")
    ring = [(i, (i + 1) % count) for i in range(count)]
    swap = [(0, 1), (1, 0)]
    rows = heads * 3 * DH // count
    padded = -(-(rows + 2) // 8) * 8

    near_keys = lax.ppermute(key_rows[:, tokens - WINDOW :, :], "tok", ring)
    near_values = lax.ppermute(value_rows[:, tokens - WINDOW :, :], "tok", ring)
    sent_weight = lax.dynamic_slice_in_dim(out_weight, (1 - side) * width, width, 1)
    other_weight = lax.ppermute(sent_weight, "head", swap)

    exchange = lambda x: lax.all_to_all(x, "tok", split_axis=0, concat_axis=0, tiled=True)
    flat = jnp.concatenate([gate_init, up_init, down_init], axis=1).reshape(heads * 3 * DH, DH)
    flat = jnp.concatenate([flat, jnp.zeros((padded - rows, DH), F32)], axis=0)
    held = lax.dynamic_slice_in_dim(flat, place * rows, padded, 0)

    local = local_attention(queries, key_rows, value_rows)
    near = near_attention(
        place.reshape(1), queries, near_keys, near_values, key_rows, value_rows
    )
    weights = (gate_init, up_init, down_init)
    result = None
    for block_at in range(blocks):
        parts = gradients(
            block_at, key_rows, value_rows, step_rates, weights, count, rows, padded
        )
        held, copies = update(exchange(parts), held, rows)
        packed = exchange(copies)
        weights = (packed,)
        own = query_heads(block_at, queries, packed, near, local, rows)
        other = lax.ppermute(own, "head", swap)
        result = output(
            block_at, blocks, side.reshape(1), own, other, out_weight, other_weight, result
        )
    return result


def solution(mesh):
    in_specs = (
        P(None, "tok", "head"),
        P(None, "tok", "head"),
        P(None, "tok", "head"),
        P("head", None, "tok"),
        P("head", None, None),
        P("head", None, None),
        P("head", None, None),
        P("head", None),
    )
    out_specs = P(None, "tok", "head")
    return jax.shard_map(shards, mesh=mesh, in_specs=in_specs, out_specs=out_specs, check_vma=False)
```

time: 472 us -> 249 us (0.53)
  blocking collectives: 170 us -> 64.7 us
  matrix products: 74.2 us -> 0 us
  Pallas kernels: 0 us -> 61.7 us
  waiting for transfers between devices: 131 us -> 85.6 us
  local copies, waits for them, and re-layouts: 43.8 us -> 7.73 us
  other arithmetic: 33.8 us -> 1.86 us
  starting transfers between devices: 4.4 us -> 26.5 us
  between operations: 13.3 us -> 0.08 us
    psum x1 -> x0, blocking collectives: 170 us -> none  [shards(): rate_total = lax.psum(jnp.sum(step_rates[:, block_at, :], axis=1), 'tok')]
    psum x2 -> x0, waiting for transfers between devices: 111 us -> none  [shards(): lax.psum((grad_gate, grad_up, grad_down), 'tok')]
    all_to_all x0 -> x2, blocking collectives: none -> 64.7 us  [shards(): lax.all_to_all(x, 'tok', split_axis=0, concat_axis=0, tiled=True)]
    ppermute x2 -> x5, waiting for transfers between devices: 0.01 us -> 61.7 us  [the longest x1 36.4 us: shards(): near_keys = lax.ppermute(key_rows[:, tokens - WINDOW:, :], 'tok', ring)]
    pallas_call x0 -> x10, Pallas kernels: none -> 61.7 us  [the longest x2 15.6 us: gradients(): pl.pallas_call(functools.partial(gradient_kernel, first, block_at, rows),...]
    dot_general x18 -> x0, matrix products: 61.2 us -> none  [the longest x2 13.1 us: shards(): jnp.einsum('nhf,hdf->nhd', query_hidden, cast_down, preferred_element_typ...]
    all_to_all x0 -> x2, waiting for transfers between devices: none -> 23.9 us  [shards(): lax.all_to_all(x, 'tok', split_axis=0, concat_axis=0, tiled=True)]
    all_to_all x0 -> x2, starting transfers between devices: none -> 20.4 us  [shards(): lax.all_to_all(x, 'tok', split_axis=0, concat_axis=0, tiled=True)]
  transfers between devices with their start and end apart: 5 -> 7, of which waited for: 2 -> 3; matrix products, arithmetic and copies ran while one was open for 21% -> 2% of each run, Pallas kernels for 0% -> 14%
where the time goes in v1:
time: 249 us; the launch traced here: 248 us
  waiting for transfers between devices  85.6 us (34%)
  blocking collectives  64.7 us (26%)
  Pallas kernels  61.7 us (25%)
  starting transfers between devices  26.5 us (11%)
  local copies, waits for them, and re-layouts  7.73 us (3%)
    all_to_all x2, blocking collectives, shards(): lax.all_to_all(x, 'tok', split_axis=0, concat_axis=0, tiled=True)  64.7 us
    ppermute x1, waiting for transfers between devices, shards(): near_keys = lax.ppermute(key_rows[:, tokens - WINDOW:, :], 'tok', ring)  36.4 us
    ppermute x1, waiting for transfers between devices, shards(): near_values = lax.ppermute(value_rows[:, tokens - WINDOW:, :], 'tok', ring)  25.4 us
    all_to_all x2, waiting for transfers between devices, shards(): lax.all_to_all(x, 'tok', split_axis=0, concat_axis=0, tiled=True)  23.9 us
    all_to_all x2, starting transfers between devices, shards(): lax.all_to_all(x, 'tok', split_axis=0, concat_axis=0, tiled=True)  20.4 us
    pallas_call x2, Pallas kernels, gradients(): pl.pallas_call(functools.partial(gradient_kernel, first, block_at, rows),...  15.6 us
    pallas_call x2, Pallas kernels, query_heads(): pl.pallas_call(functools.partial(query_kernel, rows), grid=(heads,), in_s...  11.4 us
    pallas_call x2, Pallas kernels, output(): pl.pallas_call(output_kernel, grid_spec=pltpu.PrefetchScalarGridSpec(num_...  10.9 us
  transfers between devices with their start and end apart: 7, of which 3 were waited for; matrix products, arithmetic and copies ran while one was open for 2% of the time, Pallas kernels for 14%

profile of v1, /device:TPU:1, one launch (start us, length us, event | category | flops | bytes accessed | tf_op | source)
XLA Modules:
  0.0 248.2 jit_solution(8596734263601073203)
XLA Ops:
  0.0 7.9 %gradients.2 = bf16[64,40,384]{2,1,0:T(8,128)(2,1)} custom-call(bf16[2,768,768]{2,1,0:T(8,128)(2,1)} %key_ref.3, bf16[2,768,768]{2,1,0:T(8,128)(2,1)} %value_ref.3, f32[2,2,768]{2,1,0:T(2,128)} %refs_2_.3, f32[2,384,384]{2,1,0:T(8,128)} %refs_3_.1, f32[2,384,384]{2,1,0:T(8,128)} %refs_4_.1, f32[2,384,384]{2,1,0:T(8,128)} %refs_5_.1), custom_call_target="tpu_custom_call" | custom-call | flops 2717908992 | bytes 8000000 | tf_op jit(solution)/shard_map/gradients/pallas_call | solution.py:91
  7.9 12.1 %all-to-all-start = ((bf16[64,40,384]{2,1,0:T(8,128)(2,1)}), bf16[64,40,384]{2,1,0:T(8,128)(2,1)S(1)}, u32[]{:S(2)}, u32[]{:S(2)}) async-start(bf16[64,40,384]{2,1,0:T(8,128)(2,1)} %gradients.2), calls=%async_computation | async-start | bytes 3932160 | tf_op jit(solution)/shard_map/all_to_all | solution.py:297
  20.0 1.9 pad_maximum_fusion
  21.9 0.6 pad_dynamic-slice_fusion.old_ref
  22.5 23.9 %all-to-all-done.parts_ref = bf16[64,40,384]{2,1,0:T(8,128)(2,1)S(1)} async-done(((bf16[64,40,384]{2,1,0:T(8,128)(2,1)}), bf16[64,40,384]{2,1,0:T(8,128)(2,1)S(1)}, u32[]{:S(2)}, u32[]{:S(2)}) %all-to-all-start) | async-done | bytes 1966112 | tf_op jit(solution)/shard_map/all_to_all | solution.py:297
  46.4 1.3 copy-done.3
  47.6 3.4 %update.2 = (f32[40,384]{1,0:T(8,128)}, bf16[64,40,384]{2,1,0:T(8,128)(2,1)}) custom-call(bf16[64,40,384]{2,1,0:T(8,128)(2,1)} %copy-done.3, f32[40,384]{1,0:T(8,128)} %pad_dynamic-slice_fusion.old_ref), custom_call_target="tpu_custom_call" | custom-call | flops 1966080 | bytes 4000000 | tf_op jit(solution)/shard_map/update/pallas_call | solution.py:124
  51.0 32.0 %all_to_all.20.refs_3_.packed_ref = bf16[64,40,384]{2,1,0:T(8,128)(2,1)} all-to-all(bf16[64,40,384]{2,1,0:T(8,128)(2,1)} %get-tuple-element.8), channel_id=1, replica_groups=mesh['tok'=64,'head'=2] {'tok'}, dimensions={0} | all-to-all | bytes 3932160 | tf_op jit(solution)/shard_map/all_to_all | solution.py:297
  83.0 7.7 %gradients.3 = bf16[64,40,384]{2,1,0:T(8,128)(2,1)} custom-call(bf16[2,768,768]{2,1,0:T(8,128)(2,1)} %key_ref.3, bf16[2,768,768]{2,1,0:T(8,128)(2,1)} %value_ref.3, f32[2,2,768]{2,1,0:T(2,128)} %refs_2_.3, bf16[64,40,384]{2,1,0:T(8,128)(2,1)} %all_to_all.20.refs_3_.packed_ref), custom_call_target="tpu_custom_call" | custom-call | flops 2717908992 | bytes 8000000 | tf_op jit(solution)/shard_map/gradients/pallas_call | solution.py:91
  90.7 32.7 %all_to_all.21.parts_ref = bf16[64,40,384]{2,1,0:T(8,128)(2,1)} all-to-all(bf16[64,40,384]{2,1,0:T(8,128)(2,1)} %gradients.3), channel_id=1, replica_groups=mesh['tok'=64,'head'=2] {'tok'}, dimensions={0} | all-to-all | bytes 3932160 | tf_op jit(solution)/shard_map/all_to_all | solution.py:297
  123.5 3.4 %update.3 = (f32[40,384]{1,0:T(8,128)}, bf16[64,40,384]{2,1,0:T(8,128)(2,1)}) custom-call(bf16[64,40,384]{2,1,0:T(8,128)(2,1)} %all_to_all.21.parts_ref, f32[40,384]{1,0:T(8,128)} %get-tuple-element.9.old_ref), custom_call_target="tpu_custom_call" | custom-call | flops 1966080 | bytes 4000000 | tf_op jit(solution)/shard_map/update/pallas_call | solution.py:124
  126.9 8.3 %all-to-all-start.3 = ((bf16[64,40,384]{2,1,0:T(8,128)(2,1)}), bf16[64,40,384]{2,1,0:T(8,128)(2,1)}, u32[]{:S(2)}, u32[]{:S(2)}) async-start(bf16[64,40,384]{2,1,0:T(8,128)(2,1)} %get-tuple-element.10), calls=%async_computation.3 | async-start | bytes 3932160 | tf_op jit(solution)/shard_map/all_to_all | solution.py:297
  135.1 1.1 slice.6
  136.2 0.9 collective-permute-start
  137.2 0.0 copy-done.1
  137.2 1.1 slice.7
  138.3 1.1 collective-permute-start.1
  139.5 1.2 constant_dynamic-slice_fusion
  140.6 2.5 collective-permute-start.3
  143.1 8.5 %local_attention.1.local_ref = f32[2,384,768]{2,1,0:T(8,128)} custom-call(bf16[2,768,768]{2,1,0:T(8,128)(2,1)} %query_ref.7, bf16[2,768,768]{2,1,0:T(8,128)(2,1)} %key_ref.3, bf16[2,768,768]{2,1,0:T(8,128)(2,1)} %value_ref.3), custom_call_target="tpu_custom_call" | custom-call | flops 1207959552 | bytes 10000000 | tf_op jit(solution)/shard_map/local_attention/pallas_call | solution.py:166
  151.6 36.4 %collective-permute-done.near_key = bf16[2,384,768]{2,1,0:T(8,128)(2,1)S(1)} collective-permute-done((bf16[2,384,768]{2,1,0:T(8,128)(2,1)}, bf16[2,384,768]{2,1,0:T(8,128)(2,1)S(1)}, u32[]{:S(2)}, u32[]{:S(2)}) %collective-permute-start) | collective-permute-done | bytes 1179680 | tf_op jit(solution)/shard_map/ppermute | solution.py:292
  187.9 25.4 %collective-permute-done.1.near_value = bf16[2,384,768]{2,1,0:T(8,128)(2,1)} collective-permute-done((bf16[2,384,768]{2,1,0:T(8,128)(2,1)}, bf16[2,384,768]{2,1,0:T(8,128)(2,1)}, u32[]{:S(2)}, u32[]{:S(2)}) %collective-permute-start.1) | collective-permute-done | bytes 1179680 | tf_op jit(solution)/shard_map/ppermute | solution.py:293
  213.3 8.6 %near_attention.1.near_ref = f32[2,384,768]{2,1,0:T(8,128)} custom-call(s32[1]{0:T(128)} %bitcast.2.place_ref, bf16[2,768,768]{2,1,0:T(8,128)(2,1)} %query_ref.7, bf16[2,384,768]{2,1,0:T(8,128)(2,1)} %copy-done.6, bf16[2,384,768]{2,1,0:T(8,128)(2,1)} %collective-permute-done.1.near_value, bf16[2,768,768]{2,1,0:T(8,128)(2,1)} %key_ref.3, ...), custom_call_target="tpu_custom_call" | custom-call | flops 1207959552 | bytes 10000000 | tf_op jit(solution)/shard_map/near_attention/pallas_call | solution.py:198
  221.9 5.7 %query_heads.3.own_ref = bf16[768,768]{1,0:T(8,128)(2,1)} custom-call(bf16[2,768,768]{2,1,0:T(8,128)(2,1)} %query_ref.7, bf16[64,40,384]{2,1,0:T(8,128)(2,1)} %all_to_all.20.refs_3_.packed_ref, f32[2,384,768]{2,1,0:T(8,128)} %near_attention.1.near_ref, f32[2,384,768]{2,1,0:T(8,128)} %local_attention.1.local_ref), custom_call_target="tpu_custom_call" | custom-call | flops 1358954496 | bytes 7000000 | tf_op jit(solution)/shard_map/query_heads/pallas_call | solution.py:232
  227.6 1.6 collective-permute-start.4
  229.1 5.7 %query_heads.2.own_ref = bf16[768,768]{1,0:T(8,128)(2,1)} custom-call(bf16[2,768,768]{2,1,0:T(8,128)(2,1)} %query_ref.7, bf16[64,40,384]{2,1,0:T(8,128)(2,1)} %all-to-all-done.3.packed_ref, f32[2,384,768]{2,1,0:T(8,128)} %near_attention.1.near_ref, f32[2,384,768]{2,1,0:T(8,128)} %local_attention.1.local_ref), custom_call_target="tpu_custom_call" | custom-call | flops 1358954496 | bytes 7000000 | tf_op jit(solution)/shard_map/query_heads/pallas_call | solution.py:232
  234.8 0.0 collective-permute-start.2
  234.9 1.0 copy-done.5
  235.9 0.4 copy-done.7
  236.3 5.4 %output.2.refs_0_ = bf16[2,768,768]{2,1,0:T(8,128)(2,1)} custom-call(s32[1]{0:T(128)} %bitcast.side_ref, bf16[768,768]{1,0:T(8,128)(2,1)} %query_heads.3.own_ref, bf16[768,768]{1,0:T(8,128)(2,1)} %copy-done.7, bf16[768,1536]{1,0:T(8,128)(2,1)} %own_weight.3, bf16[768,768]{1,0:T(8,128)(2,1)} %copy-done.5), custom_call_target="tpu_custom_call" | custom-call | flops 1811939328 | bytes 6000000 | tf_op jit(solution)/shard_map/output/pallas_call | solution.py:260
  241.7 1.0 copy-done.8
  242.7 5.4 %output.3 = bf16[2,768,768]{2,1,0:T(8,128)(2,1)} custom-call(s32[1]{0:T(128)} %bitcast.side_ref, bf16[768,768]{1,0:T(8,128)(2,1)} %query_heads.2.own_ref, bf16[768,768]{1,0:T(8,128)(2,1)} %copy-done.8, bf16[768,1536]{1,0:T(8,128)(2,1)} %own_weight.3, bf16[768,768]{1,0:T(8,128)(2,1)} %copy-done.5, ...), custom_call_target="tpu_custom_call", output_to_operand_aliasing={{}: (5, {})} | custom-call | flops 1811939328 | bytes 6000000 | tf_op jit(solution)/shard_map/output/pallas_call | solution.py:260
  (17 shorter events, 0.0 us)
Async XLA Ops:
  7.9 12.1 %copy-start.4 = (f32[2,384,384]{2,1,0:T(8,128)S(1)}, f32[2,384,384]{2,1,0:T(8,128)}, u32[]{:S(2)}) copy-start(f32[2,384,384]{2,1,0:T(8,128)} %refs_3_.1) | copy-start | bytes 3538948
  7.9 38.5 %all-to-all-start = ((bf16[64,40,384]{2,1,0:T(8,128)(2,1)}), bf16[64,40,384]{2,1,0:T(8,128)(2,1)S(1)}, u32[]{:S(2)}, u32[]{:S(2)}) async-start(bf16[64,40,384]{2,1,0:T(8,128)(2,1)} %gradients.2), calls=%async_computation | async-start | bytes 3932160 | tf_op jit(solution)/shard_map/all_to_all | solution.py:297
  46.4 1.3 copy-start.3
  126.9 8.3 %copy-start = (bf16[2,768,768]{2,1,0:T(8,128)(2,1)S(1)}, bf16[2,768,768]{2,1,0:T(8,128)(2,1)}, u32[]{:S(2)}) copy-start(bf16[2,768,768]{2,1,0:T(8,128)(2,1)} %key_ref.3) | copy-start | bytes 7077892
  126.9 102.3 %all-to-all-start.3 = ((bf16[64,40,384]{2,1,0:T(8,128)(2,1)}), bf16[64,40,384]{2,1,0:T(8,128)(2,1)}, u32[]{:S(2)}, u32[]{:S(2)}) async-start(bf16[64,40,384]{2,1,0:T(8,128)(2,1)} %get-tuple-element.10), calls=%async_computation.3 | async-start | bytes 3932160 | tf_op jit(solution)/shard_map/all_to_all | solution.py:297
  135.1 2.1 copy-start.1
  136.2 3.2 %copy-start.2 = (bf16[768,1536]{1,0:T(8,128)(2,1)S(1)}, bf16[768,1536]{1,0:T(8,128)(2,1)}, u32[]{:S(2)}) copy-start(bf16[768,1536]{1,0:T(8,128)(2,1)} %own_weight.3) | copy-start | bytes 7077892
  136.2 51.7 %collective-permute-start = (bf16[2,384,768]{2,1,0:T(8,128)(2,1)}, bf16[2,384,768]{2,1,0:T(8,128)(2,1)S(1)}, u32[]{:S(2)}, u32[]{:S(2)}) collective-permute-start(bf16[2,384,768]{2,1,0:T(8,128)(2,1)} %slice.6), channel_id=1, source_target_pairs={{0,2},{2,4},{4,6},{6,8},{8,10},{10,12},{12,14},{14,16},{16,18},{18... | collective-permute-start | bytes 3538952 | tf_op jit(solution)/shard_map/ppermute | solution.py:292
  138.3 75.0 %collective-permute-start.1 = (bf16[2,384,768]{2,1,0:T(8,128)(2,1)}, bf16[2,384,768]{2,1,0:T(8,128)(2,1)}, u32[]{:S(2)}, u32[]{:S(2)}) collective-permute-start(bf16[2,384,768]{2,1,0:T(8,128)(2,1)} %slice.7), channel_id=1, source_target_pairs={{0,2},{2,4},{4,6},{6,8},{8,10},{10,12},{12,14},{14,16},{16,18},{18... | collective-permute-start | bytes 3538952 | tf_op jit(solution)/shard_map/ppermute | solution.py:293
  140.6 94.2 %collective-permute-start.3 = (bf16[768,768]{1,0:T(8,128)(2,1)}, bf16[768,768]{1,0:T(8,128)(2,1)S(1)}, u32[]{:S(2)}, u32[]{:S(2)}) collective-permute-start(bf16[768,768]{1,0:T(8,128)(2,1)} %constant_dynamic-slice_fusion), channel_id=1, source_target_pairs={{0,1},{1,0},{2,3},{3,2},{4,5},{5,4},{6,7},{7,6},{8,9},{9,8},{10,11... | collective-permute-start | bytes 3538952 | tf_op jit(solution)/shard_map/ppermute | solution.py:295
  187.9 25.4 %copy-start.6 = (bf16[2,384,768]{2,1,0:T(8,128)(2,1)}, bf16[2,384,768]{2,1,0:T(8,128)(2,1)S(1)}, u32[]{:S(2)}) copy-start(bf16[2,384,768]{2,1,0:T(8,128)(2,1)S(1)} %collective-permute-done.near_key) | copy-start | bytes 3538948
  227.6 7.3 %collective-permute-start.4 = (bf16[768,768]{1,0:T(8,128)(2,1)}, bf16[768,768]{1,0:T(8,128)(2,1)S(1)}, u32[]{:S(2)}, u32[]{:S(2)}) collective-permute-start(bf16[768,768]{1,0:T(8,128)(2,1)} %query_heads.3.own_ref), channel_id=1, source_target_pairs={{0,1},{1,0},{2,3},{3,2},{4,5},{5,4},{6,7},{7,6},{8,9},{9,8},{10,11... | collective-permute-start | bytes 3538952 | tf_op jit(solution)/shard_map/ppermute | solution.py:316
  234.8 6.9 %collective-permute-start.2 = (bf16[768,768]{1,0:T(8,128)(2,1)}, bf16[768,768]{1,0:T(8,128)(2,1)S(1)}, u32[]{:S(2)}, u32[]{:S(2)}) collective-permute-start(bf16[768,768]{1,0:T(8,128)(2,1)} %query_heads.2.own_ref), channel_id=1, source_target_pairs={{0,1},{1,0},{2,3},{3,2},{4,5},{5,4},{6,7},{7,6},{8,9},{9,8},{10,11... | collective-permute-start | bytes 3538952 | tf_op jit(solution)/shard_map/ppermute | solution.py:316
  234.8 1.1 copy-start.5
  234.9 1.4 copy-start.7
  241.7 1.0 copy-start.8

commit v2 on v1

--- a/solution.py
+++ b/solution.py
@@ -7,6 +7,7 @@
 from jax.experimental import pallas as pl
 from jax.experimental.pallas import tpu as pltpu
 from jax.sharding import PartitionSpec as P
+
 
 DH = 384
 WINDOW = 384
@@ -129,6 +130,7 @@
         ),
         in_specs=[pl.BlockSpec(memory_space=pltpu.VMEM)] * 2,
         out_specs=(pl.BlockSpec(memory_space=pltpu.VMEM),) * 2,
+        compiler_params=pltpu.CompilerParams(vmem_limit_bytes=32 * 2**20),
         cost_estimate=cost(2 * shards * padded * DH, 4e6),
         name="update",
     )(parts, old)
@@ -178,36 +180,44 @@
     )(queries, key_rows, value_rows)
 
 
-def near_kernel(place_ref, query_ref, near_key, near_value, key_ref, value_ref, out_ref, keys, values):
-    keys[:WINDOW, :] = near_key[...]
+def near_kernel(block_at, place_ref, query_ref, key_ref, value_ref, *refs):
+    near, (out_ref, keys, values) = refs[:-3], refs[-3:]
     keys[WINDOW:, :] = key_ref[...]
-    values[:WINDOW, :] = near_value[...]
     values[WINDOW:, :] = value_ref[...]
-    absent = (place_ref[0] == 0) & (pl.program_id(0) == 0)
-    attend(query_ref, keys, values, out_ref, jnp.where(absent, WINDOW, 0))
-
-
-def near_attention(place, queries, near_keys, near_values, key_rows, value_rows):
-    blocks, _, width = queries.shape
-    heads = width // DH
-    own = pl.BlockSpec((None, WINDOW, DH), lambda b, h, place: (b, 0, h))
-    near = pl.BlockSpec(
-        (None, WINDOW, DH),
-        lambda b, h, place: (jnp.where(place[0] == 0, jnp.maximum(b - 1, 0), b), 0, h),
-    )
-    return pl.pallas_call(
-        near_kernel,
+    keys[:WINDOW, :] = near[0][...]
+    values[:WINDOW, :] = near[1][...]
+    first = place_ref[0] == 0
+    barred = None
+    if block_at == 0:
+        barred = jnp.where(first, WINDOW, 0)
+    else:
+
+        @pl.when(first)
+        def _():
+            keys[:WINDOW, :] = near[2][...]
+            values[:WINDOW, :] = near[3][...]
+
+    attend(query_ref, keys, values, out_ref, barred)
+
+
+def near_attention(block_at, place, queries, key_rows, value_rows, near):
+    width = queries.shape[2]
+    heads = width // DH
+    own = pl.BlockSpec((None, WINDOW, DH), lambda h, place: (block_at, 0, h))
+    rows = pl.BlockSpec((WINDOW, DH), lambda h, place: (0, h))
+    return pl.pallas_call(
+        functools.partial(near_kernel, block_at),
         grid_spec=pltpu.PrefetchScalarGridSpec(
             num_scalar_prefetch=1,
-            grid=(blocks, heads),
-            in_specs=[own, near, near, own, own],
-            out_specs=own,
+            grid=(heads,),
+            in_specs=[own] * 3 + [rows] * len(near),
+            out_specs=rows,
             scratch_shapes=[pltpu.VMEM((2 * WINDOW, DH), BF16)] * 2,
         ),
-        out_shape=jax.ShapeDtypeStruct((blocks, WINDOW, width), F32),
-        cost_estimate=attention_cost(blocks, heads),
+        out_shape=jax.ShapeDtypeStruct((WINDOW, width), F32),
+        cost_estimate=attention_cost(1, heads),
         name="near_attention",
-    )(place, queries, near_keys, near_values, key_rows, value_rows)
+    )(place, queries, key_rows, value_rows, *near)
 
 
 def query_kernel(rows, query_ref, packed_ref, near_ref, local_ref, out_ref, flat):
@@ -228,15 +238,14 @@
     _, tokens, width = queries.shape
     heads = width // DH
     shards, padded, _ = packed.shape
-    piece = pl.BlockSpec((None, WINDOW, DH), lambda h: (block_at, 0, h))
     return pl.pallas_call(
         functools.partial(query_kernel, rows),
         grid=(heads,),
         in_specs=[
             pl.BlockSpec((None, tokens, DH), lambda h: (block_at, 0, h)),
             pl.BlockSpec((shards // heads, padded, DH), lambda h: (h, 0, 0)),
-            piece,
-            piece,
+            pl.BlockSpec((WINDOW, DH), lambda h: (0, h)),
+            pl.BlockSpec((None, WINDOW, DH), lambda h: (block_at, 0, h)),
         ],
         out_specs=pl.BlockSpec((tokens, DH), lambda h: (0, h)),
         out_shape=jax.ShapeDtypeStruct((tokens, width), BF16),
@@ -289,8 +298,9 @@
     rows = heads * 3 * DH // count
     padded = -(-(rows + 2) // 8) * 8
 
-    near_keys = lax.ppermute(key_rows[:, tokens - WINDOW :, :], "tok", ring)
-    near_values = lax.ppermute(value_rows[:, tokens - WINDOW :, :], "tok", ring)
+    near = []
+    for at, array in enumerate((key_rows, value_rows) * blocks):
+        near.append(lax.ppermute(array[at // 2, tokens - WINDOW :, :], "tok", ring))
     sent_weight = lax.dynamic_slice_in_dim(out_weight, (1 - side) * width, width, 1)
     other_weight = lax.ppermute(sent_weight, "head", swap)
 
@@ -300,19 +310,21 @@
     held = lax.dynamic_slice_in_dim(flat, place * rows, padded, 0)
 
     local = local_attention(queries, key_rows, value_rows)
-    near = near_attention(
-        place.reshape(1), queries, near_keys, near_values, key_rows, value_rows
-    )
+    nears = []
+    for block_at in range(blocks):
+        reach = near[2 * block_at : 2 * block_at + 2] + near[: 2 * block_at][-2:]
+        nears.append(
+            near_attention(block_at, place.reshape(1), queries, key_rows, value_rows, reach)
+        )
     weights = (gate_init, up_init, down_init)
     result = None
     for block_at in range(blocks):
-        parts = gradients(
-            block_at, key_rows, value_rows, step_rates, weights, count, rows, padded
-        )
-        held, copies = update(exchange(parts), held, rows)
+        parts = gradients(block_at, key_rows, value_rows, step_rates, weights, count, rows, padded)
+        parts = exchange(parts)
+        held, copies = update(parts, held, rows)
         packed = exchange(copies)
         weights = (packed,)
-        own = query_heads(block_at, queries, packed, near, local, rows)
+        own = query_heads(block_at, queries, packed, nears[block_at], local, rows)
         other = lax.ppermute(own, "head", swap)
         result = output(
             block_at, blocks, side.reshape(1), own, other, out_weight, other_weight, result

time: 249 us -> 234 us (0.940)
  waiting for transfers between devices: 85.6 us -> 69.1 us
  starting transfers between devices: 26.5 us -> 31.2 us
    ppermute x2 -> x4, waiting for transfers between devices: 61.7 us -> 44.6 us  [shards(): near.append(lax.ppermute(array[at // 2, tokens - WINDOW:, :], 'tok', ring))]
    pallas_call x2, Pallas kernels: 6.74 us -> 2.3 us  [update(): pl.pallas_call(functools.partial(update_kernel, rows), out_shape=(jax.Sha...]
    ppermute x2, starting transfers between devices: 1.59 us -> 4.31 us  [shards(): other = lax.ppermute(own, 'head', swap)]
    pallas_call x1 -> x2, Pallas kernels: 8.59 us -> 11.2 us  [near_attention(): pl.pallas_call(functools.partial(near_kernel, block_at), grid_spec=pltpu....]
  transfers between devices with their start and end apart: 7 -> 9, of which waited for: 3 -> 4; matrix products, arithmetic and copies ran while one was open for 2% -> 2% of each run, Pallas kernels for 14% -> 16%
where the time goes in v2:
time: 234 us
  waiting for transfers between devices  69.1 us (30%)
  blocking collectives  65.2 us (28%)
  Pallas kernels  59.8 us (26%)
  starting transfers between devices  31.2 us (13%)
  local copies, waits for them, and re-layouts  6.63 us (3%)
    all_to_all x2, blocking collectives, shards(): lax.all_to_all(x, 'tok', split_axis=0, concat_axis=0, tiled=True)  65.2 us
    ppermute x4, waiting for transfers between devices, shards(): near.append(lax.ppermute(array[at // 2, tokens - WINDOW:, :], 'tok', ring))  44.6 us
    all_to_all x2, waiting for transfers between devices, shards(): lax.all_to_all(x, 'tok', split_axis=0, concat_axis=0, tiled=True)  24.5 us
    all_to_all x2, starting transfers between devices, shards(): lax.all_to_all(x, 'tok', split_axis=0, concat_axis=0, tiled=True)  19.8 us
    pallas_call x2, Pallas kernels, gradients(): pl.pallas_call(functools.partial(gradient_kernel, first, block_at, rows),...  15.6 us
    pallas_call x2, Pallas kernels, query_heads(): pl.pallas_call(functools.partial(query_kernel, rows), grid=(heads,), in_s...  11.4 us
    pallas_call x2, Pallas kernels, near_attention(): pl.pallas_call(functools.partial(near_kernel, block_at), grid_spec=pltpu....  11.2 us
    pallas_call x2, Pallas kernels, output(): pl.pallas_call(output_kernel, grid_spec=pltpu.PrefetchScalarGridSpec(num_...  10.9 us
  transfers between devices with their start and end apart: 9, of which 4 were waited for; matrix products, arithmetic and copies ran while one was open for 2% of the time, Pallas kernels for 16%

profile of v2, /device:TPU:1, one launch (start us, length us, event | category | flops | bytes accessed | tf_op | source)
XLA Modules:
  0.0 233.8 jit_solution(11290405710966904991)
XLA Ops:
  0.0 7.9 %gradients.2 = bf16[64,40,384]{2,1,0:T(8,128)(2,1)} custom-call(bf16[2,768,768]{2,1,0:T(8,128)(2,1)} %key_ref.5, bf16[2,768,768]{2,1,0:T(8,128)(2,1)} %value_ref.5, f32[2,2,768]{2,1,0:T(2,128)} %refs_2_.3, f32[2,384,384]{2,1,0:T(8,128)} %refs_3_.1, f32[2,384,384]{2,1,0:T(8,128)} %refs_4_.1, f32[2,384,384]{2,1,0:T(8,128)} %refs_5_.1), custom_call_target="tpu_custom_call" | custom-call | flops 2717908992 | bytes 8000000 | tf_op jit(solution)/shard_map/gradients/pallas_call | solution.py:92
  7.9 12.1 %all-to-all-start = ((bf16[64,40,384]{2,1,0:T(8,128)(2,1)}), bf16[64,40,384]{2,1,0:T(8,128)(2,1)S(1)}, u32[]{:S(2)}, u32[]{:S(2)}) async-start(bf16[64,40,384]{2,1,0:T(8,128)(2,1)} %gradients.2), calls=%async_computation | async-start | bytes 3932160 | tf_op jit(solution)/shard_map/all_to_all | solution.py:307
  20.0 1.9 pad_maximum_fusion
  21.9 24.5 %all-to-all-done.parts_ref = bf16[64,40,384]{2,1,0:T(8,128)(2,1)S(1)} async-done(((bf16[64,40,384]{2,1,0:T(8,128)(2,1)}), bf16[64,40,384]{2,1,0:T(8,128)(2,1)S(1)}, u32[]{:S(2)}, u32[]{:S(2)}) %all-to-all-start) | async-done | bytes 1966112 | tf_op jit(solution)/shard_map/all_to_all | solution.py:307
  46.9 32.0 %all_to_all.20.refs_3_.packed_ref = bf16[64,40,384]{2,1,0:T(8,128)(2,1)} all-to-all(bf16[64,40,384]{2,1,0:T(8,128)(2,1)S(1)} %get-tuple-element.8), channel_id=1, replica_groups=mesh['tok'=64,'head'=2] {'tok'}, dimensions={0} | all-to-all | bytes 3932160 | tf_op jit(solution)/shard_map/all_to_all | solution.py:307
  78.9 7.7 %gradients.3 = bf16[64,40,384]{2,1,0:T(8,128)(2,1)} custom-call(bf16[2,768,768]{2,1,0:T(8,128)(2,1)} %key_ref.5, bf16[2,768,768]{2,1,0:T(8,128)(2,1)} %value_ref.5, f32[2,2,768]{2,1,0:T(2,128)} %refs_2_.3, bf16[64,40,384]{2,1,0:T(8,128)(2,1)} %all_to_all.20.refs_3_.packed_ref), custom_call_target="tpu_custom_call" | custom-call | flops 2717908992 | bytes 8000000 | tf_op jit(solution)/shard_map/gradients/pallas_call | solution.py:92
  86.6 33.2 %all_to_all.21.parts_ref = bf16[64,40,384]{2,1,0:T(8,128)(2,1)S(1)} all-to-all(bf16[64,40,384]{2,1,0:T(8,128)(2,1)} %gradients.3), channel_id=1, replica_groups=mesh['tok'=64,'head'=2] {'tok'}, dimensions={0} | all-to-all | bytes 3932160 | tf_op jit(solution)/shard_map/all_to_all | solution.py:307
  119.8 1.8 update.3
  121.6 7.7 %all-to-all-start.3 = ((bf16[64,40,384]{2,1,0:T(8,128)(2,1)}), bf16[64,40,384]{2,1,0:T(8,128)(2,1)}, u32[]{:S(2)}, u32[]{:S(2)}) async-start(bf16[64,40,384]{2,1,0:T(8,128)(2,1)} %get-tuple-element.10), calls=%async_computation.3 | async-start | bytes 3932160 | tf_op jit(solution)/shard_map/all_to_all | solution.py:307
  129.3 1.1 slice_bitcast_fusion.1
  130.4 0.9 collective-permute-start.2
  131.4 1.1 slice_bitcast_fusion
  132.4 1.1 collective-permute-start.3
  133.6 1.0 collective-permute-start
  134.6 1.1 collective-permute-start.1
  135.7 1.1 constant_dynamic-slice_fusion
  136.8 2.9 %collective-permute-start.5 = (bf16[768,768]{1,0:T(8,128)(2,1)}, bf16[768,768]{1,0:T(8,128)(2,1)S(1)}, u32[]{:S(2)}, u32[]{:S(2)}) collective-permute-start(bf16[768,768]{1,0:T(8,128)(2,1)} %constant_dynamic-slice_fusion), channel_id=1, source_target_pairs={{0,1},{1,0},{2,3},{3,2},{4,5},{5,4},{6,7},{7,6},{8,9},{9,8},{10,11... | collective-permute-start | bytes 3538952 | tf_op jit(solution)/shard_map/ppermute | solution.py:305
  139.7 8.4 %local_attention.1.local_ref = f32[2,384,768]{2,1,0:T(8,128)} custom-call(bf16[2,768,768]{2,1,0:T(8,128)(2,1)} %query_ref.9, bf16[2,768,768]{2,1,0:T(8,128)(2,1)} %key_ref.5, bf16[2,768,768]{2,1,0:T(8,128)(2,1)} %value_ref.5), custom_call_target="tpu_custom_call" | custom-call | flops 1207959552 | bytes 10000000 | tf_op jit(solution)/shard_map/local_attention/pallas_call | solution.py:168
  148.2 21.2 %collective-permute-done.2.refs_2_.refs_0_ = bf16[384,768]{1,0:T(8,128)(2,1)S(1)} collective-permute-done((bf16[384,768]{1,0:T(8,128)(2,1)}, bf16[384,768]{1,0:T(8,128)(2,1)S(1)}, u32[]{:S(2)}, u32[]{:S(2)}) %collective-permute-start.2) | collective-permute-done | bytes 589856 | tf_op jit(solution)/shard_map/ppermute | solution.py:303
  169.4 12.6 %collective-permute-done.3.refs_3_.refs_1_ = bf16[384,768]{1,0:T(8,128)(2,1)S(1)} collective-permute-done((bf16[384,768]{1,0:T(8,128)(2,1)}, bf16[384,768]{1,0:T(8,128)(2,1)S(1)}, u32[]{:S(2)}, u32[]{:S(2)}) %collective-permute-start.3) | collective-permute-done | bytes 589856 | tf_op jit(solution)/shard_map/ppermute | solution.py:303
  182.0 0.8 copy-done.6
  182.9 5.3 %near_attention.3.near_ref = f32[384,768]{1,0:T(8,128)} custom-call(s32[1]{0:T(128)} %bitcast.2.place_ref, bf16[2,768,768]{2,1,0:T(8,128)(2,1)} %query_ref.9, bf16[2,768,768]{2,1,0:T(8,128)(2,1)} %key_ref.5, bf16[2,768,768]{2,1,0:T(8,128)(2,1)} %value_ref.5, bf16[384,768]{1,0:T(8,128)(2,1)} %copy-done.5, bf16[384,768]{1,0:T(8,128)(2,1)} %copy-done.6), custom_call_target="tpu_custom_call" | custom-call | flops 603979776 | bytes 10000000 | tf_op jit(solution)/shard_map/near_attention/pallas_call | solution.py:208
  188.2 5.7 %query_heads.3.own_ref = bf16[768,768]{1,0:T(8,128)(2,1)} custom-call(bf16[2,768,768]{2,1,0:T(8,128)(2,1)} %query_ref.9, bf16[64,40,384]{2,1,0:T(8,128)(2,1)} %all_to_all.20.refs_3_.packed_ref, f32[384,768]{1,0:T(8,128)} %near_attention.3.near_ref, f32[2,384,768]{2,1,0:T(8,128)} %local_attention.1.local_ref), custom_call_target="tpu_custom_call" | custom-call | flops 1358954496 | bytes 7000000 | tf_op jit(solution)/shard_map/query_heads/pallas_call | solution.py:241
  194.0 2.7 %collective-permute-start.6 = (bf16[768,768]{1,0:T(8,128)(2,1)}, bf16[768,768]{1,0:T(8,128)(2,1)S(1)}, u32[]{:S(2)}, u32[]{:S(2)}) collective-permute-start(bf16[768,768]{1,0:T(8,128)(2,1)} %query_heads.3.own_ref), channel_id=1, source_target_pairs={{0,1},{1,0},{2,3},{3,2},{4,5},{5,4},{6,7},{7,6},{8,9},{9,8},{10,11... | collective-permute-start | bytes 3538952 | tf_op jit(solution)/shard_map/ppermute | solution.py:328
  196.7 10.7 %collective-permute-done.1.refs_1_ = bf16[384,768]{1,0:T(8,128)(2,1)} collective-permute-done((bf16[384,768]{1,0:T(8,128)(2,1)}, bf16[384,768]{1,0:T(8,128)(2,1)}, u32[]{:S(2)}, u32[]{:S(2)}) %collective-permute-start.1) | collective-permute-done | bytes 589856 | tf_op jit(solution)/shard_map/ppermute | solution.py:303
  207.4 5.8 %near_attention.2.near_ref = f32[384,768]{1,0:T(8,128)} custom-call(s32[1]{0:T(128)} %bitcast.2.place_ref, bf16[2,768,768]{2,1,0:T(8,128)(2,1)} %query_ref.9, bf16[2,768,768]{2,1,0:T(8,128)(2,1)} %key_ref.5, bf16[2,768,768]{2,1,0:T(8,128)(2,1)} %value_ref.5, bf16[384,768]{1,0:T(8,128)(2,1)} %collective-permute-done.refs_0_, ...), custom_call_target="tpu_custom_call" | custom-call | flops 603979776 | bytes 10000000 | tf_op jit(solution)/shard_map/near_attention/pallas_call | solution.py:208
  213.3 5.6 %query_heads.2.own_ref = bf16[768,768]{1,0:T(8,128)(2,1)} custom-call(bf16[2,768,768]{2,1,0:T(8,128)(2,1)} %query_ref.9, bf16[64,40,384]{2,1,0:T(8,128)(2,1)} %all-to-all-done.3.packed_ref, f32[384,768]{1,0:T(8,128)} %near_attention.2.near_ref, f32[2,384,768]{2,1,0:T(8,128)} %local_attention.1.local_ref), custom_call_target="tpu_custom_call" | custom-call | flops 1358954496 | bytes 7000000 | tf_op jit(solution)/shard_map/query_heads/pallas_call | solution.py:241
  218.9 1.6 collective-permute-start.4
  220.5 1.0 copy-done.4
  221.9 5.4 %output.2.refs_0_ = bf16[2,768,768]{2,1,0:T(8,128)(2,1)} custom-call(s32[1]{0:T(128)} %bitcast.side_ref, bf16[768,768]{1,0:T(8,128)(2,1)} %query_heads.3.own_ref, bf16[768,768]{1,0:T(8,128)(2,1)} %copy-done.7, bf16[768,1536]{1,0:T(8,128)(2,1)} %own_weight.3, bf16[768,768]{1,0:T(8,128)(2,1)} %copy-done.4), custom_call_target="tpu_custom_call" | custom-call | flops 1811939328 | bytes 6000000 | tf_op jit(solution)/shard_map/output/pallas_call | solution.py:269
  227.4 1.0 copy-done.8
  228.4 5.4 %output.3 = bf16[2,768,768]{2,1,0:T(8,128)(2,1)} custom-call(s32[1]{0:T(128)} %bitcast.side_ref, bf16[768,768]{1,0:T(8,128)(2,1)} %query_heads.2.own_ref, bf16[768,768]{1,0:T(8,128)(2,1)} %copy-done.8, bf16[768,1536]{1,0:T(8,128)(2,1)} %own_weight.3, bf16[768,768]{1,0:T(8,128)(2,1)} %copy-done.4, ...), custom_call_target="tpu_custom_call", output_to_operand_aliasing={{}: (5, {})} | custom-call | flops 1811939328 | bytes 6000000 | tf_op jit(solution)/shard_map/output/pallas_call | solution.py:269
  (22 shorter events, 1.0 us)
Async XLA Ops:
  7.9 12.1 %copy-start.3 = (f32[2,384,384]{2,1,0:T(8,128)S(1)}, f32[2,384,384]{2,1,0:T(8,128)}, u32[]{:S(2)}) copy-start(f32[2,384,384]{2,1,0:T(8,128)} %refs_3_.1) | copy-start | bytes 3538948
  7.9 38.5 %all-to-all-start = ((bf16[64,40,384]{2,1,0:T(8,128)(2,1)}), bf16[64,40,384]{2,1,0:T(8,128)(2,1)S(1)}, u32[]{:S(2)}, u32[]{:S(2)}) async-start(bf16[64,40,384]{2,1,0:T(8,128)(2,1)} %gradients.2), calls=%async_computation | async-start | bytes 3932160 | tf_op jit(solution)/shard_map/all_to_all | solution.py:307
  121.6 7.7 %copy-start = (bf16[2,768,768]{2,1,0:T(8,128)(2,1)S(1)}, bf16[2,768,768]{2,1,0:T(8,128)(2,1)}, u32[]{:S(2)}) copy-start(bf16[2,768,768]{2,1,0:T(8,128)(2,1)} %key_ref.5) | copy-start | bytes 7077892
  121.6 91.7 %all-to-all-start.3 = ((bf16[64,40,384]{2,1,0:T(8,128)(2,1)}), bf16[64,40,384]{2,1,0:T(8,128)(2,1)}, u32[]{:S(2)}, u32[]{:S(2)}) async-start(bf16[64,40,384]{2,1,0:T(8,128)(2,1)} %get-tuple-element.10), calls=%async_computation.3 | async-start | bytes 3932160 | tf_op jit(solution)/shard_map/all_to_all | solution.py:307
  129.3 2.1 copy-start.1
  130.4 5.3 %copy-start.2 = (bf16[768,1536]{1,0:T(8,128)(2,1)S(1)}, bf16[768,1536]{1,0:T(8,128)(2,1)}, u32[]{:S(2)}) copy-start(bf16[768,1536]{1,0:T(8,128)(2,1)} %own_weight.3) | copy-start | bytes 7077892
  130.4 39.0 %collective-permute-start.2 = (bf16[384,768]{1,0:T(8,128)(2,1)}, bf16[384,768]{1,0:T(8,128)(2,1)S(1)}, u32[]{:S(2)}, u32[]{:S(2)}) collective-permute-start(bf16[384,768]{1,0:T(8,128)(2,1)} %get-tuple-element.13), channel_id=1, source_target_pairs={{0,2},{2,4},{4,6},{6,8},{8,10},{10,12},{12,14},{14,16},{16,18},{18... | collective-permute-start | bytes 1769480 | tf_op jit(solution)/shard_map/ppermute | solution.py:303
  132.4 49.6 %collective-permute-start.3 = (bf16[384,768]{1,0:T(8,128)(2,1)}, bf16[384,768]{1,0:T(8,128)(2,1)S(1)}, u32[]{:S(2)}, u32[]{:S(2)}) collective-permute-start(bf16[384,768]{1,0:T(8,128)(2,1)} %get-tuple-element.11), channel_id=1, source_target_pairs={{0,2},{2,4},{4,6},{6,8},{8,10},{10,12},{12,14},{14,16},{16,18},{18... | collective-permute-start | bytes 1769480 | tf_op jit(solution)/shard_map/ppermute | solution.py:303
  133.6 63.1 %collective-permute-start = (bf16[384,768]{1,0:T(8,128)(2,1)}, bf16[384,768]{1,0:T(8,128)(2,1)}, u32[]{:S(2)}, u32[]{:S(2)}) collective-permute-start(bf16[384,768]{1,0:T(8,128)(2,1)} %get-tuple-element.14), channel_id=1, source_target_pairs={{0,2},{2,4},{4,6},{6,8},{8,10},{10,12},{12,14},{14,16},{16,18},{18... | collective-permute-start | bytes 1769480 | tf_op jit(solution)/shard_map/ppermute | solution.py:303
  134.6 72.9 %collective-permute-start.1 = (bf16[384,768]{1,0:T(8,128)(2,1)}, bf16[384,768]{1,0:T(8,128)(2,1)}, u32[]{:S(2)}, u32[]{:S(2)}) collective-permute-start(bf16[384,768]{1,0:T(8,128)(2,1)} %get-tuple-element.12), channel_id=1, source_target_pairs={{0,2},{2,4},{4,6},{6,8},{8,10},{10,12},{12,14},{14,16},{16,18},{18... | collective-permute-start | bytes 1769480 | tf_op jit(solution)/shard_map/ppermute | solution.py:303
  136.8 83.7 %collective-permute-start.5 = (bf16[768,768]{1,0:T(8,128)(2,1)}, bf16[768,768]{1,0:T(8,128)(2,1)S(1)}, u32[]{:S(2)}, u32[]{:S(2)}) collective-permute-start(bf16[768,768]{1,0:T(8,128)(2,1)} %constant_dynamic-slice_fusion), channel_id=1, source_target_pairs={{0,1},{1,0},{2,3},{3,2},{4,5},{5,4},{6,7},{7,6},{8,9},{9,8},{10,11... | collective-permute-start | bytes 3538952 | tf_op jit(solution)/shard_map/ppermute | solution.py:305
  169.4 12.6 %copy-start.5 = (bf16[384,768]{1,0:T(8,128)(2,1)}, bf16[384,768]{1,0:T(8,128)(2,1)S(1)}, u32[]{:S(2)}) copy-start(bf16[384,768]{1,0:T(8,128)(2,1)S(1)} %collective-permute-done.2.refs_2_.refs_0_) | copy-start | bytes 1769476
  182.0 0.9 copy-start.6
  194.0 26.5 %collective-permute-start.6 = (bf16[768,768]{1,0:T(8,128)(2,1)}, bf16[768,768]{1,0:T(8,128)(2,1)S(1)}, u32[]{:S(2)}, u32[]{:S(2)}) collective-permute-start(bf16[768,768]{1,0:T(8,128)(2,1)} %query_heads.3.own_ref), channel_id=1, source_target_pairs={{0,1},{1,0},{2,3},{3,2},{4,5},{5,4},{6,7},{7,6},{8,9},{9,8},{10,11... | collective-permute-start | bytes 3538952 | tf_op jit(solution)/shard_map/ppermute | solution.py:328
  218.9 8.5 %collective-permute-start.4 = (bf16[768,768]{1,0:T(8,128)(2,1)}, bf16[768,768]{1,0:T(8,128)(2,1)S(1)}, u32[]{:S(2)}, u32[]{:S(2)}) collective-permute-start(bf16[768,768]{1,0:T(8,128)(2,1)} %query_heads.2.own_ref), channel_id=1, source_target_pairs={{0,1},{1,0},{2,3},{3,2},{4,5},{5,4},{6,7},{7,6},{8,9},{9,8},{10,11... | collective-permute-start | bytes 3538952 | tf_op jit(solution)/shard_map/ppermute | solution.py:328
  220.5 1.0 copy-start.4
  220.5 1.4 copy-start.7
  227.4 1.0 copy-start.8

commit v3 on v2

--- a/solution.py
+++ b/solution.py
@@ -15,6 +15,7 @@
 BF16 = jnp.bfloat16
 F32 = jnp.float32
 TOKENS_AT_ONCE = 256
+LEAN = pltpu.CompilerParams(vmem_limit_bytes=36 * 2**20)
 QUERY_TILE = 128
 
 NT = (((1,), (1,)), ((), ()))
@@ -130,7 +131,7 @@
         ),
         in_specs=[pl.BlockSpec(memory_space=pltpu.VMEM)] * 2,
         out_specs=(pl.BlockSpec(memory_space=pltpu.VMEM),) * 2,
-        compiler_params=pltpu.CompilerParams(vmem_limit_bytes=32 * 2**20),
+        compiler_params=LEAN,
         cost_estimate=cost(2 * shards * padded * DH, 4e6),
         name="update",
     )(parts, old)
@@ -149,7 +150,8 @@
         scores = jnp.where(allowed, scores, -jnp.inf)
         expos = jnp.exp(scores - jnp.max(scores, axis=1, keepdims=True))
         weights = (expos * (1.0 / jnp.sum(expos, axis=1, keepdims=True))).astype(BF16)
-        out_ref[low : low + QUERY_TILE, :] = dot(weights, values[low : low + span, :], NN)
+        mixed = dot(weights, values[low : low + span, :], NN)
+        out_ref[low : low + QUERY_TILE, :] = mixed.astype(BF16)
 
 
 def local_kernel(query_ref, key_ref, value_ref, out_ref):
@@ -174,7 +176,7 @@
             pl.BlockSpec((None, tokens, DH), lambda b, h: (b, 0, h)),
         ],
         out_specs=pl.BlockSpec((None, WINDOW, DH), lambda b, h: (b, 0, h)),
-        out_shape=jax.ShapeDtypeStruct((blocks, WINDOW, width), F32),
+        out_shape=jax.ShapeDtypeStruct((blocks, WINDOW, width), BF16),
         cost_estimate=attention_cost(blocks, heads),
         name="local_attention",
     )(queries, key_rows, value_rows)
@@ -214,7 +216,7 @@
             out_specs=rows,
             scratch_shapes=[pltpu.VMEM((2 * WINDOW, DH), BF16)] * 2,
         ),
-        out_shape=jax.ShapeDtypeStruct((WINDOW, width), F32),
+        out_shape=jax.ShapeDtypeStruct((WINDOW, width), BF16),
         cost_estimate=attention_cost(1, heads),
         name="near_attention",
     )(place, queries, key_rows, value_rows, *near)
@@ -231,60 +233,91 @@
         hidden = (pre_gate * jax.nn.sigmoid(pre_gate) * dot(query, up, NT)).astype(BF16)
         fast = dot(hidden, down, NT)
         fast = fast / row_scale(fast)
-        out_ref[piece, :] = (fast + (near_ref if at == 0 else local_ref)[...]).astype(BF16)
-
-
-def query_heads(block_at, queries, packed, near, local, rows):
+        attended = (near_ref if at == 0 else local_ref)[...].astype(F32)
+        out_ref[piece, :] = (fast + attended).astype(BF16)
+
+
+def query_heads(block_at, first, heads, queries, packed, near, local, rows, params):
     _, tokens, width = queries.shape
-    heads = width // DH
     shards, padded, _ = packed.shape
+    per_head = shards * DH // width
     return pl.pallas_call(
         functools.partial(query_kernel, rows),
         grid=(heads,),
         in_specs=[
-            pl.BlockSpec((None, tokens, DH), lambda h: (block_at, 0, h)),
-            pl.BlockSpec((shards // heads, padded, DH), lambda h: (h, 0, 0)),
-            pl.BlockSpec((WINDOW, DH), lambda h: (0, h)),
-            pl.BlockSpec((None, WINDOW, DH), lambda h: (block_at, 0, h)),
+            pl.BlockSpec((None, tokens, DH), lambda h: (block_at, 0, first + h)),
+            pl.BlockSpec((per_head, padded, DH), lambda h: (first + h, 0, 0)),
+            pl.BlockSpec((WINDOW, DH), lambda h: (0, first + h)),
+            pl.BlockSpec((None, WINDOW, DH), lambda h: (block_at, 0, first + h)),
         ],
         out_specs=pl.BlockSpec((tokens, DH), lambda h: (0, h)),
-        out_shape=jax.ShapeDtypeStruct((tokens, width), BF16),
+        out_shape=jax.ShapeDtypeStruct((tokens, heads * DH), BF16),
         scratch_shapes=[pltpu.VMEM((3 * DH, DH), F32)],
-        cost_estimate=cost(heads * 6 * tokens * DH * DH, 7e6, heads * tokens * DH),
+        compiler_params=params,
+        cost_estimate=cost(heads * 6 * tokens * DH * DH, heads * 3.5e6, heads * tokens * DH),
         name="query_heads",
     )(queries, packed, near, local)
 
 
-def output_kernel(side_ref, own_ref, other_ref, own_weight, other_weight, *refs):
+def project_kernel(terms, has_sum, side_ref, *refs):
     out_ref = refs[-1]
-    total = dot(own_ref[...], own_weight[...], NN) + dot(other_ref[...], other_weight[...], NN)
-    out_ref[...] = total.astype(BF16)
-
-
-def output(block_at, blocks, side, own, other, weight, other_weight, into):
-    tokens, width = own.shape
+    total = refs[2 * terms][...] if has_sum else None
+    for at in range(terms):
+        term = dot(refs[2 * at][...], refs[2 * at + 1][...], NN)
+        total = term if total is None else total + term
+    out_ref[...] = total.astype(out_ref.dtype)
+
+
+def project(side, terms, tokens, summed=None, into=None, block_at=0, blocks=0, params=None):
     tile = 256
-    heads = pl.BlockSpec((tile, width), lambda t, side: (t, 0))
-    operands = [side, own, other, weight, other_weight] + ([] if into is None else [into])
-    return pl.pallas_call(
-        output_kernel,
+    specs, operands = [], []
+    columns = terms[0][1].shape[0]
+    for array, weight, first, own in terms:
+        depth = array.shape[1]
+        operands += [array, weight]
+        specs.append(pl.BlockSpec((tile, depth), lambda t, side: (t, 0)))
+        specs.append(
+            pl.BlockSpec(
+                (depth, columns),
+                lambda t, side, first=first, own=own: (first, side[0] if own else 0),
+            )
+        )
+    if summed is not None:
+        operands.append(summed)
+        specs.append(pl.BlockSpec((tile, columns), lambda t, side: (t, 0)))
+    if into is not None:
+        operands.append(into)
+        specs.append(pl.BlockSpec(memory_space=pl.ANY))
+    if blocks:
+        out_spec = pl.BlockSpec((None, tile, columns), lambda t, side: (block_at, t, 0))
+        out_shape = jax.ShapeDtypeStruct((blocks, tokens, columns), BF16)
+    else:
+        out_spec = pl.BlockSpec((tile, columns), lambda t, side: (t, 0))
+        out_shape = jax.ShapeDtypeStruct((tokens, columns), F32)
+    depth = sum(term[0].shape[1] for term in terms)
+    return pl.pallas_call(
+        functools.partial(project_kernel, len(terms), summed is not None),
         grid_spec=pltpu.PrefetchScalarGridSpec(
-            num_scalar_prefetch=1,
-            grid=(tokens // tile,),
-            in_specs=[
-                heads,
-                heads,
-                pl.BlockSpec((width, width), lambda t, side: (0, side[0])),
-                pl.BlockSpec((width, width), lambda t, side: (0, 0)),
-            ]
-            + ([] if into is None else [pl.BlockSpec(memory_space=pl.ANY)]),
-            out_specs=pl.BlockSpec((None, tile, width), lambda t, side: (block_at, t, 0)),
+            num_scalar_prefetch=1, grid=(tokens // tile,), in_specs=specs, out_specs=out_spec
         ),
-        out_shape=jax.ShapeDtypeStruct((blocks, tokens, width), BF16),
-        input_output_aliases={} if into is None else {5: 0},
-        cost_estimate=cost(4 * tokens * width * width, 6e6),
-        name="output",
-    )(*operands)
+        out_shape=out_shape,
+        input_output_aliases={} if into is None else {len(operands): 0},
+        compiler_params=params,
+        cost_estimate=cost(2 * tokens * columns * depth, 6e6),
+        name="project",
+    )(side, *operands)
+
+
+def exchange_order(count):
+    side = round(count ** (1 / 3))
+    if side**3 != count:
+        return list(range(count))
+    order = []
+    for step in range(count):
+        a, b, c = step // (side * side), step // side % side, step % side
+        x, y, z = a, b, c
+        order.append((x * side + y) * side + z)
+    return order
 
 
 def shards(queries, key_rows, value_rows, step_rates, gate_init, up_init, down_init, out_weight):
@@ -298,16 +331,24 @@
     rows = heads * 3 * DH // count
     padded = -(-(rows + 2) // 8) * 8
 
-    near = []
-    for at, array in enumerate((key_rows, value_rows) * blocks):
-        near.append(lax.ppermute(array[at // 2, tokens - WINDOW :, :], "tok", ring))
+    weights = (gate_init, up_init, down_init)
+    near = [lax.ppermute(key_rows[0, tokens - WINDOW :, :], "tok", ring)]
+    parts = gradients(0, key_rows, value_rows, step_rates, weights, count, rows, padded)
+    later_keys, later_values, parts = lax.optimization_barrier((key_rows, value_rows, parts))
+    for at, array in enumerate((later_keys, later_values) * blocks):
+        if at:
+            near.append(lax.ppermute(array[at // 2, tokens - WINDOW :, :], "tok", ring))
     sent_weight = lax.dynamic_slice_in_dim(out_weight, (1 - side) * width, width, 1)
     other_weight = lax.ppermute(sent_weight, "head", swap)
 
-    exchange = lambda x: lax.all_to_all(x, "tok", split_axis=0, concat_axis=0, tiled=True)
+    order = exchange_order(count)
+    exchange = lambda x: lax.all_to_all(
+        x, "tok", split_axis=0, concat_axis=0, tiled=True, axis_index_groups=[order]
+    )
     flat = jnp.concatenate([gate_init, up_init, down_init], axis=1).reshape(heads * 3 * DH, DH)
     flat = jnp.concatenate([flat, jnp.zeros((padded - rows, DH), F32)], axis=0)
-    held = lax.dynamic_slice_in_dim(flat, place * rows, padded, 0)
+    shard = jnp.asarray([order.index(i) for i in range(count)], jnp.int32)[place]
+    held = lax.dynamic_slice_in_dim(flat, shard * rows, padded, 0)
 
     local = local_attention(queries, key_rows, value_rows)
     nears = []
@@ -316,19 +357,29 @@
         nears.append(
             near_attention(block_at, place.reshape(1), queries, key_rows, value_rows, reach)
         )
-    weights = (gate_init, up_init, down_init)
     result = None
+    side_ref = side.reshape(1)
     for block_at in range(blocks):
-        parts = gradients(block_at, key_rows, value_rows, step_rates, weights, count, rows, padded)
+        last = block_at == blocks - 1
         parts = exchange(parts)
         held, copies = update(parts, held, rows)
         packed = exchange(copies)
-        weights = (packed,)
-        own = query_heads(block_at, queries, packed, nears[block_at], local, rows)
+        near_now = nears[block_at]
+        if not last:
+            parts = gradients(
+                block_at + 1, key_rows, value_rows, step_rates, (packed,), count, rows, padded
+            )
+            own = query_heads(
+                block_at, 0, heads, queries, packed, near_now, local, rows, None
+            )
+            other = lax.ppermute(own, "head", swap)
+            terms = [(own, out_weight, 0, True), (other, other_weight, 0, False)]
+            result = project(side_ref, terms, tokens, None, result, block_at, blocks)
+            continue
+        own = query_heads(block_at, 0, heads, queries, packed, near_now, local, rows, None)
         other = lax.ppermute(own, "head", swap)
-        result = output(
-            block_at, blocks, side.reshape(1), own, other, out_weight, other_weight, result
-        )
+        terms = [(own, out_weight, 0, True), (other, other_weight, 0, False)]
+        result = project(side_ref, terms, tokens, None, result, block_at, blocks, LEAN)
     return result
 
 

time: 234 us -> 234 us (level)
  local copies, waits for them, and re-layouts: 6.63 us -> 11.5 us
  waiting for transfers between devices: 69.1 us -> 65.4 us
    ppermute x4 -> x3, waiting for transfers between devices: 44.6 us -> 23.7 us  [shards(): near.append(lax.ppermute(array[at // 2, tokens - WINDOW:, :], 'tok', ring))]
    ppermute x0 -> x1, waiting for transfers between devices: none -> 17.3 us  [shards(): near = [lax.ppermute(key_rows[0, tokens - WINDOW:, :], 'tok', ring)]]
  transfers between devices with their start and end apart: 9 -> 9, of which waited for: 4 -> 4; matrix products, arithmetic and copies ran while one was open for 2% -> 4% of each run, Pallas kernels for 16% -> 15%
where the time goes in v3:
time: 234 us
  waiting for transfers between devices  65.4 us (28%)
  blocking collectives  65.2 us (28%)
  Pallas kernels  58.3 us (25%)
  starting transfers between devices  31.1 us (13%)
  local copies, waits for them, and re-layouts  11.5 us (5%)
    all_to_all x2, blocking collectives, shards(): lax.all_to_all(x, 'tok', split_axis=0, concat_axis=0, tiled=True, axis_in...  65.2 us
    all_to_all x2, waiting for transfers between devices, shards(): lax.all_to_all(x, 'tok', split_axis=0, concat_axis=0, tiled=True, axis_in...  24.5 us
    ppermute x3, waiting for transfers between devices, shards(): near.append(lax.ppermute(array[at // 2, tokens - WINDOW:, :], 'tok', ring))  23.7 us
    all_to_all x2, starting transfers between devices, shards(): lax.all_to_all(x, 'tok', split_axis=0, concat_axis=0, tiled=True, axis_in...  19.7 us
    ppermute x1, waiting for transfers between devices, shards(): near = [lax.ppermute(key_rows[0, tokens - WINDOW:, :], 'tok', ring)]  17.3 us
    pallas_call x2, Pallas kernels, gradients(): pl.pallas_call(functools.partial(gradient_kernel, first, block_at, rows),...  15.6 us
    pallas_call x2, Pallas kernels, query_heads(): pl.pallas_call(functools.partial(query_kernel, rows), grid=(heads,), in_s...  11 us
    pallas_call x2, Pallas kernels, near_attention(): pl.pallas_call(functools.partial(near_kernel, block_at), grid_spec=pltpu....  11 us
  transfers between devices with their start and end apart: 9, of which 4 were waited for; matrix products, arithmetic and copies ran while one was open for 4% of the time, Pallas kernels for 15%

profile of v3, /device:TPU:1, one launch (start us, length us, event | category | flops | bytes accessed | tf_op | source)
XLA Modules:
  0.0 233.5 jit_solution(14830784386016808570)
XLA Ops:
  0.0 7.9 %gradients.2 = bf16[64,40,384]{2,1,0:T(8,128)(2,1)} custom-call(bf16[2,768,768]{2,1,0:T(8,128)(2,1)} %key_ref.5, bf16[2,768,768]{2,1,0:T(8,128)(2,1)} %value_ref.5, f32[2,2,768]{2,1,0:T(2,128)} %refs_2_.3, f32[2,384,384]{2,1,0:T(8,128)} %refs_3_.1, f32[2,384,384]{2,1,0:T(8,128)} %refs_4_.1, f32[2,384,384]{2,1,0:T(8,128)} %refs_5_.1), custom_call_target="tpu_custom_call" | custom-call | flops 2717908992 | bytes 8000000 | tf_op jit(solution)/shard_map/gradients/pallas_call | solution.py:93
  7.9 12.1 %all-to-all-start = ((bf16[64,40,384]{2,1,0:T(8,128)(2,1)}), bf16[64,40,384]{2,1,0:T(8,128)(2,1)S(1)}, u32[]{:S(2)}, u32[]{:S(2)}) async-start(bf16[64,40,384]{2,1,0:T(8,128)(2,1)} %gradients.2), calls=%async_computation | async-start | bytes 3932160 | tf_op jit(solution)/shard_map/all_to_all | solution.py:345
  20.0 1.9 pad_maximum_fusion
  21.9 24.5 %all-to-all-done.parts_ref = bf16[64,40,384]{2,1,0:T(8,128)(2,1)S(1)} async-done(((bf16[64,40,384]{2,1,0:T(8,128)(2,1)}), bf16[64,40,384]{2,1,0:T(8,128)(2,1)S(1)}, u32[]{:S(2)}, u32[]{:S(2)}) %all-to-all-start) | async-done | bytes 1966112 | tf_op jit(solution)/shard_map/all_to_all | solution.py:345
  46.9 32.0 %all_to_all.20.refs_3_.packed_ref = bf16[64,40,384]{2,1,0:T(8,128)(2,1)} all-to-all(bf16[64,40,384]{2,1,0:T(8,128)(2,1)S(1)} %get-tuple-element.12), channel_id=1, replica_groups={{0,2,4,6,8,10,12,14,16,18,20,22,24,26,28,30,32,34,36,38,40,42,44,46,48,..., dimensions={0} | all-to-all | bytes 3932160 | tf_op jit(solution)/shard_map/all_to_all | solution.py:345
  78.9 7.7 %gradients.3 = bf16[64,40,384]{2,1,0:T(8,128)(2,1)} custom-call(bf16[2,768,768]{2,1,0:T(8,128)(2,1)} %key_ref.5, bf16[2,768,768]{2,1,0:T(8,128)(2,1)} %value_ref.5, f32[2,2,768]{2,1,0:T(2,128)} %refs_2_.3, bf16[64,40,384]{2,1,0:T(8,128)(2,1)} %all_to_all.20.refs_3_.packed_ref), custom_call_target="tpu_custom_call" | custom-call | flops 2717908992 | bytes 8000000 | tf_op jit(solution)/shard_map/gradients/pallas_call | solution.py:93
  86.6 33.2 %all_to_all.21.parts_ref = bf16[64,40,384]{2,1,0:T(8,128)(2,1)S(1)} all-to-all(bf16[64,40,384]{2,1,0:T(8,128)(2,1)} %gradients.3), channel_id=1, replica_groups={{0,2,4,6,8,10,12,14,16,18,20,22,24,26,28,30,32,34,36,38,40,42,44,46,48,..., dimensions={0} | all-to-all | bytes 3932160 | tf_op jit(solution)/shard_map/all_to_all | solution.py:345
  119.8 1.8 update.3
  121.6 7.6 %all-to-all-start.3 = ((bf16[64,40,384]{2,1,0:T(8,128)(2,1)}), bf16[64,40,384]{2,1,0:T(8,128)(2,1)}, u32[]{:S(2)}, u32[]{:S(2)}) async-start(bf16[64,40,384]{2,1,0:T(8,128)(2,1)} %get-tuple-element.14), calls=%async_computation.3 | async-start | bytes 3932160 | tf_op jit(solution)/shard_map/all_to_all | solution.py:345
  129.1 1.9 slice_bitcast_fusion.1
  131.1 0.9 collective-permute-start.2
  132.0 2.4 %slice_bitcast_fusion = (bf16[384,768]{1,0:T(8,128)(2,1)}, bf16[384,768]{1,0:T(8,128)(2,1)}) fusion(bf16[2,768,768]{2,1,0:T(8,128)(2,1)} %value_ref.5), kind=kLoop, calls=%fused_computation.2 | loop fusion | bytes 2359296 | tf_op jit(solution)/shard_map/squeeze | solution.py:340
  134.4 1.2 collective-permute-start.3
  135.6 1.9 slice_bitcast_fusion.3
  138.4 1.2 collective-permute-start.1
  139.6 1.1 constant_dynamic-slice_fusion
  140.7 3.0 %collective-permute-start.5 = (bf16[768,768]{1,0:T(8,128)(2,1)}, bf16[768,768]{1,0:T(8,128)(2,1)S(1)}, u32[]{:S(2)}, u32[]{:S(2)}) collective-permute-start(bf16[768,768]{1,0:T(8,128)(2,1)} %constant_dynamic-slice_fusion), channel_id=1, source_target_pairs={{0,1},{1,0},{2,3},{3,2},{4,5},{5,4},{6,7},{7,6},{8,9},{9,8},{10,11... | collective-permute-start | bytes 3538952 | tf_op jit(solution)/shard_map/ppermute | solution.py:342
  143.6 8.4 %local_attention.1.local_ref = bf16[2,384,768]{2,1,0:T(8,128)(2,1)} custom-call(bf16[2,768,768]{2,1,0:T(8,128)(2,1)} %query_ref.9, bf16[2,768,768]{2,1,0:T(8,128)(2,1)} %key_ref.5, bf16[2,768,768]{2,1,0:T(8,128)(2,1)} %value_ref.5), custom_call_target="tpu_custom_call" | custom-call | flops 1207959552 | bytes 10000000 | tf_op jit(solution)/shard_map/local_attention/pallas_call | solution.py:170
  152.0 17.3 %collective-permute-done.2.refs_2_.refs_0_ = bf16[384,768]{1,0:T(8,128)(2,1)S(1)} collective-permute-done((bf16[384,768]{1,0:T(8,128)(2,1)}, bf16[384,768]{1,0:T(8,128)(2,1)S(1)}, u32[]{:S(2)}, u32[]{:S(2)}) %collective-permute-start.2) | collective-permute-done | bytes 589856 | tf_op jit(solution)/shard_map/ppermute | solution.py:335
  169.3 12.6 %collective-permute-done.3.refs_3_.refs_1_ = bf16[384,768]{1,0:T(8,128)(2,1)S(1)} collective-permute-done((bf16[384,768]{1,0:T(8,128)(2,1)}, bf16[384,768]{1,0:T(8,128)(2,1)S(1)}, u32[]{:S(2)}, u32[]{:S(2)}) %collective-permute-start.3) | collective-permute-done | bytes 589856 | tf_op jit(solution)/shard_map/ppermute | solution.py:340
  182.7 5.2 %near_attention.3.near_ref = bf16[384,768]{1,0:T(8,128)(2,1)} custom-call(s32[1]{0:T(128)} %bitcast.2.place_ref, bf16[2,768,768]{2,1,0:T(8,128)(2,1)} %query_ref.9, bf16[2,768,768]{2,1,0:T(8,128)(2,1)} %key_ref.5, bf16[2,768,768]{2,1,0:T(8,128)(2,1)} %value_ref.5, bf16[384,768]{1,0:T(8,128)(2,1)} %copy-done.6, bf16[384,768]{1,0:T(8,128)(2,1)} %copy-done.7), custom_call_target="tpu_custom_call" | custom-call | flops 603979776 | bytes 10000000 | tf_op jit(solution)/shard_map/near_attention/pallas_call | solution.py:210
  188.0 5.5 %query_heads.3.refs_0_ = bf16[768,768]{1,0:T(8,128)(2,1)} custom-call(bf16[2,768,768]{2,1,0:T(8,128)(2,1)} %query_ref.9, bf16[64,40,384]{2,1,0:T(8,128)(2,1)} %all_to_all.20.refs_3_.packed_ref, bf16[384,768]{1,0:T(8,128)(2,1)} %near_attention.3.near_ref, bf16[2,384,768]{2,1,0:T(8,128)(2,1)} %local_attention.1.local_ref), custom_call_target="tpu_custom_call" | custom-call | flops 1358954496 | bytes 7000000 | tf_op jit(solution)/shard_map/query_heads/pallas_call | solution.py:244
  193.5 2.7 %collective-permute-start.6 = (bf16[768,768]{1,0:T(8,128)(2,1)}, bf16[768,768]{1,0:T(8,128)(2,1)S(1)}, u32[]{:S(2)}, u32[]{:S(2)}) collective-permute-start(bf16[768,768]{1,0:T(8,128)(2,1)} %query_heads.3.refs_0_), channel_id=1, source_target_pairs={{0,1},{1,0},{2,3},{3,2},{4,5},{5,4},{6,7},{7,6},{8,9},{9,8},{10,11... | collective-permute-start | bytes 3538952 | tf_op jit(solution)/shard_map/ppermute | solution.py:375
  196.2 11.1 %collective-permute-done.1.refs_1_ = bf16[384,768]{1,0:T(8,128)(2,1)} collective-permute-done((bf16[384,768]{1,0:T(8,128)(2,1)}, bf16[384,768]{1,0:T(8,128)(2,1)}, u32[]{:S(2)}, u32[]{:S(2)}) %collective-permute-start.1) | collective-permute-done | bytes 589856 | tf_op jit(solution)/shard_map/ppermute | solution.py:340
  207.3 5.7 %near_attention.2.near_ref = bf16[384,768]{1,0:T(8,128)(2,1)} custom-call(s32[1]{0:T(128)} %bitcast.2.place_ref, bf16[2,768,768]{2,1,0:T(8,128)(2,1)} %query_ref.9, bf16[2,768,768]{2,1,0:T(8,128)(2,1)} %key_ref.5, bf16[2,768,768]{2,1,0:T(8,128)(2,1)} %value_ref.5, bf16[384,768]{1,0:T(8,128)(2,1)} %collective-permute-done.refs_0_, ...), custom_call_target="tpu_custom_call" | custom-call | flops 603979776 | bytes 10000000 | tf_op jit(solution)/shard_map/near_attention/pallas_call | solution.py:210
  213.0 5.5 %query_heads.2.refs_0_ = bf16[768,768]{1,0:T(8,128)(2,1)} custom-call(bf16[2,768,768]{2,1,0:T(8,128)(2,1)} %query_ref.9, bf16[64,40,384]{2,1,0:T(8,128)(2,1)} %all-to-all-done.3.packed_ref, bf16[384,768]{1,0:T(8,128)(2,1)} %near_attention.2.near_ref, bf16[2,384,768]{2,1,0:T(8,128)(2,1)} %local_attention.1.local_ref), custom_call_target="tpu_custom_call" | custom-call | flops 1358954496 | bytes 7000000 | tf_op jit(solution)/shard_map/query_heads/pallas_call | solution.py:244
  218.5 1.6 collective-permute-start.4
  220.1 1.0 copy-done.3
  221.2 1.0 copy-done.8
  222.2 5.6 %project.2.refs_4_ = bf16[2,768,768]{2,1,0:T(8,128)(2,1)} custom-call(s32[1]{0:T(128)} %bitcast.side_ref, bf16[768,768]{1,0:T(8,128)(2,1)} %query_heads.3.refs_0_, bf16[768,1536]{1,0:T(8,128)(2,1)} %refs_1_.7, bf16[768,768]{1,0:T(8,128)(2,1)} %copy-done.8, bf16[768,768]{1,0:T(8,128)(2,1)} %copy-done.3), custom_call_target="tpu_custom_call" | custom-call | flops 1811939328 | bytes 6000000 | tf_op jit(solution)/shard_map/project/pallas_call | solution.py:298
  227.8 1.3 copy-done.4
  229.1 4.4 %project.3 = bf16[2,768,768]{2,1,0:T(8,128)(2,1)} custom-call(s32[1]{0:T(128)} %bitcast.side_ref, bf16[768,768]{1,0:T(8,128)(2,1)S(1)} %copy-done.2, bf16[768,1536]{1,0:T(8,128)(2,1)S(1)} %copy-done.1, bf16[768,768]{1,0:T(8,128)(2,1)} %collective-permute-done.4.refs_2_, bf16[768,768]{1,0:T(8,128)(2,1)S(1)} %copy-done.4, ...), custom_call_target="tpu_custom_call", output_to_operand_aliasing={{}: (5, {})} | custom-call | flops 1811939328 | bytes 6000000 | tf_op jit(solution)/shard_map/project/pallas_call | solution.py:298
  (23 shorter events, 2.3 us)
Async XLA Ops:
  7.9 12.1 %copy-start.5 = (f32[2,384,384]{2,1,0:T(8,128)S(1)}, f32[2,384,384]{2,1,0:T(8,128)}, u32[]{:S(2)}) copy-start(f32[2,384,384]{2,1,0:T(8,128)} %refs_3_.1) | copy-start | bytes 3538948
  7.9 38.5 %all-to-all-start = ((bf16[64,40,384]{2,1,0:T(8,128)(2,1)}), bf16[64,40,384]{2,1,0:T(8,128)(2,1)S(1)}, u32[]{:S(2)}, u32[]{:S(2)}) async-start(bf16[64,40,384]{2,1,0:T(8,128)(2,1)} %gradients.2), calls=%async_computation | async-start | bytes 3932160 | tf_op jit(solution)/shard_map/all_to_all | solution.py:345
  121.6 91.5 %all-to-all-start.3 = ((bf16[64,40,384]{2,1,0:T(8,128)(2,1)}), bf16[64,40,384]{2,1,0:T(8,128)(2,1)}, u32[]{:S(2)}, u32[]{:S(2)}) async-start(bf16[64,40,384]{2,1,0:T(8,128)(2,1)} %get-tuple-element.14), calls=%async_computation.3 | async-start | bytes 3932160 | tf_op jit(solution)/shard_map/all_to_all | solution.py:345
  131.1 8.5 %copy-start = (bf16[768,1536]{1,0:T(8,128)(2,1)S(1)}, bf16[768,1536]{1,0:T(8,128)(2,1)}, u32[]{:S(2)}) copy-start(bf16[768,1536]{1,0:T(8,128)(2,1)} %refs_1_.7) | copy-start | bytes 7077892
  131.1 38.2 %collective-permute-start.2 = (bf16[384,768]{1,0:T(8,128)(2,1)}, bf16[384,768]{1,0:T(8,128)(2,1)S(1)}, u32[]{:S(2)}, u32[]{:S(2)}) collective-permute-start(bf16[384,768]{1,0:T(8,128)(2,1)} %slice_bitcast_fusion.1), channel_id=1, source_target_pairs={{0,2},{2,4},{4,6},{6,8},{8,10},{10,12},{12,14},{14,16},{16,18},{18... | collective-permute-start | bytes 1769480 | tf_op jit(solution)/shard_map/ppermute | solution.py:335
  134.4 47.5 %collective-permute-start.3 = (bf16[384,768]{1,0:T(8,128)(2,1)}, bf16[384,768]{1,0:T(8,128)(2,1)S(1)}, u32[]{:S(2)}, u32[]{:S(2)}) collective-permute-start(bf16[384,768]{1,0:T(8,128)(2,1)} %get-tuple-element.17), channel_id=1, source_target_pairs={{0,2},{2,4},{4,6},{6,8},{8,10},{10,12},{12,14},{14,16},{16,18},{18... | collective-permute-start | bytes 1769480 | tf_op jit(solution)/shard_map/ppermute | solution.py:340
  137.5 58.7 %collective-permute-start = (bf16[384,768]{1,0:T(8,128)(2,1)}, bf16[384,768]{1,0:T(8,128)(2,1)}, u32[]{:S(2)}, u32[]{:S(2)}) collective-permute-start(bf16[384,768]{1,0:T(8,128)(2,1)} %slice_bitcast_fusion.3), channel_id=1, source_target_pairs={{0,2},{2,4},{4,6},{6,8},{8,10},{10,12},{12,14},{14,16},{16,18},{18... | collective-permute-start | bytes 1769480 | tf_op jit(solution)/shard_map/ppermute | solution.py:340
  138.4 68.9 %collective-permute-start.1 = (bf16[384,768]{1,0:T(8,128)(2,1)}, bf16[384,768]{1,0:T(8,128)(2,1)}, u32[]{:S(2)}, u32[]{:S(2)}) collective-permute-start(bf16[384,768]{1,0:T(8,128)(2,1)} %get-tuple-element.18), channel_id=1, source_target_pairs={{0,2},{2,4},{4,6},{6,8},{8,10},{10,12},{12,14},{14,16},{16,18},{18... | collective-permute-start | bytes 1769480 | tf_op jit(solution)/shard_map/ppermute | solution.py:340
  140.7 79.4 %collective-permute-start.5 = (bf16[768,768]{1,0:T(8,128)(2,1)}, bf16[768,768]{1,0:T(8,128)(2,1)S(1)}, u32[]{:S(2)}, u32[]{:S(2)}) collective-permute-start(bf16[768,768]{1,0:T(8,128)(2,1)} %constant_dynamic-slice_fusion), channel_id=1, source_target_pairs={{0,1},{1,0},{2,3},{3,2},{4,5},{5,4},{6,7},{7,6},{8,9},{9,8},{10,11... | collective-permute-start | bytes 3538952 | tf_op jit(solution)/shard_map/ppermute | solution.py:342
  169.3 12.6 %copy-start.6 = (bf16[384,768]{1,0:T(8,128)(2,1)}, bf16[384,768]{1,0:T(8,128)(2,1)S(1)}, u32[]{:S(2)}) copy-start(bf16[384,768]{1,0:T(8,128)(2,1)S(1)} %collective-permute-done.2.refs_2_.refs_0_) | copy-start | bytes 1769476
  181.9 0.8 copy-start.7
  193.5 26.6 %collective-permute-start.6 = (bf16[768,768]{1,0:T(8,128)(2,1)}, bf16[768,768]{1,0:T(8,128)(2,1)S(1)}, u32[]{:S(2)}, u32[]{:S(2)}) collective-permute-start(bf16[768,768]{1,0:T(8,128)(2,1)} %query_heads.3.refs_0_), channel_id=1, source_target_pairs={{0,1},{1,0},{2,3},{3,2},{4,5},{5,4},{6,7},{7,6},{8,9},{9,8},{10,11... | collective-permute-start | bytes 3538952 | tf_op jit(solution)/shard_map/ppermute | solution.py:375
  218.5 9.2 %collective-permute-start.4 = (bf16[768,768]{1,0:T(8,128)(2,1)}, bf16[768,768]{1,0:T(8,128)(2,1)}, u32[]{:S(2)}, u32[]{:S(2)}) collective-permute-start(bf16[768,768]{1,0:T(8,128)(2,1)} %query_heads.2.refs_0_), channel_id=1, source_target_pairs={{0,1},{1,0},{2,3},{3,2},{4,5},{5,4},{6,7},{7,6},{8,9},{9,8},{10,11... | collective-permute-start | bytes 3538952 | tf_op jit(solution)/shard_map/ppermute | solution.py:380
  220.1 1.0 copy-start.3
  221.2 1.0 copy-start.8
  222.2 5.6 %copy-start.1 = (bf16[768,1536]{1,0:T(8,128)(2,1)S(1)}, bf16[768,1536]{1,0:T(8,128)(2,1)}, u32[]{:S(2)}) copy-start(bf16[768,1536]{1,0:T(8,128)(2,1)} %refs_1_.7) | copy-start | bytes 7077892
  222.2 5.6 %copy-start.2 = (bf16[768,768]{1,0:T(8,128)(2,1)S(1)}, bf16[768,768]{1,0:T(8,128)(2,1)}, u32[]{:S(2)}) copy-start(bf16[768,768]{1,0:T(8,128)(2,1)} %query_heads.2.refs_0_) | copy-start | bytes 3538948
  227.8 1.3 copy-start.4

commit v4 on v3

--- a/solution.py
+++ b/solution.py
@@ -14,7 +14,8 @@
 EPSILON = 1e-06
 BF16 = jnp.bfloat16
 F32 = jnp.float32
-TOKENS_AT_ONCE = 256
+LANES = 128
+PARTS = DH // LANES
 LEAN = pltpu.CompilerParams(vmem_limit_bytes=36 * 2**20)
 QUERY_TILE = 128
 
@@ -34,52 +35,48 @@
 
 def load_packed(packed_ref, flat, rows):
     for at in range(packed_ref.shape[0]):
-        flat[at * rows : (at + 1) * rows, :] = packed_ref[at, :rows, :].astype(F32)
+        shard = packed_ref[at].astype(F32)
+        for part in range(PARTS):
+            columns = slice(part * LANES, (part + 1) * LANES)
+            flat[at * rows : (at + 1) * rows, columns] = shard[part * rows : (part + 1) * rows, :]
 
 
 def gradient_kernel(first, block_at, rows, *refs):
     if first:
-        key_ref, value_ref, rate_ref, gate_ref, up_ref, down_ref, out_ref, flat, sums = refs
+        key_ref, value_ref, rate_ref, gate_ref, up_ref, down_ref, out_ref, flat = refs
         gate, up = gate_ref[...].astype(BF16), up_ref[...].astype(BF16)
         down_t = jnp.transpose(down_ref[...]).astype(BF16)
     else:
-        key_ref, value_ref, rate_ref, packed_ref, out_ref, flat, sums = refs
+        key_ref, value_ref, rate_ref, packed_ref, out_ref, flat = refs
         load_packed(packed_ref, flat, rows)
         gate, up = flat[:DH, :].astype(BF16), flat[DH : 2 * DH, :].astype(BF16)
         down_t = jnp.transpose(flat[2 * DH :, :]).astype(BF16)
-    tokens = key_ref.shape[0]
-    rates = rate_ref[block_at : block_at + 1, :]
-    for at in range(tokens // TOKENS_AT_ONCE):
-        piece = slice(at * TOKENS_AT_ONCE, (at + 1) * TOKENS_AT_ONCE)
-        key, value = key_ref[piece, :], value_ref[piece, :]
-        rate = rates[:, piece]
-        pre_gate = dot(gate, key, NT)
-        pre_up = dot(up, key, NT)
-        backed = dot(down_t, value, NT) * rate
-        sigmoid = jax.nn.sigmoid(pre_gate)
-        active = pre_gate * sigmoid
-        hidden = (active * pre_up * rate).astype(BF16)
-        to_up = (backed * active).astype(BF16)
-        slope = sigmoid * (1.0 + pre_gate * (1.0 - sigmoid))
-        to_gate = (backed * pre_up * slope).astype(BF16)
-        for which, (left, right) in enumerate(((to_gate, key), (to_up, key), (hidden, value))):
-            term = dot(left, right, NN)
-            if at == 0:
-                sums[which] = term
-            else:
-                sums[which] += term
-    flat[:DH, :] = sums[0]
-    flat[DH : 2 * DH, :] = sums[1]
-    flat[2 * DH :, :] = jnp.transpose(sums[2])
-    total = jnp.sum(rates, axis=1, keepdims=True)
+    key, value = key_ref[...], value_ref[...]
+    rate = rate_ref[block_at : block_at + 1, :]
+    pre_gate = dot(gate, key, NT)
+    pre_up = dot(up, key, NT)
+    backed = dot(down_t, value, NT) * rate
+    sigmoid = jax.nn.sigmoid(pre_gate)
+    active = pre_gate * sigmoid
+    hidden = (active * pre_up * rate).astype(BF16)
+    to_up = (backed * active).astype(BF16)
+    slope = sigmoid * (1.0 + pre_gate * (1.0 - sigmoid))
+    to_gate = (backed * pre_up * slope).astype(BF16)
+    flat[:DH, :] = dot(to_gate, key, NN)
+    flat[DH : 2 * DH, :] = dot(to_up, key, NN)
+    flat[2 * DH :, :] = jnp.transpose(dot(hidden, value, NN))
+    total = jnp.sum(rate, axis=1, keepdims=True)
     high = total.astype(BF16)
     low = (total - high.astype(F32)).astype(BF16)
-    extra = out_ref.shape[1] - rows
-    place = lax.broadcasted_iota(jnp.int32, (extra, DH), 0)
+    extra = out_ref.shape[1] - PARTS * rows
+    place = lax.broadcasted_iota(jnp.int32, (extra, LANES), 0)
     tail = jnp.where(place == 0, high.astype(F32), jnp.where(place == 1, low.astype(F32), 0.0))
     for at in range(out_ref.shape[0]):
-        piece = jnp.concatenate([flat[at * rows : (at + 1) * rows, :], tail], axis=0)
-        out_ref[at] = piece.astype(BF16)
+        shard = [
+            flat[at * rows : (at + 1) * rows, part * LANES : (part + 1) * LANES]
+            for part in range(PARTS)
+        ]
+        out_ref[at] = jnp.concatenate(shard + [tail], axis=0).astype(BF16)
 
 
 def gradients(block_at, key_rows, value_rows, step_rates, weights, shards, rows, padded):
@@ -88,7 +85,7 @@
     first = len(weights) == 3
     matrix = pl.BlockSpec((None, DH, DH), lambda h: (h, 0, 0))
     per_head = shards // heads
-    packed = pl.BlockSpec((per_head, padded, DH), lambda h: (h, 0, 0))
+    packed = pl.BlockSpec((per_head, padded, LANES), lambda h: (h, 0, 0))
     rowed = pl.BlockSpec((None, tokens, DH), lambda h: (block_at, 0, h))
     return pl.pallas_call(
         functools.partial(gradient_kernel, first, block_at, rows),
@@ -96,8 +93,8 @@
         in_specs=[rowed, rowed, pl.BlockSpec((None, step_rates.shape[1], tokens), lambda h: (h, 0, 0))]
         + ([matrix] * 3 if first else [packed]),
         out_specs=packed,
-        out_shape=jax.ShapeDtypeStruct((shards, padded, DH), BF16),
-        scratch_shapes=[pltpu.VMEM((3 * DH, DH), F32), pltpu.VMEM((3, DH, DH), F32)],
+        out_shape=jax.ShapeDtypeStruct((shards, padded, LANES), BF16),
+        scratch_shapes=[pltpu.VMEM((3 * DH, DH), F32)],
         cost_estimate=cost(heads * 12 * tokens * DH * DH, 8e6, heads * tokens * DH * 2),
         name="gradients",
     )(key_rows, value_rows, step_rates, *weights)
@@ -105,16 +102,25 @@
 
 def row_scale(matrix):
     return jnp.sqrt(jnp.mean(matrix * matrix, axis=-1, keepdims=True) + EPSILON)
+
+
+def shard_scale(shard, rows):
+    square = jnp.sum(shard * shard, axis=-1, keepdims=True)
+    total = sum(square[part * rows : (part + 1) * rows] for part in range(PARTS))
+    return jnp.sqrt(total / DH + EPSILON)
 
 
 def update_kernel(rows, parts_ref, old_ref, new_ref, copies_ref):
     total = parts_ref[0].astype(F32)
     for at in range(1, parts_ref.shape[0]):
         total += parts_ref[at].astype(F32)
-    rate = total[rows : rows + 1, :] + total[rows + 1 : rows + 2, :]
+    top = PARTS * rows
+    rate = total[top : top + 1, :] + total[top + 1 : top + 2, :]
     old = old_ref[...]
     updated = old + total / rate
-    new = updated * (row_scale(old) / row_scale(updated))
+    ratio = shard_scale(old, rows) / shard_scale(updated, rows)
+    rest = jnp.ones((old.shape[0] - top, 1), F32)
+    new = updated * jnp.concatenate([ratio] * PARTS + [rest], axis=0)
     new_ref[...] = new
     rounded = new.astype(BF16)
     for at in range(copies_ref.shape[0]):
@@ -126,13 +132,13 @@
     return pl.pallas_call(
         functools.partial(update_kernel, rows),
         out_shape=(
-            jax.ShapeDtypeStruct((padded, DH), F32),
-            jax.ShapeDtypeStruct((shards, padded, DH), BF16),
+            jax.ShapeDtypeStruct((padded, LANES), F32),
+            jax.ShapeDtypeStruct((shards, padded, LANES), BF16),
         ),
         in_specs=[pl.BlockSpec(memory_space=pltpu.VMEM)] * 2,
         out_specs=(pl.BlockSpec(memory_space=pltpu.VMEM),) * 2,
         compiler_params=LEAN,
-        cost_estimate=cost(2 * shards * padded * DH, 4e6),
+        cost_estimate=cost(2 * shards * padded * LANES, 4e6),
         name="update",
     )(parts, old)
 
@@ -246,7 +252,7 @@
         grid=(heads,),
         in_specs=[
             pl.BlockSpec((None, tokens, DH), lambda h: (block_at, 0, first + h)),
-            pl.BlockSpec((per_head, padded, DH), lambda h: (first + h, 0, 0)),
+            pl.BlockSpec((per_head, padded, LANES), lambda h: (first + h, 0, 0)),
             pl.BlockSpec((WINDOW, DH), lambda h: (0, first + h)),
             pl.BlockSpec((None, WINDOW, DH), lambda h: (block_at, 0, first + h)),
         ],
@@ -308,18 +314,6 @@
     )(side, *operands)
 
 
-def exchange_order(count):
-    side = round(count ** (1 / 3))
-    if side**3 != count:
-        return list(range(count))
-    order = []
-    for step in range(count):
-        a, b, c = step // (side * side), step // side % side, step % side
-        x, y, z = a, b, c
-        order.append((x * side + y) * side + z)
-    return order
-
-
 def shards(queries, key_rows, value_rows, step_rates, gate_init, up_init, down_init, out_weight):
     blocks, tokens, width = queries.shape
     heads = width // DH
@@ -329,7 +323,7 @@
     ring = [(i, (i + 1) % count) for i in range(count)]
     swap = [(0, 1), (1, 0)]
     rows = heads * 3 * DH // count
-    padded = -(-(rows + 2) // 8) * 8
+    padded = -(-(PARTS * rows + 2) // 8) * 8
 
     weights = (gate_init, up_init, down_init)
     near = [lax.ppermute(key_rows[0, tokens - WINDOW :, :], "tok", ring)]
@@ -341,14 +335,11 @@
     sent_weight = lax.dynamic_slice_in_dim(out_weight, (1 - side) * width, width, 1)
     other_weight = lax.ppermute(sent_weight, "head", swap)
 
-    order = exchange_order(count)
-    exchange = lambda x: lax.all_to_all(
-        x, "tok", split_axis=0, concat_axis=0, tiled=True, axis_index_groups=[order]
-    )
+    exchange = lambda x: lax.all_to_all(x, "tok", split_axis=0, concat_axis=0, tiled=True)
     flat = jnp.concatenate([gate_init, up_init, down_init], axis=1).reshape(heads * 3 * DH, DH)
-    flat = jnp.concatenate([flat, jnp.zeros((padded - rows, DH), F32)], axis=0)
-    shard = jnp.asarray([order.index(i) for i in range(count)], jnp.int32)[place]
-    held = lax.dynamic_slice_in_dim(flat, shard * rows, padded, 0)
+    held = lax.dynamic_slice_in_dim(flat, place * rows, rows, 0)
+    held = [held[:, part * LANES : (part + 1) * LANES] for part in range(PARTS)]
+    held = jnp.concatenate(held + [jnp.zeros((padded - PARTS * rows, LANES), F32)], axis=0)
 
     local = local_attention(queries, key_rows, value_rows)
     nears = []

time: 234 us -> 227 us (0.970)
  waiting for transfers between devices: 65.4 us -> 61.9 us
  blocking collectives: 65.2 us -> 61.7 us
    all_to_all x2, blocking collectives: 65.2 us -> 61.7 us  [shards(): lax.all_to_all(x, 'tok', split_axis=0, concat_axis=0, tiled=True)]
  transfers between devices with their start and end apart: 9 -> 9, of which waited for: 4 -> 4; matrix products, arithmetic and copies ran while one was open for 4% -> 4% of each run, Pallas kernels for 15% -> 16%
where the time goes in v4:
time: 227 us; the launch traced here: 226 us
  waiting for transfers between devices  61.9 us (27%)
  blocking collectives  61.7 us (27%)
  Pallas kernels  57.3 us (25%)
  starting transfers between devices  31.8 us (14%)
  local copies, waits for them, and re-layouts  11.7 us (5%)
    all_to_all x2, blocking collectives, shards(): lax.all_to_all(x, 'tok', split_axis=0, concat_axis=0, tiled=True)  61.7 us
    ppermute x3, waiting for transfers between devices, shards(): near.append(lax.ppermute(array[at // 2, tokens - WINDOW:, :], 'tok', ring))  23.4 us
    all_to_all x2, waiting for transfers between devices, shards(): lax.all_to_all(x, 'tok', split_axis=0, concat_axis=0, tiled=True)  22.8 us
    all_to_all x2, starting transfers between devices, shards(): lax.all_to_all(x, 'tok', split_axis=0, concat_axis=0, tiled=True)  19.8 us
    ppermute x1, waiting for transfers between devices, shards(): near = [lax.ppermute(key_rows[0, tokens - WINDOW:, :], 'tok', ring)]  15.6 us
    pallas_call x2, Pallas kernels, gradients(): pl.pallas_call(functools.partial(gradient_kernel, first, block_at, rows),...  14.5 us
    pallas_call x2, Pallas kernels, query_heads(): pl.pallas_call(functools.partial(query_kernel, rows), grid=(heads,), in_s...  11 us
    pallas_call x2, Pallas kernels, near_attention(): pl.pallas_call(functools.partial(near_kernel, block_at), grid_spec=pltpu....  11 us
  transfers between devices with their start and end apart: 9, of which 4 were waited for; matrix products, arithmetic and copies ran while one was open for 4% of the time, Pallas kernels for 16%

profile of v4, /device:TPU:1, one launch (start us, length us, event | category | flops | bytes accessed | tf_op | source)
XLA Modules:
  0.0 226.4 jit_solution(3808965200018316890)
XLA Ops:
  0.0 7.4 %gradients.2 = bf16[64,112,128]{2,1,0:T(8,128)(2,1)} custom-call(bf16[2,768,768]{2,1,0:T(8,128)(2,1)} %key_ref.5, bf16[2,768,768]{2,1,0:T(8,128)(2,1)} %value_ref.5, f32[2,2,768]{2,1,0:T(2,128)} %refs_2_.3, f32[2,384,384]{2,1,0:T(8,128)} %refs_3_.1, f32[2,384,384]{2,1,0:T(8,128)} %refs_4_.1, f32[2,384,384]{2,1,0:T(8,128)} %refs_5_.1), custom_call_target="tpu_custom_call" | custom-call | flops 2717908992 | bytes 8000000 | tf_op jit(solution)/shard_map/gradients/pallas_call | solution.py:90
  7.4 12.1 %all-to-all-start = ((bf16[64,112,128]{2,1,0:T(8,128)(2,1)}), bf16[64,112,128]{2,1,0:T(8,128)(2,1)S(1)}, u32[]{:S(2)}, u32[]{:S(2)}) async-start(bf16[64,112,128]{2,1,0:T(8,128)(2,1)} %gradients.2), calls=%async_computation | async-start | bytes 3670016 | tf_op jit(solution)/shard_map/all_to_all | solution.py:338
  19.6 1.9 pad_maximum_fusion
  21.6 22.8 %all-to-all-done.parts_ref = bf16[64,112,128]{2,1,0:T(8,128)(2,1)S(1)} async-done(((bf16[64,112,128]{2,1,0:T(8,128)(2,1)}), bf16[64,112,128]{2,1,0:T(8,128)(2,1)S(1)}, u32[]{:S(2)}, u32[]{:S(2)}) %all-to-all-start) | async-done | bytes 1835040 | tf_op jit(solution)/shard_map/all_to_all | solution.py:338
  45.0 30.5 %all_to_all.20.refs_3_.packed_ref = bf16[64,112,128]{2,1,0:T(8,128)(2,1)} all-to-all(bf16[64,112,128]{2,1,0:T(8,128)(2,1)S(1)} %get-tuple-element.12), channel_id=1, replica_groups=mesh['tok'=64,'head'=2] {'tok'}, dimensions={0} | all-to-all | bytes 3670016 | tf_op jit(solution)/shard_map/all_to_all | solution.py:338
  75.5 7.1 %gradients.3 = bf16[64,112,128]{2,1,0:T(8,128)(2,1)} custom-call(bf16[2,768,768]{2,1,0:T(8,128)(2,1)} %key_ref.5, bf16[2,768,768]{2,1,0:T(8,128)(2,1)} %value_ref.5, f32[2,2,768]{2,1,0:T(2,128)} %refs_2_.3, bf16[64,112,128]{2,1,0:T(8,128)(2,1)} %all_to_all.20.refs_3_.packed_ref), custom_call_target="tpu_custom_call" | custom-call | flops 2717908992 | bytes 8000000 | tf_op jit(solution)/shard_map/gradients/pallas_call | solution.py:90
  82.6 31.2 %all_to_all.21.parts_ref = bf16[64,112,128]{2,1,0:T(8,128)(2,1)S(1)} all-to-all(bf16[64,112,128]{2,1,0:T(8,128)(2,1)} %gradients.3), channel_id=1, replica_groups=mesh['tok'=64,'head'=2] {'tok'}, dimensions={0} | all-to-all | bytes 3670016 | tf_op jit(solution)/shard_map/all_to_all | solution.py:338
  113.9 1.8 update.3
  115.7 7.7 %all-to-all-start.3 = ((bf16[64,112,128]{2,1,0:T(8,128)(2,1)}), bf16[64,112,128]{2,1,0:T(8,128)(2,1)}, u32[]{:S(2)}, u32[]{:S(2)}) async-start(bf16[64,112,128]{2,1,0:T(8,128)(2,1)} %get-tuple-element.14), calls=%async_computation.3 | async-start | bytes 3670016 | tf_op jit(solution)/shard_map/all_to_all | solution.py:338
  123.4 1.9 slice_bitcast_fusion.1
  125.3 0.9 collective-permute-start.2
  126.3 2.4 %slice_bitcast_fusion = (bf16[384,768]{1,0:T(8,128)(2,1)}, bf16[384,768]{1,0:T(8,128)(2,1)}) fusion(bf16[2,768,768]{2,1,0:T(8,128)(2,1)} %value_ref.5), kind=kLoop, calls=%fused_computation.1 | loop fusion | bytes 2359296 | tf_op jit(solution)/shard_map/squeeze | solution.py:334
  128.7 1.2 collective-permute-start.3
  129.9 1.9 slice_bitcast_fusion.3
  132.7 1.2 collective-permute-start.1
  133.9 1.1 constant_dynamic-slice_fusion.1
  135.0 3.1 %collective-permute-start.5 = (bf16[768,768]{1,0:T(8,128)(2,1)}, bf16[768,768]{1,0:T(8,128)(2,1)S(1)}, u32[]{:S(2)}, u32[]{:S(2)}) collective-permute-start(bf16[768,768]{1,0:T(8,128)(2,1)} %constant_dynamic-slice_fusion.1), channel_id=1, source_target_pairs={{0,1},{1,0},{2,3},{3,2},{4,5},{5,4},{6,7},{7,6},{8,9},{9,8},{10,11... | collective-permute-start | bytes 3538952 | tf_op jit(solution)/shard_map/ppermute | solution.py:336
  138.0 8.4 %local_attention.1.local_ref = bf16[2,384,768]{2,1,0:T(8,128)(2,1)} custom-call(bf16[2,768,768]{2,1,0:T(8,128)(2,1)} %query_ref.9, bf16[2,768,768]{2,1,0:T(8,128)(2,1)} %key_ref.5, bf16[2,768,768]{2,1,0:T(8,128)(2,1)} %value_ref.5), custom_call_target="tpu_custom_call" | custom-call | flops 1207959552 | bytes 10000000 | tf_op jit(solution)/shard_map/local_attention/pallas_call | solution.py:176
  146.4 15.6 %collective-permute-done.2.refs_2_.refs_0_ = bf16[384,768]{1,0:T(8,128)(2,1)S(1)} collective-permute-done((bf16[384,768]{1,0:T(8,128)(2,1)}, bf16[384,768]{1,0:T(8,128)(2,1)S(1)}, u32[]{:S(2)}, u32[]{:S(2)}) %collective-permute-start.2) | collective-permute-done | bytes 589856 | tf_op jit(solution)/shard_map/ppermute | solution.py:329
  162.0 12.6 %collective-permute-done.3.refs_3_.refs_1_ = bf16[384,768]{1,0:T(8,128)(2,1)S(1)} collective-permute-done((bf16[384,768]{1,0:T(8,128)(2,1)}, bf16[384,768]{1,0:T(8,128)(2,1)S(1)}, u32[]{:S(2)}, u32[]{:S(2)}) %collective-permute-start.3) | collective-permute-done | bytes 589856 | tf_op jit(solution)/shard_map/ppermute | solution.py:334
  175.5 5.2 %near_attention.3.near_ref = bf16[384,768]{1,0:T(8,128)(2,1)} custom-call(s32[1]{0:T(128)} %bitcast.2.place_ref, bf16[2,768,768]{2,1,0:T(8,128)(2,1)} %query_ref.9, bf16[2,768,768]{2,1,0:T(8,128)(2,1)} %key_ref.5, bf16[2,768,768]{2,1,0:T(8,128)(2,1)} %value_ref.5, bf16[384,768]{1,0:T(8,128)(2,1)} %copy-done.6, bf16[384,768]{1,0:T(8,128)(2,1)} %copy-done.7), custom_call_target="tpu_custom_call" | custom-call | flops 603979776 | bytes 10000000 | tf_op jit(solution)/shard_map/near_attention/pallas_call | solution.py:216
  180.7 5.5 %query_heads.3.refs_0_ = bf16[768,768]{1,0:T(8,128)(2,1)} custom-call(bf16[2,768,768]{2,1,0:T(8,128)(2,1)} %query_ref.9, bf16[64,112,128]{2,1,0:T(8,128)(2,1)} %all_to_all.20.refs_3_.packed_ref, bf16[384,768]{1,0:T(8,128)(2,1)} %near_attention.3.near_ref, bf16[2,384,768]{2,1,0:T(8,128)(2,1)} %local_attention.1.local_ref), custom_call_target="tpu_custom_call" | custom-call | flops 1358954496 | bytes 7000000 | tf_op jit(solution)/shard_map/query_heads/pallas_call | solution.py:250
  186.2 3.0 %collective-permute-start.6 = (bf16[768,768]{1,0:T(8,128)(2,1)}, bf16[768,768]{1,0:T(8,128)(2,1)S(1)}, u32[]{:S(2)}, u32[]{:S(2)}) collective-permute-start(bf16[768,768]{1,0:T(8,128)(2,1)} %query_heads.3.refs_0_), channel_id=1, source_target_pairs={{0,1},{1,0},{2,3},{3,2},{4,5},{5,4},{6,7},{7,6},{8,9},{9,8},{10,11... | collective-permute-start | bytes 3538952 | tf_op jit(solution)/shard_map/ppermute | solution.py:366
  189.2 10.8 %collective-permute-done.1.refs_1_ = bf16[384,768]{1,0:T(8,128)(2,1)} collective-permute-done((bf16[384,768]{1,0:T(8,128)(2,1)}, bf16[384,768]{1,0:T(8,128)(2,1)}, u32[]{:S(2)}, u32[]{:S(2)}) %collective-permute-start.1) | collective-permute-done | bytes 589856 | tf_op jit(solution)/shard_map/ppermute | solution.py:334
  200.0 5.7 %near_attention.2.near_ref = bf16[384,768]{1,0:T(8,128)(2,1)} custom-call(s32[1]{0:T(128)} %bitcast.2.place_ref, bf16[2,768,768]{2,1,0:T(8,128)(2,1)} %query_ref.9, bf16[2,768,768]{2,1,0:T(8,128)(2,1)} %key_ref.5, bf16[2,768,768]{2,1,0:T(8,128)(2,1)} %value_ref.5, bf16[384,768]{1,0:T(8,128)(2,1)} %collective-permute-done.refs_0_, ...), custom_call_target="tpu_custom_call" | custom-call | flops 603979776 | bytes 10000000 | tf_op jit(solution)/shard_map/near_attention/pallas_call | solution.py:216
  205.7 5.5 %query_heads.2.refs_0_ = bf16[768,768]{1,0:T(8,128)(2,1)} custom-call(bf16[2,768,768]{2,1,0:T(8,128)(2,1)} %query_ref.9, bf16[64,112,128]{2,1,0:T(8,128)(2,1)} %all-to-all-done.3.packed_ref, bf16[384,768]{1,0:T(8,128)(2,1)} %near_attention.2.near_ref, bf16[2,384,768]{2,1,0:T(8,128)(2,1)} %local_attention.1.local_ref), custom_call_target="tpu_custom_call" | custom-call | flops 1358954496 | bytes 7000000 | tf_op jit(solution)/shard_map/query_heads/pallas_call | solution.py:250
  211.3 1.7 collective-permute-start.4
  213.0 1.0 copy-done.3
  214.0 1.0 copy-done.8
  215.0 5.6 %project.2.refs_4_ = bf16[2,768,768]{2,1,0:T(8,128)(2,1)} custom-call(s32[1]{0:T(128)} %bitcast.side_ref, bf16[768,768]{1,0:T(8,128)(2,1)} %query_heads.3.refs_0_, bf16[768,1536]{1,0:T(8,128)(2,1)} %refs_1_.7, bf16[768,768]{1,0:T(8,128)(2,1)} %copy-done.8, bf16[768,768]{1,0:T(8,128)(2,1)} %copy-done.3), custom_call_target="tpu_custom_call" | custom-call | flops 1811939328 | bytes 6000000 | tf_op jit(solution)/shard_map/project/pallas_call | solution.py:304
  220.7 1.3 copy-done.4
  221.9 4.4 %project.3 = bf16[2,768,768]{2,1,0:T(8,128)(2,1)} custom-call(s32[1]{0:T(128)} %bitcast.side_ref, bf16[768,768]{1,0:T(8,128)(2,1)S(1)} %copy-done.2, bf16[768,1536]{1,0:T(8,128)(2,1)S(1)} %copy-done.1, bf16[768,768]{1,0:T(8,128)(2,1)} %collective-permute-done.4.refs_2_, bf16[768,768]{1,0:T(8,128)(2,1)S(1)} %copy-done.4, ...), custom_call_target="tpu_custom_call", output_to_operand_aliasing={{}: (5, {})} | custom-call | flops 1811939328 | bytes 6000000 | tf_op jit(solution)/shard_map/project/pallas_call | solution.py:304
  (26 shorter events, 2.6 us)
Async XLA Ops:
  7.4 12.2 %copy-start.5 = (f32[2,384,384]{2,1,0:T(8,128)S(1)}, f32[2,384,384]{2,1,0:T(8,128)}, u32[]{:S(2)}) copy-start(f32[2,384,384]{2,1,0:T(8,128)} %refs_3_.1) | copy-start | bytes 3538948
  7.4 37.1 %all-to-all-start = ((bf16[64,112,128]{2,1,0:T(8,128)(2,1)}), bf16[64,112,128]{2,1,0:T(8,128)(2,1)S(1)}, u32[]{:S(2)}, u32[]{:S(2)}) async-start(bf16[64,112,128]{2,1,0:T(8,128)(2,1)} %gradients.2), calls=%async_computation | async-start | bytes 3670016 | tf_op jit(solution)/shard_map/all_to_all | solution.py:338
  115.7 90.1 %all-to-all-start.3 = ((bf16[64,112,128]{2,1,0:T(8,128)(2,1)}), bf16[64,112,128]{2,1,0:T(8,128)(2,1)}, u32[]{:S(2)}, u32[]{:S(2)}) async-start(bf16[64,112,128]{2,1,0:T(8,128)(2,1)} %get-tuple-element.14), calls=%async_computation.3 | async-start | bytes 3670016 | tf_op jit(solution)/shard_map/all_to_all | solution.py:338
  125.3 8.5 %copy-start = (bf16[768,1536]{1,0:T(8,128)(2,1)S(1)}, bf16[768,1536]{1,0:T(8,128)(2,1)}, u32[]{:S(2)}) copy-start(bf16[768,1536]{1,0:T(8,128)(2,1)} %refs_1_.7) | copy-start | bytes 7077892
  125.3 36.7 %collective-permute-start.2 = (bf16[384,768]{1,0:T(8,128)(2,1)}, bf16[384,768]{1,0:T(8,128)(2,1)S(1)}, u32[]{:S(2)}, u32[]{:S(2)}) collective-permute-start(bf16[384,768]{1,0:T(8,128)(2,1)} %slice_bitcast_fusion.1), channel_id=1, source_target_pairs={{0,2},{2,4},{4,6},{6,8},{8,10},{10,12},{12,14},{14,16},{16,18},{18... | collective-permute-start | bytes 1769480 | tf_op jit(solution)/shard_map/ppermute | solution.py:329
  128.7 45.9 %collective-permute-start.3 = (bf16[384,768]{1,0:T(8,128)(2,1)}, bf16[384,768]{1,0:T(8,128)(2,1)S(1)}, u32[]{:S(2)}, u32[]{:S(2)}) collective-permute-start(bf16[384,768]{1,0:T(8,128)(2,1)} %get-tuple-element.20), channel_id=1, source_target_pairs={{0,2},{2,4},{4,6},{6,8},{8,10},{10,12},{12,14},{14,16},{16,18},{18... | collective-permute-start | bytes 1769480 | tf_op jit(solution)/shard_map/ppermute | solution.py:334
  131.8 57.4 %collective-permute-start = (bf16[384,768]{1,0:T(8,128)(2,1)}, bf16[384,768]{1,0:T(8,128)(2,1)}, u32[]{:S(2)}, u32[]{:S(2)}) collective-permute-start(bf16[384,768]{1,0:T(8,128)(2,1)} %slice_bitcast_fusion.3), channel_id=1, source_target_pairs={{0,2},{2,4},{4,6},{6,8},{8,10},{10,12},{12,14},{14,16},{16,18},{18... | collective-permute-start | bytes 1769480 | tf_op jit(solution)/shard_map/ppermute | solution.py:334
  132.7 67.3 %collective-permute-start.1 = (bf16[384,768]{1,0:T(8,128)(2,1)}, bf16[384,768]{1,0:T(8,128)(2,1)}, u32[]{:S(2)}, u32[]{:S(2)}) collective-permute-start(bf16[384,768]{1,0:T(8,128)(2,1)} %get-tuple-element.21), channel_id=1, source_target_pairs={{0,2},{2,4},{4,6},{6,8},{8,10},{10,12},{12,14},{14,16},{16,18},{18... | collective-permute-start | bytes 1769480 | tf_op jit(solution)/shard_map/ppermute | solution.py:334
  135.0 78.0 %collective-permute-start.5 = (bf16[768,768]{1,0:T(8,128)(2,1)}, bf16[768,768]{1,0:T(8,128)(2,1)S(1)}, u32[]{:S(2)}, u32[]{:S(2)}) collective-permute-start(bf16[768,768]{1,0:T(8,128)(2,1)} %constant_dynamic-slice_fusion.1), channel_id=1, source_target_pairs={{0,1},{1,0},{2,3},{3,2},{4,5},{5,4},{6,7},{7,6},{8,9},{9,8},{10,11... | collective-permute-start | bytes 3538952 | tf_op jit(solution)/shard_map/ppermute | solution.py:336
  162.0 12.6 %copy-start.6 = (bf16[384,768]{1,0:T(8,128)(2,1)}, bf16[384,768]{1,0:T(8,128)(2,1)S(1)}, u32[]{:S(2)}) copy-start(bf16[384,768]{1,0:T(8,128)(2,1)S(1)} %collective-permute-done.2.refs_2_.refs_0_) | copy-start | bytes 1769476
  174.6 0.8 copy-start.7
  186.2 26.8 %collective-permute-start.6 = (bf16[768,768]{1,0:T(8,128)(2,1)}, bf16[768,768]{1,0:T(8,128)(2,1)S(1)}, u32[]{:S(2)}, u32[]{:S(2)}) collective-permute-start(bf16[768,768]{1,0:T(8,128)(2,1)} %query_heads.3.refs_0_), channel_id=1, source_target_pairs={{0,1},{1,0},{2,3},{3,2},{4,5},{5,4},{6,7},{7,6},{8,9},{9,8},{10,11... | collective-permute-start | bytes 3538952 | tf_op jit(solution)/shard_map/ppermute | solution.py:366
  211.3 9.4 %collective-permute-start.4 = (bf16[768,768]{1,0:T(8,128)(2,1)}, bf16[768,768]{1,0:T(8,128)(2,1)}, u32[]{:S(2)}, u32[]{:S(2)}) collective-permute-start(bf16[768,768]{1,0:T(8,128)(2,1)} %query_heads.2.refs_0_), channel_id=1, source_target_pairs={{0,1},{1,0},{2,3},{3,2},{4,5},{5,4},{6,7},{7,6},{8,9},{9,8},{10,11... | collective-permute-start | bytes 3538952 | tf_op jit(solution)/shard_map/ppermute | solution.py:371
  213.0 1.0 copy-start.3
  214.0 1.0 copy-start.8
  215.0 5.6 %copy-start.1 = (bf16[768,1536]{1,0:T(8,128)(2,1)S(1)}, bf16[768,1536]{1,0:T(8,128)(2,1)}, u32[]{:S(2)}) copy-start(bf16[768,1536]{1,0:T(8,128)(2,1)} %refs_1_.7) | copy-start | bytes 7077892
  215.0 5.6 %copy-start.2 = (bf16[768,768]{1,0:T(8,128)(2,1)S(1)}, bf16[768,768]{1,0:T(8,128)(2,1)}, u32[]{:S(2)}) copy-start(bf16[768,768]{1,0:T(8,128)(2,1)} %query_heads.2.refs_0_) | copy-start | bytes 3538948
  220.7 1.3 copy-start.4

commit v5 on v4

--- a/solution.py
+++ b/solution.py
@@ -16,6 +16,7 @@
 F32 = jnp.float32
 LANES = 128
 PARTS = DH // LANES
+MID = pltpu.CompilerParams(vmem_limit_bytes=48 * 2**20)
 LEAN = pltpu.CompilerParams(vmem_limit_bytes=36 * 2**20)
 QUERY_TILE = 128
 
@@ -39,6 +40,10 @@
         for part in range(PARTS):
             columns = slice(part * LANES, (part + 1) * LANES)
             flat[at * rows : (at + 1) * rows, columns] = shard[part * rows : (part + 1) * rows, :]
+
+
+def in_hbm(array):
+    return pltpu.with_memory_space_constraint(array, pltpu.HBM)
 
 
 def gradient_kernel(first, block_at, rows, *refs):
@@ -93,11 +98,12 @@
         in_specs=[rowed, rowed, pl.BlockSpec((None, step_rates.shape[1], tokens), lambda h: (h, 0, 0))]
         + ([matrix] * 3 if first else [packed]),
         out_specs=packed,
-        out_shape=jax.ShapeDtypeStruct((shards, padded, LANES), BF16),
+        out_shape=pltpu.HBM((shards, padded, LANES), BF16),
+        compiler_params=None if first else MID,
         scratch_shapes=[pltpu.VMEM((3 * DH, DH), F32)],
         cost_estimate=cost(heads * 12 * tokens * DH * DH, 8e6, heads * tokens * DH * 2),
         name="gradients",
-    )(key_rows, value_rows, step_rates, *weights)
+    )(in_hbm(key_rows), in_hbm(value_rows), in_hbm(step_rates), *weights)
 
 
 def row_scale(matrix):
@@ -243,26 +249,27 @@
         out_ref[piece, :] = (fast + attended).astype(BF16)
 
 
-def query_heads(block_at, first, heads, queries, packed, near, local, rows, params):
+def query_heads(block_at, queries, packed, near, local, rows, params, kept):
     _, tokens, width = queries.shape
     shards, padded, _ = packed.shape
-    per_head = shards * DH // width
+    heads = width // DH
+    per_head = shards // heads
     return pl.pallas_call(
         functools.partial(query_kernel, rows),
         grid=(heads,),
         in_specs=[
-            pl.BlockSpec((None, tokens, DH), lambda h: (block_at, 0, first + h)),
-            pl.BlockSpec((per_head, padded, LANES), lambda h: (first + h, 0, 0)),
-            pl.BlockSpec((WINDOW, DH), lambda h: (0, first + h)),
-            pl.BlockSpec((None, WINDOW, DH), lambda h: (block_at, 0, first + h)),
+            pl.BlockSpec((None, tokens, DH), lambda h: (block_at, 0, h)),
+            pl.BlockSpec((per_head, padded, LANES), lambda h: (h, 0, 0)),
+            pl.BlockSpec((WINDOW, DH), lambda h: (0, h)),
+            pl.BlockSpec((None, WINDOW, DH), lambda h: (block_at, 0, h)),
         ],
         out_specs=pl.BlockSpec((tokens, DH), lambda h: (0, h)),
-        out_shape=jax.ShapeDtypeStruct((tokens, heads * DH), BF16),
+        out_shape=kept((tokens, heads * DH), BF16),
         scratch_shapes=[pltpu.VMEM((3 * DH, DH), F32)],
         compiler_params=params,
         cost_estimate=cost(heads * 6 * tokens * DH * DH, heads * 3.5e6, heads * tokens * DH),
         name="query_heads",
-    )(queries, packed, near, local)
+    )(in_hbm(queries), packed, in_hbm(near), in_hbm(local))
 
 
 def project_kernel(terms, has_sum, side_ref, *refs):
@@ -333,7 +340,7 @@
         if at:
             near.append(lax.ppermute(array[at // 2, tokens - WINDOW :, :], "tok", ring))
     sent_weight = lax.dynamic_slice_in_dim(out_weight, (1 - side) * width, width, 1)
-    other_weight = lax.ppermute(sent_weight, "head", swap)
+    other_weight = in_hbm(lax.ppermute(sent_weight, "head", swap))
 
     exchange = lambda x: lax.all_to_all(x, "tok", split_axis=0, concat_axis=0, tiled=True)
     flat = jnp.concatenate([gate_init, up_init, down_init], axis=1).reshape(heads * 3 * DH, DH)
@@ -361,13 +368,15 @@
                 block_at + 1, key_rows, value_rows, step_rates, (packed,), count, rows, padded
             )
             own = query_heads(
-                block_at, 0, heads, queries, packed, near_now, local, rows, None
+                block_at, queries, packed, near_now, local, rows, None, jax.ShapeDtypeStruct
             )
             other = lax.ppermute(own, "head", swap)
             terms = [(own, out_weight, 0, True), (other, other_weight, 0, False)]
             result = project(side_ref, terms, tokens, None, result, block_at, blocks)
             continue
-        own = query_heads(block_at, 0, heads, queries, packed, near_now, local, rows, None)
+        own = query_heads(
+            block_at, queries, packed, near_now, local, rows, MID, pltpu.VMEM
+        )
         other = lax.ppermute(own, "head", swap)
         terms = [(own, out_weight, 0, True), (other, other_weight, 0, False)]
         result = project(side_ref, terms, tokens, None, result, block_at, blocks, LEAN)

time: 227 us -> 226 us (level)
  no operation moved by 1% of the time
where the time goes in v5:
time: 226 us; the launch traced here: 225 us
  waiting for transfers between devices  61.9 us (27%)
  blocking collectives  61.6 us (27%)
  Pallas kernels  57.4 us (25%)
  starting transfers between devices  31.9 us (14%)
  local copies, waits for them, and re-layouts  10.4 us (5%)
    all_to_all x2, blocking collectives, shards(): lax.all_to_all(x, 'tok', split_axis=0, concat_axis=0, tiled=True)  61.6 us
    ppermute x3, waiting for transfers between devices, shards(): near.append(lax.ppermute(array[at // 2, tokens - WINDOW:, :], 'tok', ring))  23.4 us
    all_to_all x2, waiting for transfers between devices, shards(): lax.all_to_all(x, 'tok', split_axis=0, concat_axis=0, tiled=True)  22.8 us
    all_to_all x2, starting transfers between devices, shards(): lax.all_to_all(x, 'tok', split_axis=0, concat_axis=0, tiled=True)  19.8 us
    ppermute x1, waiting for transfers between devices, shards(): near = [lax.ppermute(key_rows[0, tokens - WINDOW:, :], 'tok', ring)]  15.6 us
    pallas_call x2, Pallas kernels, gradients(): pl.pallas_call(functools.partial(gradient_kernel, first, block_at, rows),...  14.9 us
    pallas_call x2, Pallas kernels, near_attention(): pl.pallas_call(functools.partial(near_kernel, block_at), grid_spec=pltpu....  11 us
    pallas_call x2, Pallas kernels, project(): pl.pallas_call(functools.partial(project_kernel, len(terms), summed is no...  10.5 us
  transfers between devices with their start and end apart: 9, of which 4 were waited for; matrix products, arithmetic and copies ran while one was open for 4% of the time, Pallas kernels for 16%

profile of v5, /device:TPU:1, one launch (start us, length us, event | category | flops | bytes accessed | tf_op | source)
XLA Modules:
  0.0 225.1 jit_solution(13385494270683842419)
XLA Ops:
  0.0 7.4 %gradients.2 = bf16[64,112,128]{2,1,0:T(8,128)(2,1)} custom-call(bf16[2,768,768]{2,1,0:T(8,128)(2,1)} %key_ref.5, bf16[2,768,768]{2,1,0:T(8,128)(2,1)} %value_ref.5, f32[2,2,768]{2,1,0:T(2,128)} %refs_2_.3, f32[2,384,384]{2,1,0:T(8,128)} %refs_3_.1, f32[2,384,384]{2,1,0:T(8,128)} %refs_4_.1, f32[2,384,384]{2,1,0:T(8,128)} %refs_5_.1), custom_call_target="tpu_custom_call" | custom-call | flops 2717908992 | bytes 8000000 | tf_op jit(solution)/shard_map/gradients/pallas_call | solution.py:95
  7.4 12.1 %all-to-all-start = ((bf16[64,112,128]{2,1,0:T(8,128)(2,1)}), bf16[64,112,128]{2,1,0:T(8,128)(2,1)S(1)}, u32[]{:S(2)}, u32[]{:S(2)}) async-start(bf16[64,112,128]{2,1,0:T(8,128)(2,1)} %gradients.2), calls=%async_computation | async-start | bytes 3670016 | tf_op jit(solution)/shard_map/all_to_all | solution.py:345
  19.6 1.9 pad_maximum_fusion
  21.6 22.8 %all-to-all-done.parts_ref = bf16[64,112,128]{2,1,0:T(8,128)(2,1)S(1)} async-done(((bf16[64,112,128]{2,1,0:T(8,128)(2,1)}), bf16[64,112,128]{2,1,0:T(8,128)(2,1)S(1)}, u32[]{:S(2)}, u32[]{:S(2)}) %all-to-all-start) | async-done | bytes 1835040 | tf_op jit(solution)/shard_map/all_to_all | solution.py:345
  45.0 30.4 %all_to_all.20.refs_3_.packed_ref = bf16[64,112,128]{2,1,0:T(8,128)(2,1)S(1)} all-to-all(bf16[64,112,128]{2,1,0:T(8,128)(2,1)S(1)} %get-tuple-element.12), channel_id=1, replica_groups=mesh['tok'=64,'head'=2] {'tok'}, dimensions={0} | all-to-all | bytes 3670016 | tf_op jit(solution)/shard_map/all_to_all | solution.py:345
  75.4 7.5 %gradients.3 = bf16[64,112,128]{2,1,0:T(8,128)(2,1)} custom-call(bf16[2,768,768]{2,1,0:T(8,128)(2,1)} %key_ref.5, bf16[2,768,768]{2,1,0:T(8,128)(2,1)} %value_ref.5, f32[2,2,768]{2,1,0:T(2,128)} %refs_2_.3, bf16[64,112,128]{2,1,0:T(8,128)(2,1)S(1)} %all_to_all.20.refs_3_.packed_ref), custom_call_target="tpu_custom_call" | custom-call | flops 2717908992 | bytes 8000000 | tf_op jit(solution)/shard_map/gradients/pallas_call | solution.py:95
  82.9 31.2 %all_to_all.21.parts_ref = bf16[64,112,128]{2,1,0:T(8,128)(2,1)S(1)} all-to-all(bf16[64,112,128]{2,1,0:T(8,128)(2,1)} %gradients.3), channel_id=1, replica_groups=mesh['tok'=64,'head'=2] {'tok'}, dimensions={0} | all-to-all | bytes 3670016 | tf_op jit(solution)/shard_map/all_to_all | solution.py:345
  114.1 1.8 update.3
  115.9 7.7 %all-to-all-start.3 = ((bf16[64,112,128]{2,1,0:T(8,128)(2,1)}), bf16[64,112,128]{2,1,0:T(8,128)(2,1)}, u32[]{:S(2)}, u32[]{:S(2)}) async-start(bf16[64,112,128]{2,1,0:T(8,128)(2,1)} %get-tuple-element.14), calls=%async_computation.3 | async-start | bytes 3670016 | tf_op jit(solution)/shard_map/all_to_all | solution.py:345
  123.7 1.9 slice_bitcast_fusion.1
  125.6 0.9 collective-permute-start.2
  126.5 2.4 %slice_bitcast_fusion = (bf16[384,768]{1,0:T(8,128)(2,1)}, bf16[384,768]{1,0:T(8,128)(2,1)}) fusion(bf16[2,768,768]{2,1,0:T(8,128)(2,1)} %value_ref.5), kind=kLoop, calls=%fused_computation.1 | loop fusion | bytes 2359296 | tf_op jit(solution)/shard_map/squeeze | solution.py:341
  128.9 1.2 collective-permute-start.3
  130.1 1.9 slice_bitcast_fusion.3
  132.0 0.9 collective-permute-start
  132.9 1.2 collective-permute-start.1
  134.1 1.1 constant_dynamic-slice_fusion.1
  135.2 3.1 %collective-permute-start.5 = (bf16[768,768]{1,0:T(8,128)(2,1)}, bf16[768,768]{1,0:T(8,128)(2,1)S(1)}, u32[]{:S(2)}, u32[]{:S(2)}) collective-permute-start(bf16[768,768]{1,0:T(8,128)(2,1)} %constant_dynamic-slice_fusion.1), channel_id=1, source_target_pairs={{0,1},{1,0},{2,3},{3,2},{4,5},{5,4},{6,7},{7,6},{8,9},{9,8},{10,11... | collective-permute-start | bytes 3538952 | tf_op jit(solution)/shard_map/ppermute | solution.py:343
  138.3 8.4 %local_attention.1.local_ref = bf16[2,384,768]{2,1,0:T(8,128)(2,1)} custom-call(bf16[2,768,768]{2,1,0:T(8,128)(2,1)} %query_ref.9, bf16[2,768,768]{2,1,0:T(8,128)(2,1)} %key_ref.5, bf16[2,768,768]{2,1,0:T(8,128)(2,1)} %value_ref.5), custom_call_target="tpu_custom_call" | custom-call | flops 1207959552 | bytes 10000000 | tf_op jit(solution)/shard_map/local_attention/pallas_call | solution.py:182
  146.7 15.6 %collective-permute-done.2.refs_2_.refs_0_ = bf16[384,768]{1,0:T(8,128)(2,1)S(1)} collective-permute-done((bf16[384,768]{1,0:T(8,128)(2,1)}, bf16[384,768]{1,0:T(8,128)(2,1)S(1)}, u32[]{:S(2)}, u32[]{:S(2)}) %collective-permute-start.2) | collective-permute-done | bytes 589856 | tf_op jit(solution)/shard_map/ppermute | solution.py:336
  162.3 12.6 %collective-permute-done.3.refs_3_.refs_1_ = bf16[384,768]{1,0:T(8,128)(2,1)S(1)} collective-permute-done((bf16[384,768]{1,0:T(8,128)(2,1)}, bf16[384,768]{1,0:T(8,128)(2,1)S(1)}, u32[]{:S(2)}, u32[]{:S(2)}) %collective-permute-start.3) | collective-permute-done | bytes 589856 | tf_op jit(solution)/shard_map/ppermute | solution.py:341
  175.7 5.2 %near_attention.3.near_ref = bf16[384,768]{1,0:T(8,128)(2,1)} custom-call(s32[1]{0:T(128)} %bitcast.2.place_ref, bf16[2,768,768]{2,1,0:T(8,128)(2,1)} %query_ref.9, bf16[2,768,768]{2,1,0:T(8,128)(2,1)} %key_ref.5, bf16[2,768,768]{2,1,0:T(8,128)(2,1)} %value_ref.5, bf16[384,768]{1,0:T(8,128)(2,1)} %copy-done.5, bf16[384,768]{1,0:T(8,128)(2,1)} %copy-done.6), custom_call_target="tpu_custom_call" | custom-call | flops 603979776 | bytes 10000000 | tf_op jit(solution)/shard_map/near_attention/pallas_call | solution.py:222
  181.0 5.5 %query_heads.3.refs_0_ = bf16[768,768]{1,0:T(8,128)(2,1)} custom-call(bf16[2,768,768]{2,1,0:T(8,128)(2,1)} %query_ref.9, bf16[64,112,128]{2,1,0:T(8,128)(2,1)} %copy-done.2, bf16[384,768]{1,0:T(8,128)(2,1)} %near_attention.3.near_ref, bf16[2,384,768]{2,1,0:T(8,128)(2,1)} %local_attention.1.local_ref), custom_call_target="tpu_custom_call" | custom-call | flops 1358954496 | bytes 7000000 | tf_op jit(solution)/shard_map/query_heads/pallas_call | solution.py:257
  186.5 3.0 %collective-permute-start.6 = (bf16[768,768]{1,0:T(8,128)(2,1)}, bf16[768,768]{1,0:T(8,128)(2,1)S(1)}, u32[]{:S(2)}, u32[]{:S(2)}) collective-permute-start(bf16[768,768]{1,0:T(8,128)(2,1)} %query_heads.3.refs_0_), channel_id=1, source_target_pairs={{0,1},{1,0},{2,3},{3,2},{4,5},{5,4},{6,7},{7,6},{8,9},{9,8},{10,11... | collective-permute-start | bytes 3538952 | tf_op jit(solution)/shard_map/ppermute | solution.py:373
  189.5 10.8 %collective-permute-done.1.refs_1_ = bf16[384,768]{1,0:T(8,128)(2,1)} collective-permute-done((bf16[384,768]{1,0:T(8,128)(2,1)}, bf16[384,768]{1,0:T(8,128)(2,1)}, u32[]{:S(2)}, u32[]{:S(2)}) %collective-permute-start.1) | collective-permute-done | bytes 589856 | tf_op jit(solution)/shard_map/ppermute | solution.py:341
  200.3 5.7 %near_attention.2.near_ref = bf16[384,768]{1,0:T(8,128)(2,1)} custom-call(s32[1]{0:T(128)} %bitcast.2.place_ref, bf16[2,768,768]{2,1,0:T(8,128)(2,1)} %query_ref.9, bf16[2,768,768]{2,1,0:T(8,128)(2,1)} %key_ref.5, bf16[2,768,768]{2,1,0:T(8,128)(2,1)} %value_ref.5, bf16[384,768]{1,0:T(8,128)(2,1)} %collective-permute-done.refs_0_, ...), custom_call_target="tpu_custom_call" | custom-call | flops 603979776 | bytes 10000000 | tf_op jit(solution)/shard_map/near_attention/pallas_call | solution.py:222
  206.0 4.8 %query_heads.2.refs_0_ = bf16[768,768]{1,0:T(8,128)(2,1)S(1)} custom-call(bf16[2,768,768]{2,1,0:T(8,128)(2,1)} %query_ref.9, bf16[64,112,128]{2,1,0:T(8,128)(2,1)} %all-to-all-done.3.packed_ref, bf16[384,768]{1,0:T(8,128)(2,1)} %near_attention.2.near_ref, bf16[2,384,768]{2,1,0:T(8,128)(2,1)} %local_attention.1.local_ref), custom_call_target="tpu_custom_call" | custom-call | flops 1358954496 | bytes 7000000 | tf_op jit(solution)/shard_map/query_heads/pallas_call | solution.py:257
  210.8 1.8 collective-permute-start.4
  212.6 1.0 copy-done.4
  213.6 1.0 copy-done.7
  214.7 5.6 %project.2.refs_4_ = bf16[2,768,768]{2,1,0:T(8,128)(2,1)} custom-call(s32[1]{0:T(128)} %bitcast.side_ref, bf16[768,768]{1,0:T(8,128)(2,1)} %query_heads.3.refs_0_, bf16[768,1536]{1,0:T(8,128)(2,1)} %refs_1_.7, bf16[768,768]{1,0:T(8,128)(2,1)} %copy-done.7, bf16[768,768]{1,0:T(8,128)(2,1)} %copy-done.4), custom_call_target="tpu_custom_call" | custom-call | flops 1811939328 | bytes 6000000 | tf_op jit(solution)/shard_map/project/pallas_call | solution.py:311
  220.3 4.9 %project.3 = bf16[2,768,768]{2,1,0:T(8,128)(2,1)} custom-call(s32[1]{0:T(128)} %bitcast.side_ref, bf16[768,768]{1,0:T(8,128)(2,1)S(1)} %query_heads.2.refs_0_, bf16[768,1536]{1,0:T(8,128)(2,1)S(1)} %copy-done.1, bf16[768,768]{1,0:T(8,128)(2,1)} %collective-permute-done.4.refs_2_, bf16[768,768]{1,0:T(8,128)(2,1)} %copy-done.4, ...), custom_call_target="tpu_custom_call", output_to_operand_aliasing={{}: (5, {})} | custom-call | flops 1811939328 | bytes 6000000 | tf_op jit(solution)/shard_map/project/pallas_call | solution.py:311
  (24 shorter events, 1.7 us)
Async XLA Ops:
  7.4 12.2 %copy-start.3 = (f32[2,384,384]{2,1,0:T(8,128)S(1)}, f32[2,384,384]{2,1,0:T(8,128)}, u32[]{:S(2)}) copy-start(f32[2,384,384]{2,1,0:T(8,128)} %refs_3_.1) | copy-start | bytes 3538948
  7.4 37.1 %all-to-all-start = ((bf16[64,112,128]{2,1,0:T(8,128)(2,1)}), bf16[64,112,128]{2,1,0:T(8,128)(2,1)S(1)}, u32[]{:S(2)}, u32[]{:S(2)}) async-start(bf16[64,112,128]{2,1,0:T(8,128)(2,1)} %gradients.2), calls=%async_computation | async-start | bytes 3670016 | tf_op jit(solution)/shard_map/all_to_all | solution.py:345
  75.4 7.5 %copy-start.2 = (bf16[64,112,128]{2,1,0:T(8,128)(2,1)}, bf16[64,112,128]{2,1,0:T(8,128)(2,1)S(1)}, u32[]{:S(2)}) copy-start(bf16[64,112,128]{2,1,0:T(8,128)(2,1)S(1)} %all_to_all.20.refs_3_.packed_ref) | copy-start | bytes 5505028
  115.9 90.1 %all-to-all-start.3 = ((bf16[64,112,128]{2,1,0:T(8,128)(2,1)}), bf16[64,112,128]{2,1,0:T(8,128)(2,1)}, u32[]{:S(2)}, u32[]{:S(2)}) async-start(bf16[64,112,128]{2,1,0:T(8,128)(2,1)} %get-tuple-element.14), calls=%async_computation.3 | async-start | bytes 3670016 | tf_op jit(solution)/shard_map/all_to_all | solution.py:345
  125.6 8.5 %copy-start = (bf16[768,1536]{1,0:T(8,128)(2,1)S(1)}, bf16[768,1536]{1,0:T(8,128)(2,1)}, u32[]{:S(2)}) copy-start(bf16[768,1536]{1,0:T(8,128)(2,1)} %refs_1_.7) | copy-start | bytes 7077892
  125.6 36.7 %collective-permute-start.2 = (bf16[384,768]{1,0:T(8,128)(2,1)}, bf16[384,768]{1,0:T(8,128)(2,1)S(1)}, u32[]{:S(2)}, u32[]{:S(2)}) collective-permute-start(bf16[384,768]{1,0:T(8,128)(2,1)} %slice_bitcast_fusion.1), channel_id=1, source_target_pairs={{0,2},{2,4},{4,6},{6,8},{8,10},{10,12},{12,14},{14,16},{16,18},{18... | collective-permute-start | bytes 1769480 | tf_op jit(solution)/shard_map/ppermute | solution.py:336
  128.9 46.0 %collective-permute-start.3 = (bf16[384,768]{1,0:T(8,128)(2,1)}, bf16[384,768]{1,0:T(8,128)(2,1)S(1)}, u32[]{:S(2)}, u32[]{:S(2)}) collective-permute-start(bf16[384,768]{1,0:T(8,128)(2,1)} %get-tuple-element.20), channel_id=1, source_target_pairs={{0,2},{2,4},{4,6},{6,8},{8,10},{10,12},{12,14},{14,16},{16,18},{18... | collective-permute-start | bytes 1769480 | tf_op jit(solution)/shard_map/ppermute | solution.py:341
  132.0 57.5 %collective-permute-start = (bf16[384,768]{1,0:T(8,128)(2,1)}, bf16[384,768]{1,0:T(8,128)(2,1)}, u32[]{:S(2)}, u32[]{:S(2)}) collective-permute-start(bf16[384,768]{1,0:T(8,128)(2,1)} %slice_bitcast_fusion.3), channel_id=1, source_target_pairs={{0,2},{2,4},{4,6},{6,8},{8,10},{10,12},{12,14},{14,16},{16,18},{18... | collective-permute-start | bytes 1769480 | tf_op jit(solution)/shard_map/ppermute | solution.py:341
  132.9 67.4 %collective-permute-start.1 = (bf16[384,768]{1,0:T(8,128)(2,1)}, bf16[384,768]{1,0:T(8,128)(2,1)}, u32[]{:S(2)}, u32[]{:S(2)}) collective-permute-start(bf16[384,768]{1,0:T(8,128)(2,1)} %get-tuple-element.21), channel_id=1, source_target_pairs={{0,2},{2,4},{4,6},{6,8},{8,10},{10,12},{12,14},{14,16},{16,18},{18... | collective-permute-start | bytes 1769480 | tf_op jit(solution)/shard_map/ppermute | solution.py:341
  135.2 77.4 %collective-permute-start.5 = (bf16[768,768]{1,0:T(8,128)(2,1)}, bf16[768,768]{1,0:T(8,128)(2,1)S(1)}, u32[]{:S(2)}, u32[]{:S(2)}) collective-permute-start(bf16[768,768]{1,0:T(8,128)(2,1)} %constant_dynamic-slice_fusion.1), channel_id=1, source_target_pairs={{0,1},{1,0},{2,3},{3,2},{4,5},{5,4},{6,7},{7,6},{8,9},{9,8},{10,11... | collective-permute-start | bytes 3538952 | tf_op jit(solution)/shard_map/ppermute | solution.py:343
  162.3 12.6 %copy-start.5 = (bf16[384,768]{1,0:T(8,128)(2,1)}, bf16[384,768]{1,0:T(8,128)(2,1)S(1)}, u32[]{:S(2)}) copy-start(bf16[384,768]{1,0:T(8,128)(2,1)S(1)} %collective-permute-done.2.refs_2_.refs_0_) | copy-start | bytes 1769476
  174.9 0.8 copy-start.6
  186.5 26.1 %collective-permute-start.6 = (bf16[768,768]{1,0:T(8,128)(2,1)}, bf16[768,768]{1,0:T(8,128)(2,1)S(1)}, u32[]{:S(2)}, u32[]{:S(2)}) collective-permute-start(bf16[768,768]{1,0:T(8,128)(2,1)} %query_heads.3.refs_0_), channel_id=1, source_target_pairs={{0,1},{1,0},{2,3},{3,2},{4,5},{5,4},{6,7},{7,6},{8,9},{9,8},{10,11... | collective-permute-start | bytes 3538952 | tf_op jit(solution)/shard_map/ppermute | solution.py:373
  210.8 9.4 %collective-permute-start.4 = (bf16[768,768]{1,0:T(8,128)(2,1)S(1)}, bf16[768,768]{1,0:T(8,128)(2,1)}, u32[]{:S(2)}, u32[]{:S(2)}) collective-permute-start(bf16[768,768]{1,0:T(8,128)(2,1)S(1)} %query_heads.2.refs_0_), channel_id=1, source_target_pairs={{0,1},{1,0},{2,3},{3,2},{4,5},{5,4},{6,7},{7,6},{8,9},{9,8},{10,11... | collective-permute-start | bytes 3538952 | tf_op jit(solution)/shard_map/ppermute | solution.py:380
  212.6 1.0 copy-start.4
  213.6 1.0 copy-start.7
  214.7 5.6 %copy-start.1 = (bf16[768,1536]{1,0:T(8,128)(2,1)S(1)}, bf16[768,1536]{1,0:T(8,128)(2,1)}, u32[]{:S(2)}) copy-start(bf16[768,1536]{1,0:T(8,128)(2,1)} %refs_1_.7) | copy-start | bytes 7077892

commit v6 on v5

--- a/solution.py
+++ b/solution.py
@@ -40,10 +40,6 @@
         for part in range(PARTS):
             columns = slice(part * LANES, (part + 1) * LANES)
             flat[at * rows : (at + 1) * rows, columns] = shard[part * rows : (part + 1) * rows, :]
-
-
-def in_hbm(array):
-    return pltpu.with_memory_space_constraint(array, pltpu.HBM)
 
 
 def gradient_kernel(first, block_at, rows, *refs):
@@ -98,12 +94,11 @@
         in_specs=[rowed, rowed, pl.BlockSpec((None, step_rates.shape[1], tokens), lambda h: (h, 0, 0))]
         + ([matrix] * 3 if first else [packed]),
         out_specs=packed,
-        out_shape=pltpu.HBM((shards, padded, LANES), BF16),
-        compiler_params=None if first else MID,
+        out_shape=jax.ShapeDtypeStruct((shards, padded, LANES), BF16),
         scratch_shapes=[pltpu.VMEM((3 * DH, DH), F32)],
         cost_estimate=cost(heads * 12 * tokens * DH * DH, 8e6, heads * tokens * DH * 2),
         name="gradients",
-    )(in_hbm(key_rows), in_hbm(value_rows), in_hbm(step_rates), *weights)
+    )(key_rows, value_rows, step_rates, *weights)
 
 
 def row_scale(matrix):
@@ -249,6 +244,10 @@
         out_ref[piece, :] = (fast + attended).astype(BF16)
 
 
+def in_hbm(array):
+    return pltpu.with_memory_space_constraint(array, pltpu.HBM)
+
+
 def query_heads(block_at, queries, packed, near, local, rows, params, kept):
     _, tokens, width = queries.shape
     shards, padded, _ = packed.shape
@@ -269,7 +268,7 @@
         compiler_params=params,
         cost_estimate=cost(heads * 6 * tokens * DH * DH, heads * 3.5e6, heads * tokens * DH),
         name="query_heads",
-    )(in_hbm(queries), packed, in_hbm(near), in_hbm(local))
+    )(queries, packed, in_hbm(near), in_hbm(local))
 
 
 def project_kernel(terms, has_sum, side_ref, *refs):
@@ -340,7 +339,7 @@
         if at:
             near.append(lax.ppermute(array[at // 2, tokens - WINDOW :, :], "tok", ring))
     sent_weight = lax.dynamic_slice_in_dim(out_weight, (1 - side) * width, width, 1)
-    other_weight = in_hbm(lax.ppermute(sent_weight, "head", swap))
+    other_weight = lax.ppermute(sent_weight, "head", swap)
 
     exchange = lambda x: lax.all_to_all(x, "tok", split_axis=0, concat_axis=0, tiled=True)
     flat = jnp.concatenate([gate_init, up_init, down_init], axis=1).reshape(heads * 3 * DH, DH)

time: 226 us -> 223 us (0.987)
  no operation moved by 1% of the time
where the time goes in v6:
time: 223 us
  waiting for transfers between devices  61.9 us (28%)
  blocking collectives  61.7 us (28%)
  Pallas kernels  56.8 us (25%)
  starting transfers between devices  31.9 us (14%)
  local copies, waits for them, and re-layouts  8.36 us (4%)
    all_to_all x2, blocking collectives, shards(): lax.all_to_all(x, 'tok', split_axis=0, concat_axis=0, tiled=True)  61.7 us
    ppermute x3, waiting for transfers between devices, shards(): near.append(lax.ppermute(array[at // 2, tokens - WINDOW:, :], 'tok', ring))  23.4 us
    all_to_all x2, waiting for transfers between devices, shards(): lax.all_to_all(x, 'tok', split_axis=0, concat_axis=0, tiled=True)  22.8 us
    all_to_all x2, starting transfers between devices, shards(): lax.all_to_all(x, 'tok', split_axis=0, concat_axis=0, tiled=True)  19.8 us
    ppermute x1, waiting for transfers between devices, shards(): near = [lax.ppermute(key_rows[0, tokens - WINDOW:, :], 'tok', ring)]  15.6 us
    pallas_call x2, Pallas kernels, gradients(): pl.pallas_call(functools.partial(gradient_kernel, first, block_at, rows),...  14.5 us
    pallas_call x2, Pallas kernels, near_attention(): pl.pallas_call(functools.partial(near_kernel, block_at), grid_spec=pltpu....  10.9 us
    pallas_call x2, Pallas kernels, project(): pl.pallas_call(functools.partial(project_kernel, len(terms), summed is no...  10.5 us
  transfers between devices with their start and end apart: 9, of which 4 were waited for; matrix products, arithmetic and copies ran while one was open for 4% of the time, Pallas kernels for 16%

profile of v6, /device:TPU:1, one launch (start us, length us, event | category | flops | bytes accessed | tf_op | source)
XLA Modules:
  0.0 222.7 jit_solution(8185957012430872298)
XLA Ops:
  0.0 7.4 %gradients.2 = bf16[64,112,128]{2,1,0:T(8,128)(2,1)} custom-call(bf16[2,768,768]{2,1,0:T(8,128)(2,1)} %key_ref.5, bf16[2,768,768]{2,1,0:T(8,128)(2,1)} %value_ref.5, f32[2,2,768]{2,1,0:T(2,128)} %refs_2_.3, f32[2,384,384]{2,1,0:T(8,128)} %refs_3_.1, f32[2,384,384]{2,1,0:T(8,128)} %refs_4_.1, f32[2,384,384]{2,1,0:T(8,128)} %refs_5_.1), custom_call_target="tpu_custom_call" | custom-call | flops 2717908992 | bytes 8000000 | tf_op jit(solution)/shard_map/gradients/pallas_call | solution.py:91
  7.4 12.1 %all-to-all-start = ((bf16[64,112,128]{2,1,0:T(8,128)(2,1)}), bf16[64,112,128]{2,1,0:T(8,128)(2,1)S(1)}, u32[]{:S(2)}, u32[]{:S(2)}) async-start(bf16[64,112,128]{2,1,0:T(8,128)(2,1)} %gradients.2), calls=%async_computation | async-start | bytes 3670016 | tf_op jit(solution)/shard_map/all_to_all | solution.py:344
  19.6 1.9 pad_maximum_fusion
  21.6 22.8 %all-to-all-done.parts_ref = bf16[64,112,128]{2,1,0:T(8,128)(2,1)S(1)} async-done(((bf16[64,112,128]{2,1,0:T(8,128)(2,1)}), bf16[64,112,128]{2,1,0:T(8,128)(2,1)S(1)}, u32[]{:S(2)}, u32[]{:S(2)}) %all-to-all-start) | async-done | bytes 1835040 | tf_op jit(solution)/shard_map/all_to_all | solution.py:344
  44.4 0.6 update.2
  45.0 30.5 %all_to_all.20.refs_3_.packed_ref = bf16[64,112,128]{2,1,0:T(8,128)(2,1)} all-to-all(bf16[64,112,128]{2,1,0:T(8,128)(2,1)S(1)} %get-tuple-element.12), channel_id=1, replica_groups=mesh['tok'=64,'head'=2] {'tok'}, dimensions={0} | all-to-all | bytes 3670016 | tf_op jit(solution)/shard_map/all_to_all | solution.py:344
  75.5 7.1 %gradients.3 = bf16[64,112,128]{2,1,0:T(8,128)(2,1)} custom-call(bf16[2,768,768]{2,1,0:T(8,128)(2,1)} %key_ref.5, bf16[2,768,768]{2,1,0:T(8,128)(2,1)} %value_ref.5, f32[2,2,768]{2,1,0:T(2,128)} %refs_2_.3, bf16[64,112,128]{2,1,0:T(8,128)(2,1)} %all_to_all.20.refs_3_.packed_ref), custom_call_target="tpu_custom_call" | custom-call | flops 2717908992 | bytes 8000000 | tf_op jit(solution)/shard_map/gradients/pallas_call | solution.py:91
  82.6 31.2 %all_to_all.21.parts_ref = bf16[64,112,128]{2,1,0:T(8,128)(2,1)S(1)} all-to-all(bf16[64,112,128]{2,1,0:T(8,128)(2,1)} %gradients.3), channel_id=1, replica_groups=mesh['tok'=64,'head'=2] {'tok'}, dimensions={0} | all-to-all | bytes 3670016 | tf_op jit(solution)/shard_map/all_to_all | solution.py:344
  113.9 1.8 update.3
  115.7 7.7 %all-to-all-start.3 = ((bf16[64,112,128]{2,1,0:T(8,128)(2,1)}), bf16[64,112,128]{2,1,0:T(8,128)(2,1)}, u32[]{:S(2)}, u32[]{:S(2)}) async-start(bf16[64,112,128]{2,1,0:T(8,128)(2,1)} %get-tuple-element.14), calls=%async_computation.3 | async-start | bytes 3670016 | tf_op jit(solution)/shard_map/all_to_all | solution.py:344
  123.4 2.0 slice_bitcast_fusion.1
  125.3 0.9 collective-permute-start.2
  126.3 2.3 %slice_bitcast_fusion = (bf16[384,768]{1,0:T(8,128)(2,1)}, bf16[384,768]{1,0:T(8,128)(2,1)}) fusion(bf16[2,768,768]{2,1,0:T(8,128)(2,1)} %value_ref.5), kind=kLoop, calls=%fused_computation.1 | loop fusion | bytes 2359296 | tf_op jit(solution)/shard_map/squeeze | solution.py:340
  128.6 1.2 collective-permute-start.3
  129.8 1.9 slice_bitcast_fusion.3
  131.7 0.9 collective-permute-start
  132.6 1.2 collective-permute-start.1
  133.8 1.1 constant_dynamic-slice_fusion.1
  135.0 3.1 %collective-permute-start.5 = (bf16[768,768]{1,0:T(8,128)(2,1)}, bf16[768,768]{1,0:T(8,128)(2,1)}, u32[]{:S(2)}, u32[]{:S(2)}) collective-permute-start(bf16[768,768]{1,0:T(8,128)(2,1)} %constant_dynamic-slice_fusion.1), channel_id=1, source_target_pairs={{0,1},{1,0},{2,3},{3,2},{4,5},{5,4},{6,7},{7,6},{8,9},{9,8},{10,11... | collective-permute-start | bytes 3538952 | tf_op jit(solution)/shard_map/ppermute | solution.py:342
  138.0 8.3 %local_attention.1.local_ref = bf16[2,384,768]{2,1,0:T(8,128)(2,1)} custom-call(bf16[2,768,768]{2,1,0:T(8,128)(2,1)} %query_ref.9, bf16[2,768,768]{2,1,0:T(8,128)(2,1)} %key_ref.5, bf16[2,768,768]{2,1,0:T(8,128)(2,1)} %value_ref.5), custom_call_target="tpu_custom_call" | custom-call | flops 1207959552 | bytes 10000000 | tf_op jit(solution)/shard_map/local_attention/pallas_call | solution.py:177
  146.4 15.6 %collective-permute-done.2.refs_2_.refs_0_ = bf16[384,768]{1,0:T(8,128)(2,1)S(1)} collective-permute-done((bf16[384,768]{1,0:T(8,128)(2,1)}, bf16[384,768]{1,0:T(8,128)(2,1)S(1)}, u32[]{:S(2)}, u32[]{:S(2)}) %collective-permute-start.2) | collective-permute-done | bytes 589856 | tf_op jit(solution)/shard_map/ppermute | solution.py:335
  162.0 12.6 %collective-permute-done.3.refs_3_.refs_1_ = bf16[384,768]{1,0:T(8,128)(2,1)S(1)} collective-permute-done((bf16[384,768]{1,0:T(8,128)(2,1)}, bf16[384,768]{1,0:T(8,128)(2,1)S(1)}, u32[]{:S(2)}, u32[]{:S(2)}) %collective-permute-start.3) | collective-permute-done | bytes 589856 | tf_op jit(solution)/shard_map/ppermute | solution.py:340
  174.6 0.8 copy-done.5
  175.4 5.2 %near_attention.3.near_ref = bf16[384,768]{1,0:T(8,128)(2,1)} custom-call(s32[1]{0:T(128)} %bitcast.2.place_ref, bf16[2,768,768]{2,1,0:T(8,128)(2,1)} %query_ref.9, bf16[2,768,768]{2,1,0:T(8,128)(2,1)} %key_ref.5, bf16[2,768,768]{2,1,0:T(8,128)(2,1)} %value_ref.5, bf16[384,768]{1,0:T(8,128)(2,1)} %copy-done.4, bf16[384,768]{1,0:T(8,128)(2,1)} %copy-done.5), custom_call_target="tpu_custom_call" | custom-call | flops 603979776 | bytes 10000000 | tf_op jit(solution)/shard_map/near_attention/pallas_call | solution.py:217
  180.6 5.5 %query_heads.3.refs_0_ = bf16[768,768]{1,0:T(8,128)(2,1)} custom-call(bf16[2,768,768]{2,1,0:T(8,128)(2,1)} %query_ref.9, bf16[64,112,128]{2,1,0:T(8,128)(2,1)} %all_to_all.20.refs_3_.packed_ref, bf16[384,768]{1,0:T(8,128)(2,1)} %near_attention.3.near_ref, bf16[2,384,768]{2,1,0:T(8,128)(2,1)} %local_attention.1.local_ref), custom_call_target="tpu_custom_call" | custom-call | flops 1358954496 | bytes 7000000 | tf_op jit(solution)/shard_map/query_heads/pallas_call | solution.py:256
  186.2 3.0 %collective-permute-start.6 = (bf16[768,768]{1,0:T(8,128)(2,1)}, bf16[768,768]{1,0:T(8,128)(2,1)}, u32[]{:S(2)}, u32[]{:S(2)}) collective-permute-start(bf16[768,768]{1,0:T(8,128)(2,1)} %query_heads.3.refs_0_), channel_id=1, source_target_pairs={{0,1},{1,0},{2,3},{3,2},{4,5},{5,4},{6,7},{7,6},{8,9},{9,8},{10,11... | collective-permute-start | bytes 3538952 | tf_op jit(solution)/shard_map/ppermute | solution.py:372
  189.2 10.8 %collective-permute-done.1.refs_1_ = bf16[384,768]{1,0:T(8,128)(2,1)} collective-permute-done((bf16[384,768]{1,0:T(8,128)(2,1)}, bf16[384,768]{1,0:T(8,128)(2,1)}, u32[]{:S(2)}, u32[]{:S(2)}) %collective-permute-start.1) | collective-permute-done | bytes 589856 | tf_op jit(solution)/shard_map/ppermute | solution.py:340
  200.0 5.7 %near_attention.2.near_ref = bf16[384,768]{1,0:T(8,128)(2,1)} custom-call(s32[1]{0:T(128)} %bitcast.2.place_ref, bf16[2,768,768]{2,1,0:T(8,128)(2,1)} %query_ref.9, bf16[2,768,768]{2,1,0:T(8,128)(2,1)} %key_ref.5, bf16[2,768,768]{2,1,0:T(8,128)(2,1)} %value_ref.5, bf16[384,768]{1,0:T(8,128)(2,1)} %collective-permute-done.refs_0_, ...), custom_call_target="tpu_custom_call" | custom-call | flops 603979776 | bytes 10000000 | tf_op jit(solution)/shard_map/near_attention/pallas_call | solution.py:217
  205.7 4.7 %query_heads.2.refs_0_ = bf16[768,768]{1,0:T(8,128)(2,1)S(1)} custom-call(bf16[2,768,768]{2,1,0:T(8,128)(2,1)S(1)} %copy-done, bf16[64,112,128]{2,1,0:T(8,128)(2,1)} %all-to-all-done.3.packed_ref, bf16[384,768]{1,0:T(8,128)(2,1)} %near_attention.2.near_ref, bf16[2,384,768]{2,1,0:T(8,128)(2,1)} %local_attention.1.local_ref), custom_call_target="tpu_custom_call" | custom-call | flops 1358954496 | bytes 7000000 | tf_op jit(solution)/shard_map/query_heads/pallas_call | solution.py:256
  210.3 1.8 collective-permute-start.4
  212.1 5.6 %project.2.refs_4_ = bf16[2,768,768]{2,1,0:T(8,128)(2,1)} custom-call(s32[1]{0:T(128)} %bitcast.side_ref, bf16[768,768]{1,0:T(8,128)(2,1)} %query_heads.3.refs_0_, bf16[768,1536]{1,0:T(8,128)(2,1)} %refs_1_.7, bf16[768,768]{1,0:T(8,128)(2,1)} %collective-permute-done.6.refs_2_, bf16[768,768]{1,0:T(8,128)(2,1)} %collective-permute-done.5.refs_3_), custom_call_target="tpu_custom_call" | custom-call | flops 1811939328 | bytes 6000000 | tf_op jit(solution)/shard_map/project/pallas_call | solution.py:310
  217.8 4.9 %project.3 = bf16[2,768,768]{2,1,0:T(8,128)(2,1)} custom-call(s32[1]{0:T(128)} %bitcast.side_ref, bf16[768,768]{1,0:T(8,128)(2,1)S(1)} %query_heads.2.refs_0_, bf16[768,1536]{1,0:T(8,128)(2,1)S(1)} %copy-done.2, bf16[768,768]{1,0:T(8,128)(2,1)} %collective-permute-done.4.refs_2_, ...), custom_call_target="tpu_custom_call", output_to_operand_aliasing={{}: (5, {})} | custom-call | flops 1811939328 | bytes 6000000 | tf_op jit(solution)/shard_map/project/pallas_call | solution.py:310
  (20 shorter events, 0.3 us)
Async XLA Ops:
  7.4 12.2 %copy-start.3 = (f32[2,384,384]{2,1,0:T(8,128)S(1)}, f32[2,384,384]{2,1,0:T(8,128)}, u32[]{:S(2)}) copy-start(f32[2,384,384]{2,1,0:T(8,128)} %refs_3_.1) | copy-start | bytes 3538948
  7.4 37.1 %all-to-all-start = ((bf16[64,112,128]{2,1,0:T(8,128)(2,1)}), bf16[64,112,128]{2,1,0:T(8,128)(2,1)S(1)}, u32[]{:S(2)}, u32[]{:S(2)}) async-start(bf16[64,112,128]{2,1,0:T(8,128)(2,1)} %gradients.2), calls=%async_computation | async-start | bytes 3670016 | tf_op jit(solution)/shard_map/all_to_all | solution.py:344
  115.7 90.0 %all-to-all-start.3 = ((bf16[64,112,128]{2,1,0:T(8,128)(2,1)}), bf16[64,112,128]{2,1,0:T(8,128)(2,1)}, u32[]{:S(2)}, u32[]{:S(2)}) async-start(bf16[64,112,128]{2,1,0:T(8,128)(2,1)} %get-tuple-element.14), calls=%async_computation.3 | async-start | bytes 3670016 | tf_op jit(solution)/shard_map/all_to_all | solution.py:344
  125.3 8.5 %copy-start.1 = (bf16[768,1536]{1,0:T(8,128)(2,1)S(1)}, bf16[768,1536]{1,0:T(8,128)(2,1)}, u32[]{:S(2)}) copy-start(bf16[768,1536]{1,0:T(8,128)(2,1)} %refs_1_.7) | copy-start | bytes 7077892
  125.3 36.6 %collective-permute-start.2 = (bf16[384,768]{1,0:T(8,128)(2,1)}, bf16[384,768]{1,0:T(8,128)(2,1)S(1)}, u32[]{:S(2)}, u32[]{:S(2)}) collective-permute-start(bf16[384,768]{1,0:T(8,128)(2,1)} %slice_bitcast_fusion.1), channel_id=1, source_target_pairs={{0,2},{2,4},{4,6},{6,8},{8,10},{10,12},{12,14},{14,16},{16,18},{18... | collective-permute-start | bytes 1769480 | tf_op jit(solution)/shard_map/ppermute | solution.py:335
  128.6 46.0 %collective-permute-start.3 = (bf16[384,768]{1,0:T(8,128)(2,1)}, bf16[384,768]{1,0:T(8,128)(2,1)S(1)}, u32[]{:S(2)}, u32[]{:S(2)}) collective-permute-start(bf16[384,768]{1,0:T(8,128)(2,1)} %get-tuple-element.20), channel_id=1, source_target_pairs={{0,2},{2,4},{4,6},{6,8},{8,10},{10,12},{12,14},{14,16},{16,18},{18... | collective-permute-start | bytes 1769480 | tf_op jit(solution)/shard_map/ppermute | solution.py:340
  131.7 57.5 %collective-permute-start = (bf16[384,768]{1,0:T(8,128)(2,1)}, bf16[384,768]{1,0:T(8,128)(2,1)}, u32[]{:S(2)}, u32[]{:S(2)}) collective-permute-start(bf16[384,768]{1,0:T(8,128)(2,1)} %slice_bitcast_fusion.3), channel_id=1, source_target_pairs={{0,2},{2,4},{4,6},{6,8},{8,10},{10,12},{12,14},{14,16},{16,18},{18... | collective-permute-start | bytes 1769480 | tf_op jit(solution)/shard_map/ppermute | solution.py:340
  132.6 67.4 %collective-permute-start.1 = (bf16[384,768]{1,0:T(8,128)(2,1)}, bf16[384,768]{1,0:T(8,128)(2,1)}, u32[]{:S(2)}, u32[]{:S(2)}) collective-permute-start(bf16[384,768]{1,0:T(8,128)(2,1)} %get-tuple-element.21), channel_id=1, source_target_pairs={{0,2},{2,4},{4,6},{6,8},{8,10},{10,12},{12,14},{14,16},{16,18},{18... | collective-permute-start | bytes 1769480 | tf_op jit(solution)/shard_map/ppermute | solution.py:340
  135.0 77.2 %collective-permute-start.5 = (bf16[768,768]{1,0:T(8,128)(2,1)}, bf16[768,768]{1,0:T(8,128)(2,1)}, u32[]{:S(2)}, u32[]{:S(2)}) collective-permute-start(bf16[768,768]{1,0:T(8,128)(2,1)} %constant_dynamic-slice_fusion.1), channel_id=1, source_target_pairs={{0,1},{1,0},{2,3},{3,2},{4,5},{5,4},{6,7},{7,6},{8,9},{9,8},{10,11... | collective-permute-start | bytes 3538952 | tf_op jit(solution)/shard_map/ppermute | solution.py:342
  162.0 12.6 %copy-start.4 = (bf16[384,768]{1,0:T(8,128)(2,1)}, bf16[384,768]{1,0:T(8,128)(2,1)S(1)}, u32[]{:S(2)}) copy-start(bf16[384,768]{1,0:T(8,128)(2,1)S(1)} %collective-permute-done.2.refs_2_.refs_0_) | copy-start | bytes 1769476
  174.6 0.8 copy-start.5
  186.2 19.5 %copy-start = (bf16[2,768,768]{2,1,0:T(8,128)(2,1)S(1)}, bf16[2,768,768]{2,1,0:T(8,128)(2,1)}, u32[]{:S(2)}) copy-start(bf16[2,768,768]{2,1,0:T(8,128)(2,1)} %query_ref.9) | copy-start | bytes 7077892
  186.2 26.0 %collective-permute-start.6 = (bf16[768,768]{1,0:T(8,128)(2,1)}, bf16[768,768]{1,0:T(8,128)(2,1)}, u32[]{:S(2)}, u32[]{:S(2)}) collective-permute-start(bf16[768,768]{1,0:T(8,128)(2,1)} %query_heads.3.refs_0_), channel_id=1, source_target_pairs={{0,1},{1,0},{2,3},{3,2},{4,5},{5,4},{6,7},{7,6},{8,9},{9,8},{10,11... | collective-permute-start | bytes 3538952 | tf_op jit(solution)/shard_map/ppermute | solution.py:372
  210.3 7.4 %collective-permute-start.4 = (bf16[768,768]{1,0:T(8,128)(2,1)S(1)}, bf16[768,768]{1,0:T(8,128)(2,1)}, u32[]{:S(2)}, u32[]{:S(2)}) collective-permute-start(bf16[768,768]{1,0:T(8,128)(2,1)S(1)} %query_heads.2.refs_0_), channel_id=1, source_target_pairs={{0,1},{1,0},{2,3},{3,2},{4,5},{5,4},{6,7},{7,6},{8,9},{9,8},{10,11... | collective-permute-start | bytes 3538952 | tf_op jit(solution)/shard_map/ppermute | solution.py:379
  212.1 5.6 %copy-start.2 = (bf16[768,1536]{1,0:T(8,128)(2,1)S(1)}, bf16[768,1536]{1,0:T(8,128)(2,1)}, u32[]{:S(2)}) copy-start(bf16[768,1536]{1,0:T(8,128)(2,1)} %refs_1_.7) | copy-start | bytes 7077892

commit v7 on v6

--- a/solution.py
+++ b/solution.py
@@ -233,15 +233,13 @@
     load_packed(packed_ref, flat, rows)
     gate, up = flat[:DH, :].astype(BF16), flat[DH : 2 * DH, :].astype(BF16)
     down = flat[2 * DH :, :].astype(BF16)
-    for at in range(query_ref.shape[0] // WINDOW):
-        piece = slice(at * WINDOW, (at + 1) * WINDOW)
-        query = query_ref[piece, :]
-        pre_gate = dot(query, gate, NT)
-        hidden = (pre_gate * jax.nn.sigmoid(pre_gate) * dot(query, up, NT)).astype(BF16)
-        fast = dot(hidden, down, NT)
-        fast = fast / row_scale(fast)
-        attended = (near_ref if at == 0 else local_ref)[...].astype(F32)
-        out_ref[piece, :] = (fast + attended).astype(BF16)
+    query = query_ref[...]
+    pre_gate = dot(query, gate, NT)
+    hidden = (pre_gate * jax.nn.sigmoid(pre_gate) * dot(query, up, NT)).astype(BF16)
+    fast = dot(hidden, down, NT)
+    fast = fast / row_scale(fast)
+    out_ref[:WINDOW, :] = (fast[:WINDOW, :] + near_ref[...].astype(F32)).astype(BF16)
+    out_ref[WINDOW:, :] = (fast[WINDOW:, :] + local_ref[...].astype(F32)).astype(BF16)
 
 
 def in_hbm(array):
@@ -268,7 +266,7 @@
         compiler_params=params,
         cost_estimate=cost(heads * 6 * tokens * DH * DH, heads * 3.5e6, heads * tokens * DH),
         name="query_heads",
-    )(queries, packed, in_hbm(near), in_hbm(local))
+    )(in_hbm(queries), packed, in_hbm(near), in_hbm(local))
 
 
 def project_kernel(terms, has_sum, side_ref, *refs):

time: 223 us -> 226 us (1.013)
  local copies, waits for them, and re-layouts: 8.36 us -> 11.7 us
    unnamed x12 -> x16, local copies, waits for them, and re-layouts: 0.83 us -> 4.18 us
where the time goes in v7:
time: 226 us
  waiting for transfers between devices  61.9 us (27%)
  blocking collectives  61.7 us (27%)
  Pallas kernels  56.5 us (25%)
  starting transfers between devices  31.9 us (14%)
  local copies, waits for them, and re-layouts  11.7 us (5%)
    all_to_all x2, blocking collectives, shards(): lax.all_to_all(x, 'tok', split_axis=0, concat_axis=0, tiled=True)  61.7 us
    ppermute x3, waiting for transfers between devices, shards(): near.append(lax.ppermute(array[at // 2, tokens - WINDOW:, :], 'tok', ring))  23.5 us
    all_to_all x2, waiting for transfers between devices, shards(): lax.all_to_all(x, 'tok', split_axis=0, concat_axis=0, tiled=True)  22.8 us
    all_to_all x2, starting transfers between devices, shards(): lax.all_to_all(x, 'tok', split_axis=0, concat_axis=0, tiled=True)  19.8 us
    ppermute x1, waiting for transfers between devices, shards(): near = [lax.ppermute(key_rows[0, tokens - WINDOW:, :], 'tok', ring)]  15.6 us
    pallas_call x2, Pallas kernels, gradients(): pl.pallas_call(functools.partial(gradient_kernel, first, block_at, rows),...  14.5 us
    pallas_call x2, Pallas kernels, near_attention(): pl.pallas_call(functools.partial(near_kernel, block_at), grid_spec=pltpu....  11 us
    pallas_call x2, Pallas kernels, query_heads(): pl.pallas_call(functools.partial(query_kernel, rows), grid=(heads,), in_s...  10.2 us
  transfers between devices with their start and end apart: 9, of which 4 were waited for; matrix products, arithmetic and copies ran while one was open for 4% of the time, Pallas kernels for 16%

profile of v7, /device:TPU:1, one launch (start us, length us, event | category | flops | bytes accessed | tf_op | source)
XLA Modules:
  0.0 225.7 jit_solution(4547022587560007316)
XLA Ops:
  0.0 7.4 %gradients.2 = bf16[64,112,128]{2,1,0:T(8,128)(2,1)} custom-call(bf16[2,768,768]{2,1,0:T(8,128)(2,1)} %key_ref.5, bf16[2,768,768]{2,1,0:T(8,128)(2,1)} %value_ref.5, f32[2,2,768]{2,1,0:T(2,128)} %refs_2_.3, f32[2,384,384]{2,1,0:T(8,128)} %refs_3_.1, f32[2,384,384]{2,1,0:T(8,128)} %refs_4_.1, f32[2,384,384]{2,1,0:T(8,128)} %refs_5_.1), custom_call_target="tpu_custom_call" | custom-call | flops 2717908992 | bytes 8000000 | tf_op jit(solution)/shard_map/gradients/pallas_call | solution.py:91
  7.4 12.1 %all-to-all-start = ((bf16[64,112,128]{2,1,0:T(8,128)(2,1)}), bf16[64,112,128]{2,1,0:T(8,128)(2,1)S(1)}, u32[]{:S(2)}, u32[]{:S(2)}) async-start(bf16[64,112,128]{2,1,0:T(8,128)(2,1)} %gradients.2), calls=%async_computation | async-start | bytes 3670016 | tf_op jit(solution)/shard_map/all_to_all | solution.py:342
  19.6 1.9 pad_maximum_fusion
  21.6 22.8 %all-to-all-done.parts_ref = bf16[64,112,128]{2,1,0:T(8,128)(2,1)S(1)} async-done(((bf16[64,112,128]{2,1,0:T(8,128)(2,1)}), bf16[64,112,128]{2,1,0:T(8,128)(2,1)S(1)}, u32[]{:S(2)}, u32[]{:S(2)}) %all-to-all-start) | async-done | bytes 1835040 | tf_op jit(solution)/shard_map/all_to_all | solution.py:342
  45.0 30.5 %all_to_all.20.refs_3_.packed_ref = bf16[64,112,128]{2,1,0:T(8,128)(2,1)} all-to-all(bf16[64,112,128]{2,1,0:T(8,128)(2,1)S(1)} %get-tuple-element.12), channel_id=1, replica_groups=mesh['tok'=64,'head'=2] {'tok'}, dimensions={0} | all-to-all | bytes 3670016 | tf_op jit(solution)/shard_map/all_to_all | solution.py:342
  75.5 7.1 %gradients.3 = bf16[64,112,128]{2,1,0:T(8,128)(2,1)} custom-call(bf16[2,768,768]{2,1,0:T(8,128)(2,1)} %key_ref.5, bf16[2,768,768]{2,1,0:T(8,128)(2,1)} %value_ref.5, f32[2,2,768]{2,1,0:T(2,128)} %refs_2_.3, bf16[64,112,128]{2,1,0:T(8,128)(2,1)} %all_to_all.20.refs_3_.packed_ref), custom_call_target="tpu_custom_call" | custom-call | flops 2717908992 | bytes 8000000 | tf_op jit(solution)/shard_map/gradients/pallas_call | solution.py:91
  82.6 31.2 %all_to_all.21.parts_ref = bf16[64,112,128]{2,1,0:T(8,128)(2,1)S(1)} all-to-all(bf16[64,112,128]{2,1,0:T(8,128)(2,1)} %gradients.3), channel_id=1, replica_groups=mesh['tok'=64,'head'=2] {'tok'}, dimensions={0} | all-to-all | bytes 3670016 | tf_op jit(solution)/shard_map/all_to_all | solution.py:342
  113.9 1.8 update.3
  115.7 7.7 %all-to-all-start.3 = ((bf16[64,112,128]{2,1,0:T(8,128)(2,1)}), bf16[64,112,128]{2,1,0:T(8,128)(2,1)}, u32[]{:S(2)}, u32[]{:S(2)}) async-start(bf16[64,112,128]{2,1,0:T(8,128)(2,1)} %get-tuple-element.14), calls=%async_computation.3 | async-start | bytes 3670016 | tf_op jit(solution)/shard_map/all_to_all | solution.py:342
  123.4 1.9 slice_bitcast_fusion.1
  125.3 0.9 collective-permute-start.2
  126.3 2.4 %slice_bitcast_fusion = (bf16[384,768]{1,0:T(8,128)(2,1)}, bf16[384,768]{1,0:T(8,128)(2,1)}) fusion(bf16[2,768,768]{2,1,0:T(8,128)(2,1)} %value_ref.5), kind=kLoop, calls=%fused_computation.1 | loop fusion | bytes 2359296 | tf_op jit(solution)/shard_map/squeeze | solution.py:338
  128.7 1.2 collective-permute-start.3
  129.9 1.9 slice_bitcast_fusion.3
  132.7 1.2 collective-permute-start.1
  133.9 1.1 constant_dynamic-slice_fusion.1
  135.0 3.1 %collective-permute-start.5 = (bf16[768,768]{1,0:T(8,128)(2,1)}, bf16[768,768]{1,0:T(8,128)(2,1)S(1)}, u32[]{:S(2)}, u32[]{:S(2)}) collective-permute-start(bf16[768,768]{1,0:T(8,128)(2,1)} %constant_dynamic-slice_fusion.1), channel_id=1, source_target_pairs={{0,1},{1,0},{2,3},{3,2},{4,5},{5,4},{6,7},{7,6},{8,9},{9,8},{10,11... | collective-permute-start | bytes 3538952 | tf_op jit(solution)/shard_map/ppermute | solution.py:340
  138.0 8.4 %local_attention.1.local_ref = bf16[2,384,768]{2,1,0:T(8,128)(2,1)} custom-call(bf16[2,768,768]{2,1,0:T(8,128)(2,1)} %query_ref.9, bf16[2,768,768]{2,1,0:T(8,128)(2,1)} %key_ref.5, bf16[2,768,768]{2,1,0:T(8,128)(2,1)} %value_ref.5), custom_call_target="tpu_custom_call" | custom-call | flops 1207959552 | bytes 10000000 | tf_op jit(solution)/shard_map/local_attention/pallas_call | solution.py:177
  146.4 15.6 %collective-permute-done.2.refs_2_.refs_0_ = bf16[384,768]{1,0:T(8,128)(2,1)S(1)} collective-permute-done((bf16[384,768]{1,0:T(8,128)(2,1)}, bf16[384,768]{1,0:T(8,128)(2,1)S(1)}, u32[]{:S(2)}, u32[]{:S(2)}) %collective-permute-start.2) | collective-permute-done | bytes 589856 | tf_op jit(solution)/shard_map/ppermute | solution.py:333
  162.0 12.6 %collective-permute-done.3.refs_3_.refs_1_ = bf16[384,768]{1,0:T(8,128)(2,1)S(1)} collective-permute-done((bf16[384,768]{1,0:T(8,128)(2,1)}, bf16[384,768]{1,0:T(8,128)(2,1)S(1)}, u32[]{:S(2)}, u32[]{:S(2)}) %collective-permute-start.3) | collective-permute-done | bytes 589856 | tf_op jit(solution)/shard_map/ppermute | solution.py:338
  175.5 5.2 %near_attention.3.near_ref = bf16[384,768]{1,0:T(8,128)(2,1)} custom-call(s32[1]{0:T(128)} %bitcast.2.place_ref, bf16[2,768,768]{2,1,0:T(8,128)(2,1)} %query_ref.9, bf16[2,768,768]{2,1,0:T(8,128)(2,1)} %key_ref.5, bf16[2,768,768]{2,1,0:T(8,128)(2,1)} %value_ref.5, bf16[384,768]{1,0:T(8,128)(2,1)} %copy-done.5, bf16[384,768]{1,0:T(8,128)(2,1)} %copy-done.6), custom_call_target="tpu_custom_call" | custom-call | flops 603979776 | bytes 10000000 | tf_op jit(solution)/shard_map/near_attention/pallas_call | solution.py:217
  180.7 5.5 %query_heads.3.refs_0_ = bf16[768,768]{1,0:T(8,128)(2,1)} custom-call(bf16[2,768,768]{2,1,0:T(8,128)(2,1)} %query_ref.9, bf16[64,112,128]{2,1,0:T(8,128)(2,1)} %all_to_all.20.refs_3_.packed_ref, bf16[384,768]{1,0:T(8,128)(2,1)} %near_attention.3.near_ref, bf16[2,384,768]{2,1,0:T(8,128)(2,1)} %local_attention.1.local_ref), custom_call_target="tpu_custom_call" | custom-call | flops 1358954496 | bytes 7000000 | tf_op jit(solution)/shard_map/query_heads/pallas_call | solution.py:254
  186.2 3.0 %collective-permute-start.6 = (bf16[768,768]{1,0:T(8,128)(2,1)}, bf16[768,768]{1,0:T(8,128)(2,1)S(1)}, u32[]{:S(2)}, u32[]{:S(2)}) collective-permute-start(bf16[768,768]{1,0:T(8,128)(2,1)} %query_heads.3.refs_0_), channel_id=1, source_target_pairs={{0,1},{1,0},{2,3},{3,2},{4,5},{5,4},{6,7},{7,6},{8,9},{9,8},{10,11... | collective-permute-start | bytes 3538952 | tf_op jit(solution)/shard_map/ppermute | solution.py:370
  189.2 10.8 %collective-permute-done.1.refs_1_ = bf16[384,768]{1,0:T(8,128)(2,1)} collective-permute-done((bf16[384,768]{1,0:T(8,128)(2,1)}, bf16[384,768]{1,0:T(8,128)(2,1)}, u32[]{:S(2)}, u32[]{:S(2)}) %collective-permute-start.1) | collective-permute-done | bytes 589856 | tf_op jit(solution)/shard_map/ppermute | solution.py:338
  200.0 5.7 %near_attention.2.near_ref = bf16[384,768]{1,0:T(8,128)(2,1)} custom-call(s32[1]{0:T(128)} %bitcast.2.place_ref, bf16[2,768,768]{2,1,0:T(8,128)(2,1)} %query_ref.9, bf16[2,768,768]{2,1,0:T(8,128)(2,1)} %key_ref.5, bf16[2,768,768]{2,1,0:T(8,128)(2,1)} %value_ref.5, bf16[384,768]{1,0:T(8,128)(2,1)} %collective-permute-done.refs_0_, ...), custom_call_target="tpu_custom_call" | custom-call | flops 603979776 | bytes 10000000 | tf_op jit(solution)/shard_map/near_attention/pallas_call | solution.py:217
  205.8 4.7 %query_heads.2.refs_0_ = bf16[768,768]{1,0:T(8,128)(2,1)S(1)} custom-call(bf16[2,768,768]{2,1,0:T(8,128)(2,1)} %query_ref.9, bf16[64,112,128]{2,1,0:T(8,128)(2,1)} %all-to-all-done.3.packed_ref, bf16[384,768]{1,0:T(8,128)(2,1)} %near_attention.2.near_ref, bf16[2,384,768]{2,1,0:T(8,128)(2,1)} %local_attention.1.local_ref), custom_call_target="tpu_custom_call" | custom-call | flops 1358954496 | bytes 7000000 | tf_op jit(solution)/shard_map/query_heads/pallas_call | solution.py:254
  210.5 1.8 collective-permute-start.4
  212.3 1.0 copy-done.2
  213.4 1.0 copy-done.7
  214.4 5.6 %project.2.refs_4_ = bf16[2,768,768]{2,1,0:T(8,128)(2,1)} custom-call(s32[1]{0:T(128)} %bitcast.side_ref, bf16[768,768]{1,0:T(8,128)(2,1)} %query_heads.3.refs_0_, bf16[768,1536]{1,0:T(8,128)(2,1)} %refs_1_.7, bf16[768,768]{1,0:T(8,128)(2,1)} %copy-done.7, bf16[768,768]{1,0:T(8,128)(2,1)} %copy-done.2), custom_call_target="tpu_custom_call" | custom-call | flops 1811939328 | bytes 6000000 | tf_op jit(solution)/shard_map/project/pallas_call | solution.py:308
  220.0 1.3 copy-done.3
  221.2 4.4 %project.3 = bf16[2,768,768]{2,1,0:T(8,128)(2,1)} custom-call(s32[1]{0:T(128)} %bitcast.side_ref, bf16[768,768]{1,0:T(8,128)(2,1)S(1)} %query_heads.2.refs_0_, bf16[768,1536]{1,0:T(8,128)(2,1)S(1)} %copy-done.1, bf16[768,768]{1,0:T(8,128)(2,1)} %collective-permute-done.4.refs_2_, bf16[768,768]{1,0:T(8,128)(2,1)S(1)} %copy-done.3, ...), custom_call_target="tpu_custom_call", output_to_operand_aliasing={{}: (5, {})} | custom-call | flops 1811939328 | bytes 6000000 | tf_op jit(solution)/shard_map/project/pallas_call | solution.py:308
  (24 shorter events, 2.6 us)
Async XLA Ops:
  7.4 12.2 %copy-start.4 = (f32[2,384,384]{2,1,0:T(8,128)S(1)}, f32[2,384,384]{2,1,0:T(8,128)}, u32[]{:S(2)}) copy-start(f32[2,384,384]{2,1,0:T(8,128)} %refs_3_.1) | copy-start | bytes 3538948
  7.4 37.1 %all-to-all-start = ((bf16[64,112,128]{2,1,0:T(8,128)(2,1)}), bf16[64,112,128]{2,1,0:T(8,128)(2,1)S(1)}, u32[]{:S(2)}, u32[]{:S(2)}) async-start(bf16[64,112,128]{2,1,0:T(8,128)(2,1)} %gradients.2), calls=%async_computation | async-start | bytes 3670016 | tf_op jit(solution)/shard_map/all_to_all | solution.py:342
  115.7 90.1 %all-to-all-start.3 = ((bf16[64,112,128]{2,1,0:T(8,128)(2,1)}), bf16[64,112,128]{2,1,0:T(8,128)(2,1)}, u32[]{:S(2)}, u32[]{:S(2)}) async-start(bf16[64,112,128]{2,1,0:T(8,128)(2,1)} %get-tuple-element.14), calls=%async_computation.3 | async-start | bytes 3670016 | tf_op jit(solution)/shard_map/all_to_all | solution.py:342
  125.3 8.5 %copy-start = (bf16[768,1536]{1,0:T(8,128)(2,1)S(1)}, bf16[768,1536]{1,0:T(8,128)(2,1)}, u32[]{:S(2)}) copy-start(bf16[768,1536]{1,0:T(8,128)(2,1)} %refs_1_.7) | copy-start | bytes 7077892
  125.3 36.7 %collective-permute-start.2 = (bf16[384,768]{1,0:T(8,128)(2,1)}, bf16[384,768]{1,0:T(8,128)(2,1)S(1)}, u32[]{:S(2)}, u32[]{:S(2)}) collective-permute-start(bf16[384,768]{1,0:T(8,128)(2,1)} %slice_bitcast_fusion.1), channel_id=1, source_target_pairs={{0,2},{2,4},{4,6},{6,8},{8,10},{10,12},{12,14},{14,16},{16,18},{18... | collective-permute-start | bytes 1769480 | tf_op jit(solution)/shard_map/ppermute | solution.py:333
  128.7 46.0 %collective-permute-start.3 = (bf16[384,768]{1,0:T(8,128)(2,1)}, bf16[384,768]{1,0:T(8,128)(2,1)S(1)}, u32[]{:S(2)}, u32[]{:S(2)}) collective-permute-start(bf16[384,768]{1,0:T(8,128)(2,1)} %get-tuple-element.20), channel_id=1, source_target_pairs={{0,2},{2,4},{4,6},{6,8},{8,10},{10,12},{12,14},{14,16},{16,18},{18... | collective-permute-start | bytes 1769480 | tf_op jit(solution)/shard_map/ppermute | solution.py:338
  131.8 57.4 %collective-permute-start = (bf16[384,768]{1,0:T(8,128)(2,1)}, bf16[384,768]{1,0:T(8,128)(2,1)}, u32[]{:S(2)}, u32[]{:S(2)}) collective-permute-start(bf16[384,768]{1,0:T(8,128)(2,1)} %slice_bitcast_fusion.3), channel_id=1, source_target_pairs={{0,2},{2,4},{4,6},{6,8},{8,10},{10,12},{12,14},{14,16},{16,18},{18... | collective-permute-start | bytes 1769480 | tf_op jit(solution)/shard_map/ppermute | solution.py:338
  132.7 67.4 %collective-permute-start.1 = (bf16[384,768]{1,0:T(8,128)(2,1)}, bf16[384,768]{1,0:T(8,128)(2,1)}, u32[]{:S(2)}, u32[]{:S(2)}) collective-permute-start(bf16[384,768]{1,0:T(8,128)(2,1)} %get-tuple-element.21), channel_id=1, source_target_pairs={{0,2},{2,4},{4,6},{6,8},{8,10},{10,12},{12,14},{14,16},{16,18},{18... | collective-permute-start | bytes 1769480 | tf_op jit(solution)/shard_map/ppermute | solution.py:338
  135.0 77.4 %collective-permute-start.5 = (bf16[768,768]{1,0:T(8,128)(2,1)}, bf16[768,768]{1,0:T(8,128)(2,1)S(1)}, u32[]{:S(2)}, u32[]{:S(2)}) collective-permute-start(bf16[768,768]{1,0:T(8,128)(2,1)} %constant_dynamic-slice_fusion.1), channel_id=1, source_target_pairs={{0,1},{1,0},{2,3},{3,2},{4,5},{5,4},{6,7},{7,6},{8,9},{9,8},{10,11... | collective-permute-start | bytes 3538952 | tf_op jit(solution)/shard_map/ppermute | solution.py:340
  162.0 12.6 %copy-start.5 = (bf16[384,768]{1,0:T(8,128)(2,1)}, bf16[384,768]{1,0:T(8,128)(2,1)S(1)}, u32[]{:S(2)}) copy-start(bf16[384,768]{1,0:T(8,128)(2,1)S(1)} %collective-permute-done.2.refs_2_.refs_0_) | copy-start | bytes 1769476
  174.6 0.8 copy-start.6
  186.2 26.1 %collective-permute-start.6 = (bf16[768,768]{1,0:T(8,128)(2,1)}, bf16[768,768]{1,0:T(8,128)(2,1)S(1)}, u32[]{:S(2)}, u32[]{:S(2)}) collective-permute-start(bf16[768,768]{1,0:T(8,128)(2,1)} %query_heads.3.refs_0_), channel_id=1, source_target_pairs={{0,1},{1,0},{2,3},{3,2},{4,5},{5,4},{6,7},{7,6},{8,9},{9,8},{10,11... | collective-permute-start | bytes 3538952 | tf_op jit(solution)/shard_map/ppermute | solution.py:370
  210.5 9.4 %collective-permute-start.4 = (bf16[768,768]{1,0:T(8,128)(2,1)S(1)}, bf16[768,768]{1,0:T(8,128)(2,1)}, u32[]{:S(2)}, u32[]{:S(2)}) collective-permute-start(bf16[768,768]{1,0:T(8,128)(2,1)S(1)} %query_heads.2.refs_0_), channel_id=1, source_target_pairs={{0,1},{1,0},{2,3},{3,2},{4,5},{5,4},{6,7},{7,6},{8,9},{9,8},{10,11... | collective-permute-start | bytes 3538952 | tf_op jit(solution)/shard_map/ppermute | solution.py:377
  212.3 1.0 copy-start.2
  213.4 1.0 copy-start.7
  214.4 5.6 %copy-start.1 = (bf16[768,1536]{1,0:T(8,128)(2,1)S(1)}, bf16[768,1536]{1,0:T(8,128)(2,1)}, u32[]{:S(2)}) copy-start(bf16[768,1536]{1,0:T(8,128)(2,1)} %refs_1_.7) | copy-start | bytes 7077892
  220.0 1.3 copy-start.3
